TPU v7x, 32 devices: a whole 2x2x4 slice. The times are simulated.
32 devices in a mesh: dp: 8 (over y, x, core), mp: 4 (over z).
Axes of the slice: x: 2, y: 2, z: 4, core: 2. Of those that a mesh axis runs over, the one named last changes fastest.
Arguments:
- frames_in: bfloat16 [8, 512, 1024], P('dp', 'mp'), may hold values from -6 to 6
- lengths: int32 [8], replicated, may hold values from 128 to 512, as said below
- out_grad: bfloat16 [8, 512, 1024], P('dp', 'mp'), may hold values from -6 to 6
- norm_gains: float32 [5, 1024], replicated, may hold values from 0.25 to 1.75
- ffn1_up: bfloat16 [1024, 4096], P('dp', 'mp'), may hold values from -0.1875 to 0.1875
- ffn1_down: bfloat16 [4096, 1024], P('mp', 'dp'), may hold values from -0.09375 to 0.09375
- attn_in: bfloat16 [1024, 3, 1024], P('dp', None, 'mp'), may hold values from -0.1875 to 0.1875
- pos_proj: bfloat16 [1024, 1024], P('dp', 'mp'), may hold values from -0.1875 to 0.1875
- pos_bias: bfloat16 [2, 1024], P(None, ('mp', 'dp')), may hold values from -3 to 3
- attn_out: bfloat16 [1024, 1024], P('mp', 'dp'), may hold values from -1.5 to 1.5
- conv_in: bfloat16 [1024, 2, 1024], P('dp', None, 'mp'), may hold values from -0.1875 to 0.1875
- depthwise: bfloat16 [5, 1024], P(None, ('mp', 'dp')), may hold values from -2.5 to 2.5
- bn_scale: bfloat16 [1024], P(('mp', 'dp')), may hold values from 0.25 to 1.75
- bn_shift: bfloat16 [1024], P(('mp', 'dp')), may hold values from -3 to 3
- conv_out: bfloat16 [1024, 1024], P('mp', 'dp'), may hold values from -0.1875 to 0.1875
- ffn2_up: bfloat16 [1024, 4096], P('dp', 'mp'), may hold values from -0.1875 to 0.1875
- ffn2_down: bfloat16 [4096, 1024], P('mp', 'dp'), may hold values from -0.09375 to 0.09375
Outputs:
- block_out: bfloat16 [8, 512, 1024], P('dp', 'mp')
- in_grad: float32 [8, 512, 1024], P('dp', 'mp')
- grad_norm_gains: float32 [5, 1024], replicated
- grad_ffn1_up: float32 [1024, 4096], P('dp', 'mp')
- grad_ffn1_down: float32 [4096, 1024], P('mp', 'dp')
- grad_attn_in: float32 [1024, 3, 1024], P('dp', None, 'mp')
- grad_pos_proj: float32 [1024, 1024], P('dp', 'mp')
- grad_pos_bias: float32 [2, 1024], P(None, ('mp', 'dp'))
- grad_attn_out: float32 [1024, 1024], P('mp', 'dp')
- grad_conv_in: float32 [1024, 2, 1024], P('dp', None, 'mp')
- grad_depthwise: float32 [5, 1024], P(None, ('mp', 'dp'))
- grad_bn_scale: float32 [1024], P(('mp', 'dp'))
- grad_bn_shift: float32 [1024], P(('mp', 'dp'))
- grad_conv_out: float32 [1024, 1024], P('mp', 'dp')
- grad_ffn2_up: float32 [1024, 4096], P('dp', 'mp')
- grad_ffn2_down: float32 [4096, 1024], P('mp', 'dp')
Inputs may be any that keep to these rules, and one draw needn't show every extreme that they name: Frames 0 to lengths[s] - 1 of slot s hold the utterance and the rest is padding; some slot holds 512 frames.
All inputs are finite; a program needn't handle non-finite values.
Results may differ from a plain program's by a relative error of at most 0.03.
Values may be sent and summed in bfloat16 or wider, within the bound.
A program may use at most 128 MiB of HBM per device.

v0:
```python
import math

import jax
import jax.numpy as jnp
from jax import lax
from jax.sharding import PartitionSpec as P

HEAD = 128


norm_eps = 1e-05
batch_eps = 1e-05
masked_score = -1000000000.0


def matmul(left, right):
    return jnp.dot(left, right, preferred_element_type=jnp.float32)


def contract_rows(left, right):
    return lax.dot_general(
        left, right, (((0,), (0,)), ((), ())), preferred_element_type=jnp.float32
    )


def contract_cols(left, right):
    return lax.dot_general(
        left, right, (((1,), (1,)), ((), ())), preferred_element_type=jnp.float32
    )


def layer_norm(values, norm_gain):
    average = jnp.mean(values, axis=-1, keepdims=True)
    centred = values - average
    inv_std = lax.rsqrt(jnp.mean(centred * centred, axis=-1, keepdims=True) + norm_eps)
    return centred * inv_std * norm_gain


def norm_back(values, norm_gain, upstream):
    unused, pullback = jax.vjp(layer_norm, values, norm_gain)
    return pullback(upstream)


def silu_slope(values):
    logistic = jax.nn.sigmoid(values)
    return logistic * (1.0 + values * (1.0 - logistic))


def position_table(seq_len, model_width):
    distance = (seq_len - 1 - jnp.arange(2 * seq_len)).astype(jnp.float32)
    frequency = jnp.exp(
        jnp.arange(model_width // 2).astype(jnp.float32) * (-2.0 * math.log(10000.0) / model_width)
    )
    angles = distance[:, None] * frequency[None, :]
    return jnp.stack([jnp.sin(angles), jnp.cos(angles)], axis=-1).reshape(2 * seq_len, model_width)


def spread_rows(normed):
    return lax.all_gather(normed, "mp", axis=0, tiled=True)


def enter_block(residual, norm_gain):
    return spread_rows(layer_norm(residual, norm_gain).astype(jnp.bfloat16))


def branch_total(partial_value):
    return lax.psum_scatter(
        partial_value.astype(jnp.bfloat16), "mp", scatter_dimension=0, tiled=True
    ).astype(jnp.float32)


def spread_grads(upstream):
    return lax.all_gather(upstream, "mp", axis=0, tiled=True)


def input_total(partial_value):
    return lax.psum_scatter(
        partial_value.astype(jnp.bfloat16), "mp", scatter_dimension=0, tiled=True
    ).astype(jnp.float32)


def ffn_fetch(w_up, w_down):
    return (
        lax.all_gather(w_up, "dp", axis=0, tiled=True),
        lax.all_gather(w_down, "dp", axis=1, tiled=True),
    )


def attn_fetch(w_in, w_pos, bias_pair, w_out):
    return (
        lax.all_gather(w_in, "dp", axis=0, tiled=True),
        lax.all_gather(w_pos, "dp", axis=0, tiled=True),
        lax.all_gather(bias_pair, "dp", axis=1, tiled=True),
        lax.all_gather(w_out, "dp", axis=1, tiled=True),
    )


def conv_fetch(w_in, kernel, bn_gain, bn_bias, w_out):
    return (
        lax.all_gather(w_in, "dp", axis=0, tiled=True),
        lax.all_gather(kernel, "dp", axis=1, tiled=True),
        lax.all_gather(bn_gain, "dp", axis=0, tiled=True),
        lax.all_gather(bn_bias, "dp", axis=0, tiled=True),
        lax.all_gather(w_out, "dp", axis=1, tiled=True),
    )


def ffn_forward(whole, weights):
    w_up, w_down = weights
    hidden = matmul(whole, w_up)
    return matmul(jax.nn.silu(hidden).astype(jnp.bfloat16), w_down)


def ffn_backward(whole, weights, grad_whole):
    w_up, w_down = weights
    hidden = matmul(whole, w_up)
    active = jax.nn.silu(hidden).astype(jnp.bfloat16)
    grad_down = contract_rows(active, grad_whole)
    d_hidden = (contract_cols(grad_whole, w_down) * silu_slope(hidden)).astype(jnp.bfloat16)
    grad_up = contract_rows(whole, d_hidden)
    return (contract_cols(d_hidden, w_up), grad_up, grad_down)


def attention_setup(whole, weights):
    w_in, w_pos, bias_pair, w_out = weights
    seq_len, model_width = whole.shape
    local_width = w_in.shape[2]
    heads_here = local_width // HEAD
    projected = matmul(whole, w_in.reshape(model_width, 3 * local_width))
    queries = projected[:, :local_width]
    key_rows = (
        projected[:, local_width : 2 * local_width]
        .astype(jnp.bfloat16)
        .reshape(seq_len, heads_here, HEAD)
    )
    value_rows = (
        projected[:, 2 * local_width :].astype(jnp.bfloat16).reshape(seq_len, heads_here, HEAD)
    )
    scaling = HEAD ** (-0.5)
    bias_float = bias_pair.astype(jnp.float32)
    query_u = (
        ((queries + bias_float[0]) * scaling)
        .astype(jnp.bfloat16)
        .reshape(seq_len, heads_here, HEAD)
    )
    query_v = (
        ((queries + bias_float[1]) * scaling)
        .astype(jnp.bfloat16)
        .reshape(seq_len, heads_here, HEAD)
    )
    table_low = position_table(seq_len, model_width).astype(jnp.bfloat16)
    position = matmul(table_low, w_pos).astype(jnp.bfloat16).reshape(2 * seq_len, heads_here, HEAD)
    return (query_u, query_v, key_rows, value_rows, table_low, position)


def skew_rows(zeds, block_rows, seq_len):
    heads_here = zeds.shape[0]
    window = block_rows + seq_len - 1
    flat = zeds.reshape(heads_here, block_rows * window)
    flat = flat[:, block_rows - 1 : block_rows - 1 + block_rows * (window - 1)]
    return flat.reshape(heads_here, block_rows, window - 1)[:, :, :seq_len]


def unskew_rows(grads_in, block_rows, seq_len):
    heads_here = grads_in.shape[0]
    window = block_rows + seq_len - 1
    padded = jnp.pad(grads_in, ((0, 0), (0, 0), (0, window - 1 - seq_len)))
    flat = padded.reshape(heads_here, block_rows * (window - 1))
    flat = jnp.pad(flat, ((0, 0), (block_rows - 1, 1)))
    return flat.reshape(heads_here, block_rows, window)


def block_scores(query_u, query_v, key_rows, position, valid_keys, offset, block_rows):
    seq_len = key_rows.shape[0]
    window = block_rows + seq_len - 1
    lowest = seq_len - offset - block_rows
    nearby = position[lowest : lowest + window]
    content = jnp.einsum("bhd,jhd->hbj", query_u, key_rows, preferred_element_type=jnp.float32)
    zeds = jnp.einsum("bhd,whd->hbw", query_v, nearby, preferred_element_type=jnp.float32)
    scores = jnp.where(
        valid_keys[None, None, :], content + skew_rows(zeds, block_rows, seq_len), masked_score
    )
    top_score = jnp.max(scores, axis=-1, keepdims=True)
    exponent = jnp.exp(scores - top_score)
    softmax_out = exponent / jnp.sum(exponent, axis=-1, keepdims=True)
    return (softmax_out, query_u, query_v, nearby, lowest)


def attention_forward(whole, weights, valid_keys, block_rows):
    seq_len = whole.shape[0]
    query_u, query_v, key_rows, value_rows, table_low, position = attention_setup(whole, weights)
    softmax_out, part_u, part_v, nearby, lowest = block_scores(
        query_u, query_v, key_rows, position, valid_keys, 0, block_rows
    )
    contexts = jnp.einsum(
        "hbj,jhd->bhd",
        softmax_out.astype(jnp.bfloat16),
        value_rows,
        preferred_element_type=jnp.float32,
    )
    context = contexts.reshape(seq_len, -1).astype(jnp.bfloat16)
    return matmul(context, weights[3])


def attention_backward(whole, weights, valid_keys, block_rows, grad_whole):
    w_in, w_pos, bias_pair, w_out = weights
    seq_len, model_width = whole.shape
    query_u, query_v, key_rows, value_rows, table_low, position = attention_setup(whole, weights)
    heads_here = key_rows.shape[1]
    local_width = w_in.shape[2]
    scaling = HEAD ** (-0.5)
    window = block_rows + seq_len - 1
    d_context = (
        contract_cols(grad_whole, w_out).astype(jnp.bfloat16).reshape(seq_len, heads_here, HEAD)
    )
    d_position = jnp.zeros(position.shape, jnp.float32)
    softmax_out, part_u, part_v, nearby, lowest = block_scores(
        query_u, query_v, key_rows, position, valid_keys, 0, block_rows
    )
    soft_low = softmax_out.astype(jnp.bfloat16)
    contexts = jnp.einsum("hbj,jhd->bhd", soft_low, value_rows, preferred_element_type=jnp.float32)
    d_soft = jnp.einsum("bhd,jhd->hbj", d_context, value_rows, preferred_element_type=jnp.float32)
    inner = jnp.sum(softmax_out * d_soft, axis=-1, keepdims=True)
    d_scores = (softmax_out * (d_soft - inner)).astype(jnp.bfloat16)
    d_query_u = jnp.einsum("hbj,jhd->bhd", d_scores, key_rows, preferred_element_type=jnp.float32)
    d_keys = jnp.einsum("hbj,bhd->jhd", d_scores, part_u, preferred_element_type=jnp.float32)
    d_values = jnp.einsum("hbj,bhd->jhd", soft_low, d_context, preferred_element_type=jnp.float32)
    d_zeds = unskew_rows(d_scores, block_rows, seq_len)
    d_query_v = jnp.einsum("hbw,whd->bhd", d_zeds, nearby, preferred_element_type=jnp.float32)
    d_position = d_position.at[lowest : lowest + window].add(
        jnp.einsum("hbw,bhd->whd", d_zeds, part_v, preferred_element_type=jnp.float32)
    )
    grad_u = d_query_u.reshape(seq_len, local_width) * scaling
    grad_v = d_query_v.reshape(seq_len, local_width) * scaling
    d_queries = (grad_u + grad_v).astype(jnp.bfloat16)
    grad_bias = jnp.stack([jnp.sum(grad_u, axis=0), jnp.sum(grad_v, axis=0)])
    d_projected = jnp.concatenate(
        [
            d_queries,
            d_keys.reshape(seq_len, local_width).astype(jnp.bfloat16),
            d_values.reshape(seq_len, local_width).astype(jnp.bfloat16),
        ],
        axis=1,
    )
    grad_in = contract_rows(whole, d_projected).reshape(model_width, 3, local_width)
    d_normed = contract_cols(d_projected, w_in.reshape(model_width, 3 * local_width))
    grad_pos = contract_rows(
        table_low, d_position.reshape(2 * seq_len, local_width).astype(jnp.bfloat16)
    )
    context = contexts.reshape(seq_len, local_width).astype(jnp.bfloat16)
    grad_out = contract_rows(context, grad_whole)
    return (d_normed, grad_in, grad_pos, grad_bias, grad_out)


def conv_front(whole, w_in, kernel, mask_col):
    seq_len, model_width = whole.shape
    local_width = w_in.shape[2]
    glu_in = matmul(whole, w_in.reshape(model_width, 2 * local_width))
    gate_value = glu_in[:, :local_width]
    logistic = jax.nn.sigmoid(glu_in[:, local_width:])
    glu_out = gate_value * logistic * mask_col
    tap_count = kernel.shape[0]
    half_taps = (tap_count - 1) // 2
    padded = jnp.pad(glu_out, ((half_taps, half_taps), (0, 0)))
    kernel_float = kernel.astype(jnp.float32)
    conved = kernel_float[0] * padded[0:seq_len]
    for tap_index in range(1, tap_count):
        conved = conved + kernel_float[tap_index] * padded[tap_index : tap_index + seq_len]
    return (gate_value, logistic, padded, conved)


def batch_stats(conved, mask_col, frame_count):
    local_sum = jnp.sum(conved * mask_col, axis=0)
    local_squares = jnp.sum(conved * conved * mask_col, axis=0)
    total_sum, total_squares = lax.psum((local_sum, local_squares), "dp")
    average = total_sum / frame_count
    variance = total_squares / frame_count - average * average
    return (average, lax.rsqrt(variance + batch_eps))


def conv_tail(conved, stats, bn_gain, bn_bias):
    average, inv_std = stats
    normed_b = (conved - average) * inv_std * bn_gain.astype(jnp.float32) + bn_bias.astype(
        jnp.float32
    )
    return (normed_b, jax.nn.silu(normed_b).astype(jnp.bfloat16))


def conv_backward(whole, weights, mask_col, stats, frame_count, grad_whole):
    w_in, kernel, bn_gain, bn_bias, w_out = weights
    seq_len, model_width = whole.shape
    local_width = w_in.shape[2]
    gate_value, logistic, padded, conved = conv_front(whole, w_in, kernel, mask_col)
    normed_b, active = conv_tail(conved, stats, bn_gain, bn_bias)
    average, inv_std = stats
    grad_out = contract_rows(active, grad_whole)
    d_normed = contract_cols(grad_whole, w_out) * silu_slope(normed_b)
    centred = (conved - average) * inv_std
    bias_total, gain_total = lax.psum(
        (jnp.sum(d_normed, axis=0), jnp.sum(d_normed * centred, axis=0)), "dp"
    )
    d_conved = (
        bn_gain.astype(jnp.float32)
        * inv_std
        * (d_normed - mask_col * (bias_total + centred * gain_total) / frame_count)
    )
    tap_count = kernel.shape[0]
    half_taps = (tap_count - 1) // 2
    kernel_float = kernel.astype(jnp.float32)
    d_padded = jnp.pad(d_conved, ((half_taps, half_taps), (0, 0)))
    d_glu = kernel_float[0] * d_padded[tap_count - 1 : tap_count - 1 + seq_len]
    for tap_index in range(1, tap_count):
        d_glu = (
            d_glu
            + kernel_float[tap_index]
            * d_padded[tap_count - 1 - tap_index : tap_count - 1 - tap_index + seq_len]
        )
    grad_kernel = jnp.stack(
        [
            jnp.sum(d_conved * padded[tap_index : tap_index + seq_len], axis=0)
            for tap_index in range(tap_count)
        ]
    )
    d_glu = d_glu * mask_col
    d_pair = jnp.concatenate(
        [d_glu * logistic, d_glu * gate_value * logistic * (1.0 - logistic)], axis=1
    ).astype(jnp.bfloat16)
    grad_in = contract_rows(whole, d_pair).reshape(model_width, 2, local_width)
    d_normed_in = contract_cols(d_pair, w_in.reshape(model_width, 2 * local_width))
    return (d_normed_in, grad_in, grad_kernel, grad_out, gain_total, bias_total)


def body(
    frames_in,
    lengths,
    out_grad,
    norm_gains,
    ffn1_up,
    ffn1_down,
    attn_in,
    pos_proj,
    pos_bias,
    attn_out,
    conv_in,
    depthwise,
    bn_scale,
    bn_shift,
    conv_out,
    ffn2_up,
    ffn2_down,
):
    unused, local_rows, model_width = frames_in.shape
    seq_len = local_rows * lax.axis_size("mp")
    block_rows = min(seq_len, 512)
    dp_index = lax.axis_index("dp")
    own_length = lax.dynamic_slice_in_dim(lengths, dp_index, 1)[0]
    valid_keys = jnp.arange(seq_len) < own_length
    mask_col = valid_keys.astype(jnp.float32)[:, None]
    frame_count = jnp.sum(lengths).astype(jnp.float32)
    layer_input = frames_in.reshape(local_rows, model_width).astype(jnp.float32)
    ffn_first = ffn_fetch(ffn1_up, ffn1_down)
    after_first = layer_input + 0.5 * branch_total(
        ffn_forward(enter_block(layer_input, norm_gains[0]), ffn_first)
    )
    attn_held = attn_fetch(attn_in, pos_proj, pos_bias, attn_out)
    after_attn = after_first + branch_total(
        attention_forward(
            enter_block(after_first, norm_gains[1]), attn_held, valid_keys, block_rows
        )
    )
    conv_held = conv_fetch(conv_in, depthwise, bn_scale, bn_shift, conv_out)
    gate_value, logistic, padded, conved = conv_front(
        enter_block(after_attn, norm_gains[2]), conv_held[0], conv_held[1], mask_col
    )
    stats = batch_stats(conved, mask_col, frame_count)
    normed_b, active = conv_tail(conved, stats, conv_held[2], conv_held[3])
    after_conv = after_attn + branch_total(matmul(active, conv_held[4]))
    ffn_second = ffn_fetch(ffn2_up, ffn2_down)
    after_second = after_conv + 0.5 * branch_total(
        ffn_forward(enter_block(after_conv, norm_gains[3]), ffn_second)
    )
    block_out = layer_norm(after_second, norm_gains[4]).astype(jnp.bfloat16)
    d_second, gain_five = norm_back(
        after_second, norm_gains[4], out_grad.reshape(local_rows, model_width).astype(jnp.float32)
    )
    ffn_back_two = ffn_fetch(ffn2_up, ffn2_down)
    d_normed, grad_up_two, grad_down_two = ffn_backward(
        enter_block(after_conv, norm_gains[3]),
        ffn_back_two,
        spread_grads((0.5 * d_second).astype(jnp.bfloat16)),
    )
    d_branch, gain_four = norm_back(after_conv, norm_gains[3], input_total(d_normed))
    d_conv = d_second + d_branch
    conv_back_held = conv_fetch(conv_in, depthwise, bn_scale, bn_shift, conv_out)
    d_normed, grad_conv_in, grad_kernel, grad_conv_out, gain_total, bias_total = conv_backward(
        enter_block(after_attn, norm_gains[2]),
        conv_back_held,
        mask_col,
        stats,
        frame_count,
        spread_grads(d_conv.astype(jnp.bfloat16)),
    )
    d_branch, gain_three = norm_back(after_attn, norm_gains[2], input_total(d_normed))
    d_attn = d_conv + d_branch
    attn_back_held = attn_fetch(attn_in, pos_proj, pos_bias, attn_out)
    d_normed, grad_attn_in, grad_pos, grad_bias, grad_attn_out = attention_backward(
        enter_block(after_first, norm_gains[1]),
        attn_back_held,
        valid_keys,
        block_rows,
        spread_grads(d_attn.astype(jnp.bfloat16)),
    )
    d_branch, gain_two = norm_back(after_first, norm_gains[1], input_total(d_normed))
    d_first = d_attn + d_branch
    ffn_back_one = ffn_fetch(ffn1_up, ffn1_down)
    d_normed, grad_up_one, grad_down_one = ffn_backward(
        enter_block(layer_input, norm_gains[0]),
        ffn_back_one,
        spread_grads((0.5 * d_first).astype(jnp.bfloat16)),
    )
    d_branch, gain_one = norm_back(layer_input, norm_gains[0], input_total(d_normed))
    in_grad = d_first + d_branch
    summed = (
        lax.psum_scatter(grad_up_one, "dp", scatter_dimension=0, tiled=True),
        lax.psum_scatter(grad_down_one, "dp", scatter_dimension=1, tiled=True),
        lax.psum_scatter(grad_attn_in, "dp", scatter_dimension=0, tiled=True),
        lax.psum_scatter(grad_pos, "dp", scatter_dimension=0, tiled=True),
        lax.psum_scatter(grad_bias, "dp", scatter_dimension=1, tiled=True),
        lax.psum_scatter(grad_attn_out, "dp", scatter_dimension=1, tiled=True),
        lax.psum_scatter(grad_conv_in, "dp", scatter_dimension=0, tiled=True),
        lax.psum_scatter(grad_kernel, "dp", scatter_dimension=1, tiled=True),
        lax.psum_scatter(grad_conv_out, "dp", scatter_dimension=1, tiled=True),
        lax.psum_scatter(grad_up_two, "dp", scatter_dimension=0, tiled=True),
        lax.psum_scatter(grad_down_two, "dp", scatter_dimension=1, tiled=True),
    )
    gain_sum = lax.psum(
        jnp.stack([gain_one, gain_two, gain_three, gain_four, gain_five]), ("dp", "mp")
    )
    piece_len = bn_scale.shape[0]
    grad_scale = lax.dynamic_slice_in_dim(gain_total, dp_index * piece_len, piece_len)
    grad_shift = lax.dynamic_slice_in_dim(bias_total, dp_index * piece_len, piece_len)
    return (
        block_out.reshape(1, local_rows, model_width),
        in_grad.reshape(1, local_rows, model_width),
        gain_sum,
        summed[0],
        summed[1],
        summed[2],
        summed[3],
        summed[4],
        summed[5],
        summed[6],
        summed[7],
        grad_scale,
        grad_shift,
        summed[8],
        summed[9],
        summed[10],
    )


def solution(mesh):
    placed = (
        P("dp", "mp", None),
        P(),
        P("dp", "mp", None),
        P(),
        P("dp", "mp"),
        P("mp", "dp"),
        P("dp", None, "mp"),
        P("dp", "mp"),
        P(None, ("mp", "dp")),
        P("mp", "dp"),
        P("dp", None, "mp"),
        P(None, ("mp", "dp")),
        P(("mp", "dp")),
        P(("mp", "dp")),
        P("mp", "dp"),
        P("dp", "mp"),
        P("mp", "dp"),
    )
    return jax.shard_map(
        body,
        mesh=mesh,
        in_specs=placed,
        out_specs=(
            P("dp", "mp", None),
            P("dp", "mp", None),
            P(),
            P("dp", "mp"),
            P("mp", "dp"),
            P("dp", None, "mp"),
            P("dp", "mp"),
            P(None, ("mp", "dp")),
            P("mp", "dp"),
            P("dp", None, "mp"),
            P(None, ("mp", "dp")),
            P(("mp", "dp")),
            P(("mp", "dp")),
            P("mp", "dp"),
            P("dp", "mp"),
            P("mp", "dp"),
        ),
        check_vma=False,
    )
```

profile of v0, /device:TPU:0, one launch (start us, length us, event | category | flops | bytes accessed | tf_op | source)
XLA Modules:
  0.0 1316.5 jit_solution(2508751942611747793)
XLA Ops:
  13.9 29.3 %all-gather.17.cloned.1.call-done = bf16[512,1024]{1,0:T(8,128)(2,1)} async-done(((bf16[128,1024]{1,0:T(8,128)(2,1)}), bf16[512,1024]{1,0:T(8,128)(2,1)}) %all-gather.17.cloned.1.call-update) | async-done | bytes 1048592 | tf_op jit(solution)/shard_map/all_gather | solution.py:59
  43.2 29.1 %all-gather.19.cloned.1.call-done = bf16[1024,1024]{1,0:T(8,128)(2,1)} async-done(((bf16[128,1024]{1,0:T(8,128)(2,1)}), bf16[1024,1024]{1,0:T(8,128)(2,1)}) %all-gather.19.cloned.1.call-update) | async-done | bytes 2097168 | tf_op jit(solution)/shard_map/all_gather | solution.py:84
  75.5 26.8 %all-gather.21.cloned.1.call-done = bf16[1024,1024]{1,0:T(8,128)(2,1)} async-done(((bf16[1024,128]{1,0:T(8,128)(2,1)}), bf16[1024,1024]{1,0:T(8,128)(2,1)}) %all-gather.21.cloned.1.call-update) | async-done | bytes 2097168 | tf_op jit(solution)/shard_map/all_gather | solution.py:85
  107.1 8.7 all-gather
  115.9 17.7 %reduce-scatter.23.cloned.1.call-done = bf16[128,1024]{1,0:T(8,128)(2,1)} async-done(((bf16[512,1024]{1,0:T(8,128)(2,1)}), bf16[128,1024]{1,0:T(8,128)(2,1)}) %reduce-scatter.23.cloned.1.call-update) | async-done | bytes 262160 | tf_op jit(solution)/shard_map/reduce_scatter | solution.py:67
  137.9 8.1 multiply_sine_fusion
  154.5 9.9 all_gather.86
  164.4 11.2 all_gather.87
  176.4 14.6 %all-gather.23.cloned.1.call-done = bf16[512,1024]{1,0:T(8,128)(2,1)} async-done(((bf16[128,1024]{1,0:T(8,128)(2,1)}), bf16[512,1024]{1,0:T(8,128)(2,1)}) %all-gather.23.cloned.1.call-update) | async-done | bytes 1048592 | tf_op jit(solution)/shard_map/all_gather | solution.py:59
  197.4 9.7 reshape.427
  207.2 7.8 slice.186
  215.0 9.9 reshape.428
  238.3 26.0 %reduce-scatter.25.cloned.1.call-done = bf16[128,1024]{1,0:T(8,128)(2,1)} async-done(((bf16[512,1024]{1,0:T(8,128)(2,1)}), bf16[128,1024]{1,0:T(8,128)(2,1)}) %reduce-scatter.25.cloned.1.call-update) | async-done | bytes 262160 | tf_op jit(solution)/shard_map/reduce_scatter | solution.py:67
  267.3 8.9 all-gather.1
  278.0 13.3 %all-reduce.10 = (bf16[256]{0:T(256)(128)(2,1)S(1)}, bf16[256]{0:T(256)(128)(2,1)S(1)}) all-reduce(bf16[256]{0:T(256)(128)(2,1)S(1)} %dynamic-update-slice.4, bf16[256]{0:T(256)(128)(2,1)S(1)} %dynamic-update-slice.3), channel_id=1, replica_groups=mesh['dp'=8,'mp'=4] {'dp'}, use_global_device_ids=true, to_apply=%add.6 | all-reduce | flops 512 | bytes 2048
  292.6 11.1 all_gather.93
  306.1 12.2 all-gather.27.cloned.1.call-done
  322.9 13.1 all-reduce.9
  339.6 24.8 %reduce-scatter.27.cloned.1.call-done = bf16[128,1024]{1,0:T(8,128)(2,1)} async-done(((bf16[512,1024]{1,0:T(8,128)(2,1)}), bf16[128,1024]{1,0:T(8,128)(2,1)}) %reduce-scatter.27.cloned.1.call-update) | async-done | bytes 262160 | tf_op jit(solution)/shard_map/reduce_scatter | solution.py:67
  367.4 25.2 %all-gather.33.cloned.1.call-done = bf16[1024,1024]{1,0:T(8,128)(2,1)} async-done(((bf16[128,1024]{1,0:T(8,128)(2,1)}), bf16[1024,1024]{1,0:T(8,128)(2,1)}) %all-gather.33.cloned.1.call-update) | async-done | bytes 2097168 | tf_op jit(solution)/shard_map/all_gather | solution.py:84
  392.6 30.0 %all-gather.31.cloned.1.call-done = bf16[512,1024]{1,0:T(8,128)(2,1)} async-done(((bf16[128,1024]{1,0:T(8,128)(2,1)}), bf16[512,1024]{1,0:T(8,128)(2,1)}) %all-gather.31.cloned.1.call-update) | async-done | bytes 1048592 | tf_op jit(solution)/shard_map/all_gather | solution.py:59
  422.6 4.6 fusion.82
  427.2 24.8 %all-gather.35.cloned.1.call-done = bf16[1024,1024]{1,0:T(8,128)(2,1)} async-done(((bf16[1024,128]{1,0:T(8,128)(2,1)}), bf16[1024,1024]{1,0:T(8,128)(2,1)}) %all-gather.35.cloned.1.call-update) | async-done | bytes 2097168 | tf_op jit(solution)/shard_map/all_gather | solution.py:85
  452.0 4.5 convolution_convert_fusion.3
  456.6 27.4 %reduce-scatter.29.cloned.1.call-done = bf16[128,1024]{1,0:T(8,128)(2,1)} async-done(((bf16[512,1024]{1,0:T(8,128)(2,1)}), bf16[128,1024]{1,0:T(8,128)(2,1)}) %reduce-scatter.29.cloned.1.call-update) | async-done | bytes 262160 | tf_op jit(solution)/shard_map/reduce_scatter | solution.py:67
  489.2 26.6 %all-gather.37.cloned.1.call-done = bf16[512,1024]{1,0:T(8,128)(2,1)} async-done(((bf16[128,1024]{1,0:T(8,128)(2,1)}), bf16[512,1024]{1,0:T(8,128)(2,1)}) %all-gather.37.cloned.1.call-update) | async-done | bytes 1048592 | tf_op jit(solution)/shard_map/all_gather | solution.py:73
  523.4 26.8 %reduce-scatter.31.cloned.1.call-done = bf16[128,1024]{1,0:T(8,128)(2,1)} async-done(((bf16[512,1024]{1,0:T(8,128)(2,1)}), bf16[128,1024]{1,0:T(8,128)(2,1)}) %reduce-scatter.31.cloned.1.call-update) | async-done | bytes 262160 | tf_op jit(solution)/shard_map/reduce_scatter | solution.py:77
  555.0 26.6 %all-gather.39.cloned.1.call-done = bf16[512,1024]{1,0:T(8,128)(2,1)} async-done(((bf16[128,1024]{1,0:T(8,128)(2,1)}), bf16[512,1024]{1,0:T(8,128)(2,1)}) %all-gather.39.cloned.1.call-update) | async-done | bytes 1048592 | tf_op jit(solution)/shard_map/all_gather | solution.py:73
  584.5 13.1 all-reduce.8
  602.5 25.5 %reduce-scatter.33.cloned.1.call-done = bf16[128,1024]{1,0:T(8,128)(2,1)} async-done(((bf16[512,1024]{1,0:T(8,128)(2,1)}), bf16[128,1024]{1,0:T(8,128)(2,1)}) %reduce-scatter.33.cloned.1.call-update) | async-done | bytes 262160 | tf_op jit(solution)/shard_map/reduce_scatter | solution.py:77
  632.6 26.6 %all-gather.41.cloned.1.call-done = bf16[512,1024]{1,0:T(8,128)(2,1)} async-done(((bf16[128,1024]{1,0:T(8,128)(2,1)}), bf16[512,1024]{1,0:T(8,128)(2,1)}) %all-gather.41.cloned.1.call-update) | async-done | bytes 1048592 | tf_op jit(solution)/shard_map/all_gather | solution.py:73
  671.6 5.1 reshape.464
  687.1 5.1 reshape.433
  697.9 26.4 %reduce-scatter.35.cloned.1.call-done = bf16[128,1024]{1,0:T(8,128)(2,1)} async-done(((bf16[512,1024]{1,0:T(8,128)(2,1)}), bf16[128,1024]{1,0:T(8,128)(2,1)}) %reduce-scatter.35.cloned.1.call-update) | async-done | bytes 262160 | tf_op jit(solution)/shard_map/reduce_scatter | solution.py:77
  738.7 17.2 %all-gather.43.cloned.1.call-done = bf16[512,1024]{1,0:T(8,128)(2,1)} async-done(((bf16[128,1024]{1,0:T(8,128)(2,1)}), bf16[512,1024]{1,0:T(8,128)(2,1)}) %all-gather.43.cloned.1.call-update) | async-done | bytes 1048592 | tf_op jit(solution)/shard_map/all_gather | solution.py:73
  766.3 4.8 fusion.86
  772.3 4.9 fusion.62
  801.2 55.6 %all-reduce.13.cloned.1.call-done = f32[1024,2,256]{2,1,0:T(2,128)} async-done(((f32[1024,2,256]{2,1,0:T(2,128)}), f32[1024,2,256]{2,1,0:T(2,128)}) %all-reduce.13.cloned.1.call-update) | async-done | bytes 2097168
  858.5 33.9 %reduce-scatter.55.cloned.1.call-done = f32[32,2]{1,0:T(8,128)} async-done(((f32[256,2]{1,0:T(8,128)}), f32[32,2]{1,0:T(8,128)}) %reduce-scatter.55.cloned.1.call-update) | async-done | bytes 272
  893.8 28.3 %reduce-scatter.37.cloned.1.call-done = bf16[128,1024]{1,0:T(8,128)(2,1)} async-done(((bf16[512,1024]{1,0:T(8,128)(2,1)}), bf16[128,1024]{1,0:T(8,128)(2,1)}) %reduce-scatter.37.cloned.1.call-update) | async-done | bytes 262160 | tf_op jit(solution)/shard_map/reduce_scatter | solution.py:77
  924.5 39.4 %psum.39 = f32[5,1024]{1,0:T(8,128)} all-reduce(f32[5,1024]{1,0:T(8,128)S(1)} %stack.44), channel_id=1, replica_groups=mesh['dp'=8,'mp'=4] {'dp','mp'}, use_global_device_ids=true, to_apply=%region_45.46 | all-reduce | flops 5120 | bytes 40960 | tf_op jit(solution)/shard_map/psum | solution.py:436
  965.9 49.1 %reduce-scatter.51.cloned.1.call-done = f32[128,1024]{1,0:T(8,128)} async-done(((f32[1024,1024]{1,0:T(8,128)}), f32[128,1024]{1,0:T(8,128)}) %reduce-scatter.51.cloned.1.call-update) | async-done | bytes 524304 | tf_op jit(solution)/shard_map/reduce_scatter | solution.py:433
  1015.1 55.0 %reduce-scatter.53.cloned.1.call-done = f32[1024,128]{1,0:T(8,128)} async-done(((f32[1024,1024]{1,0:T(8,128)}), f32[1024,128]{1,0:T(8,128)}) %reduce-scatter.53.cloned.1.call-update) | async-done | bytes 524304 | tf_op jit(solution)/shard_map/reduce_scatter | solution.py:434
  1070.1 39.8 %reduce-scatter.45.cloned.1.call-done = f32[128,256]{1,0:T(8,128)} async-done(((f32[1024,256]{1,0:T(8,128)}), f32[128,256]{1,0:T(8,128)}) %reduce-scatter.45.cloned.1.call-update) | async-done | bytes 131088 | tf_op jit(solution)/shard_map/reduce_scatter | solution.py:427
  1109.9 39.6 %reduce-scatter.47.cloned.1.call-done = f32[256,128]{1,0:T(8,128)} async-done(((f32[256,1024]{1,0:T(8,128)}), f32[256,128]{1,0:T(8,128)}) %reduce-scatter.47.cloned.1.call-update) | async-done | bytes 131088 | tf_op jit(solution)/shard_map/reduce_scatter | solution.py:429
  1149.5 50.0 %reduce-scatter.43.cloned.1.call-done = f32[128,3,256]{2,0,1:T(8,128)} async-done(((f32[1024,3,256]{2,0,1:T(8,128)}), f32[128,3,256]{2,0,1:T(8,128)}) %reduce-scatter.43.cloned.1.call-update) | async-done | bytes 393232 | tf_op jit(solution)/shard_map/reduce_scatter | solution.py:426
  1199.5 55.1 %reduce-scatter.39.cloned.1.call-done = f32[128,1024]{1,0:T(8,128)} async-done(((f32[1024,1024]{1,0:T(8,128)}), f32[128,1024]{1,0:T(8,128)}) %reduce-scatter.39.cloned.1.call-update) | async-done | bytes 524304 | tf_op jit(solution)/shard_map/reduce_scatter | solution.py:424
  1254.6 54.9 %reduce-scatter.41.cloned.1.call-done = f32[1024,128]{1,0:T(8,128)} async-done(((f32[1024,1024]{1,0:T(8,128)}), f32[1024,128]{1,0:T(8,128)}) %reduce-scatter.41.cloned.1.call-update) | async-done | bytes 524304 | tf_op jit(solution)/shard_map/reduce_scatter | solution.py:425
  (325 shorter events, 180.9 us)
Async XLA Ops:
  7.2 36.0 %all-gather.17.cloned.1.call-start = ((), (), s32[]{:S(2)}) async-start(), calls=%async_computation.18 | async-start | bytes 1310720 | tf_op jit(solution)/shard_map/all_gather | solution.py:59
  12.4 59.9 %all-gather.19.cloned.1.call-start = ((), (), s32[]{:S(2)}) async-start(), calls=%async_computation.19 | async-start | bytes 2359296 | tf_op jit(solution)/shard_map/all_gather | solution.py:84
  13.1 89.2 %all-gather.21.cloned.1.call-start = ((), (), s32[]{:S(2)}) async-start(), calls=%async_computation.20 | async-start | bytes 2359296 | tf_op jit(solution)/shard_map/all_gather | solution.py:85
  13.8 119.8 %reduce-scatter.23.cloned.1.call-start = ((), (), s32[]{:S(2)}) async-start(), calls=%async_computation.21 | async-start | bytes 1310720 | tf_op jit(solution)/shard_map/reduce_scatter | solution.py:67
  75.5 30.7 %copy-start.56 = (f32[512,1024]{1,0:T(8,128)}, f32[512,1024]{1,0:T(8,128)S(1)}, u32[]{:S(2)}) copy-start(f32[512,1024]{1,0:T(8,128)S(1)} %fusion.78) | copy-start | bytes 6291460
  75.5 30.8 %copy-start.41 = (bf16[128,3,256]{2,0,1:T(8,128)(2,1)S(1)}, bf16[128,3,256]{2,0,1:T(8,128)(2,1)}, u32[]{:S(2)}) copy-start(bf16[128,3,256]{2,0,1:T(8,128)(2,1)} %param.25) | copy-start | bytes 589828
  75.5 31.6 %copy-start.47 = (bf16[2,32]{1,0:T(2,128)(2,1)S(1)}, bf16[2,32]{1,0:T(2,128)(2,1)}, u32[]{:S(2)}) copy-start(bf16[2,32]{1,0:T(2,128)(2,1)} %param.27) | copy-start | bytes 388
  75.5 58.1 %copy-start = (bf16[1,128,1024]{2,1,0:T(8,128)(2,1)S(1)}, bf16[1,128,1024]{2,1,0:T(8,128)(2,1)}, u32[]{:S(2)}) copy-start(bf16[1,128,1024]{2,1,0:T(8,128)(2,1)} %param.19) | copy-start | bytes 786436
  106.2 70.2 %all-gather.25.cloned.1.call-start = ((), (), s32[]{:S(2)}) async-start(), calls=%async_computation.23 | async-start | bytes 1769472 | tf_op jit(solution)/shard_map/all_gather | solution.py:91
  107.1 83.9 %all-gather.23.cloned.1.call-start = ((), (), s32[]{:S(2)}) async-start(), calls=%async_computation.22 | async-start | bytes 1310720 | tf_op jit(solution)/shard_map/all_gather | solution.py:59
  137.7 126.6 %reduce-scatter.25.cloned.1.call-start = ((), (), s32[]{:S(2)}) async-start(), calls=%async_computation.24 | async-start | bytes 1310720 | tf_op jit(solution)/shard_map/reduce_scatter | solution.py:67
  232.3 432.5 %copy-start.3 = (f32[2,512,512]{1,2,0:T(8,128)}, f32[2,512,512]{1,2,0:T(8,128)S(1)}, u32[]{:S(2)}) copy-start(f32[2,512,512]{1,2,0:T(8,128)S(1)} %get-tuple-element.101) | copy-start | bytes 6291460
  236.0 29.5 %copy-start.25 = (bf16[2,128,512]{2,1,0:T(8,128)(2,1)}, bf16[2,128,512]{2,1,0:T(8,128)(2,1)S(1)}, u32[]{:S(2)}) copy-start(bf16[2,128,512]{2,1,0:T(8,128)(2,1)S(1)} %convolution_convert_fusion.12) | copy-start | bytes 786436
  237.4 29.8 %copy-start.45 = (bf16[5,32]{1,0:T(8,128)(2,1)S(1)}, bf16[5,32]{1,0:T(8,128)(2,1)}, u32[]{:S(2)}) copy-start(bf16[5,32]{1,0:T(8,128)(2,1)} %param.30) | copy-start | bytes 964
  237.4 38.8 %copy-start.46 = (u32[32]{0:T(128)S(1)}, u32[32]{0:T(128)}, u32[]{:S(2)}) copy-start(u32[32]{0:T(128)} %constant.110) | copy-start | bytes 388
  237.4 40.0 %copy-start.54 = (bf16[32]{0:T(256)(128)(2,1)S(1)}, bf16[32]{0:T(256)(128)(2,1)}, u32[]{:S(2)}) copy-start(bf16[32]{0:T(256)(128)(2,1)} %param.32) | copy-start | bytes 196
  237.4 40.3 %copy-start.55 = (bf16[32]{0:T(256)(128)(2,1)S(1)}, bf16[32]{0:T(256)(128)(2,1)}, u32[]{:S(2)}) copy-start(bf16[32]{0:T(256)(128)(2,1)} %param.31) | copy-start | bytes 196
  237.4 55.2 %copy-start.44 = (bf16[256,128]{1,0:T(8,128)(2,1)S(1)}, bf16[256,128]{1,0:T(8,128)(2,1)}, u32[]{:S(2)}) copy-start(bf16[256,128]{1,0:T(8,128)(2,1)} %param.33) | copy-start | bytes 196612
  237.5 66.2 %all-gather.29.cloned.1.call-start = ((), (), s32[]{:S(2)}) async-start(), calls=%async_computation.26 | async-start | bytes 1179648 | tf_op jit(solution)/shard_map/all_gather | solution.py:100
  238.2 80.1 %all-gather.27.cloned.1.call-start = ((), (), s32[]{:S(2)}) async-start(), calls=%async_computation.25 | async-start | bytes 1310720 | tf_op jit(solution)/shard_map/all_gather | solution.py:59
  266.6 97.8 %reduce-scatter.27.cloned.1.call-start = ((), (), s32[]{:S(2)}) async-start(), calls=%async_computation.27 | async-start | bytes 1310720 | tf_op jit(solution)/shard_map/reduce_scatter | solution.py:67
  338.8 53.8 %all-gather.33.cloned.1.call-start = ((), (), s32[]{:S(2)}) async-start(), calls=%async_computation.29 | async-start | bytes 2359296 | tf_op jit(solution)/shard_map/all_gather | solution.py:84
  339.6 83.0 %all-gather.31.cloned.1.call-start = ((), (), s32[]{:S(2)}) async-start(), calls=%async_computation.28 | async-start | bytes 1310720 | tf_op jit(solution)/shard_map/all_gather | solution.py:59
  366.6 85.4 %all-gather.35.cloned.1.call-start = ((), (), s32[]{:S(2)}) async-start(), calls=%async_computation.30 | async-start | bytes 2359296 | tf_op jit(solution)/shard_map/all_gather | solution.py:85
  367.3 116.6 %reduce-scatter.29.cloned.1.call-start = ((), (), s32[]{:S(2)}) async-start(), calls=%async_computation.31 | async-start | bytes 1310720 | tf_op jit(solution)/shard_map/reduce_scatter | solution.py:67
  456.5 59.3 %all-gather.37.cloned.1.call-start = ((), (), s32[]{:S(2)}) async-start(), calls=%async_computation.32 | async-start | bytes 1310720 | tf_op jit(solution)/shard_map/all_gather | solution.py:73
  489.2 61.1 %reduce-scatter.31.cloned.1.call-start = ((), (), s32[]{:S(2)}) async-start(), calls=%async_computation.33 | async-start | bytes 1310720 | tf_op jit(solution)/shard_map/reduce_scatter | solution.py:77
  523.4 58.2 %all-gather.39.cloned.1.call-start = ((), (), s32[]{:S(2)}) async-start(), calls=%async_computation.34 | async-start | bytes 1310720 | tf_op jit(solution)/shard_map/all_gather | solution.py:73
  555.0 42.6 %copy-start.10 = (f32[512,256]{1,0:T(8,128)S(1)}, f32[512,256]{1,0:T(8,128)}, u32[]{:S(2)}) copy-start(f32[512,256]{1,0:T(8,128)} %copy-done.9) | copy-start | bytes 1572868
  555.0 73.0 %reduce-scatter.33.cloned.1.call-start = ((), (), s32[]{:S(2)}) async-start(), calls=%async_computation.35 | async-start | bytes 1310720 | tf_op jit(solution)/shard_map/reduce_scatter | solution.py:77
  602.4 56.8 %all-gather.41.cloned.1.call-start = ((), (), s32[]{:S(2)}) async-start(), calls=%async_computation.36 | async-start | bytes 1310720 | tf_op jit(solution)/shard_map/all_gather | solution.py:73
  630.5 34.2 %copy-start.7 = (f32[128,1024]{1,0:T(8,128)}, f32[128,1024]{1,0:T(8,128)S(1)}, u32[]{:S(2)}) copy-start(f32[128,1024]{1,0:T(8,128)S(1)} %get-tuple-element.57) | copy-start | bytes 1572868
  632.6 91.7 %reduce-scatter.35.cloned.1.call-start = ((), (), s32[]{:S(2)}) async-start(), calls=%async_computation.37 | async-start | bytes 1310720 | tf_op jit(solution)/shard_map/reduce_scatter | solution.py:77
  697.4 29.5 %copy-start.8 = (f32[128,1024]{1,0:T(8,128)S(1)}, f32[128,1024]{1,0:T(8,128)}, u32[]{:S(2)}) copy-start(f32[128,1024]{1,0:T(8,128)} %copy-done.7) | copy-start | bytes 1572868
  697.5 58.4 %all-gather.43.cloned.1.call-start = ((), (), s32[]{:S(2)}) async-start(), calls=%async_computation.38 | async-start | bytes 1310720 | tf_op jit(solution)/shard_map/all_gather | solution.py:73
  729.2 70.6 %reduce-scatter.57.cloned.1.call-start = ((), (), s32[]{:S(2)}) async-start(), calls=%async_computation.49 | async-start | bytes 147456
  730.1 126.7 %all-reduce.13.cloned.1.call-start = ((), (), s32[]{:S(2)}) async-start(), calls=%async_computation.50 | async-start | bytes 4194304
  737.7 154.7 %reduce-scatter.55.cloned.1.call-start = ((), (), s32[]{:S(2)}) async-start(), calls=%async_computation.48 | async-start | bytes 147456
  738.6 183.4 %reduce-scatter.37.cloned.1.call-start = ((), (), s32[]{:S(2)}) async-start(), calls=%async_computation.39 | async-start | bytes 1310720 | tf_op jit(solution)/shard_map/reduce_scatter | solution.py:77
  763.4 202.5 %reduce-scatter.49.cloned.1.call-start = ((), (), s32[]{:S(2)}) async-start(), calls=%async_computation.45 | async-start | bytes 1179648 | tf_op jit(solution)/shard_map/reduce_scatter | solution.py:432
  766.3 248.8 %reduce-scatter.51.cloned.1.call-start = ((), (), s32[]{:S(2)}) async-start(), calls=%async_computation.46 | async-start | bytes 4718592 | tf_op jit(solution)/shard_map/reduce_scatter | solution.py:433
  771.1 299.0 %reduce-scatter.53.cloned.1.call-start = ((), (), s32[]{:S(2)}) async-start(), calls=%async_computation.47 | async-start | bytes 4718592 | tf_op jit(solution)/shard_map/reduce_scatter | solution.py:434
  777.2 332.6 %reduce-scatter.45.cloned.1.call-start = ((), (), s32[]{:S(2)}) async-start(), calls=%async_computation.43 | async-start | bytes 1179648 | tf_op jit(solution)/shard_map/reduce_scatter | solution.py:427
  781.5 368.0 %reduce-scatter.47.cloned.1.call-start = ((), (), s32[]{:S(2)}) async-start(), calls=%async_computation.44 | async-start | bytes 1179648 | tf_op jit(solution)/shard_map/reduce_scatter | solution.py:429
  783.0 416.5 %reduce-scatter.43.cloned.1.call-start = ((), (), s32[]{:S(2)}) async-start(), calls=%async_computation.42 | async-start | bytes 3538944 | tf_op jit(solution)/shard_map/reduce_scatter | solution.py:426
  788.0 466.7 %reduce-scatter.39.cloned.1.call-start = ((), (), s32[]{:S(2)}) async-start(), calls=%async_computation.40 | async-start | bytes 4718592 | tf_op jit(solution)/shard_map/reduce_scatter | solution.py:424
  792.8 516.7 %reduce-scatter.41.cloned.1.call-start = ((), (), s32[]{:S(2)}) async-start(), calls=%async_computation.41 | async-start | bytes 4718592 | tf_op jit(solution)/shard_map/reduce_scatter | solution.py:425
  797.9 166.0 %copy-start.20 = (f32[128,1024]{1,0:T(8,128)S(1)}, f32[128,1024]{1,0:T(8,128)}, u32[]{:S(2)}) copy-start(f32[128,1024]{1,0:T(8,128)} %get-tuple-element.55) | copy-start | bytes 1572868
  (44 other events, 212.3 us)
Sparse Core Ops, SparseCore 0:
  12.5 30.6 all-gather.16
  45.1 27.1 all-gather.18
  74.2 28.0 all-gather.20
  106.3 27.2 reduce-scatter.22
  135.9 24.2 all-gather.24
  162.2 28.6 all-gather.22
  237.6 26.6 reduce-scatter.24
  266.2 21.9 all-gather.28
  290.3 27.9 all-gather.26
  339.0 25.4 reduce-scatter.26
  366.3 26.2 all-gather.32
  394.6 27.9 all-gather.30
  424.5 27.4 all-gather.34
  456.6 27.2 reduce-scatter.28
  489.3 26.4 all-gather.36
  523.5 26.6 reduce-scatter.30
  555.1 26.4 all-gather.38
  602.6 25.4 reduce-scatter.32
  632.7 26.4 all-gather.40
  697.6 26.6 reduce-scatter.34
  729.4 26.4 all-gather.42
  758.9 32.9 reduce-scatter.56
  795.1 61.7 all-reduce.12
  859.7 32.6 reduce-scatter.54
  894.7 27.2 reduce-scatter.36
  925.6 34.5 reduce-scatter.48
  964.0 51.0 reduce-scatter.50
  1019.0 51.0 reduce-scatter.52
  1073.9 35.9 reduce-scatter.44
  1113.5 35.9 reduce-scatter.46
  1153.4 46.0 reduce-scatter.42
  1203.4 51.1 reduce-scatter.38
  1258.4 51.0 reduce-scatter.40
where the time goes:
time: 1320 us
  waiting for transfers between devices  929 us (70%)
  blocking collectives  129 us (10%)
  local copies, waits for them, and re-layouts  94.3 us (7%)
  matrix products  92.1 us (7%)
  other arithmetic  53.2 us (4%)
  between operations  17.6 us (1%)
    reduce_scatter x4, waiting for transfers between devices, input_total(): lax.psum_scatter(partial_value.astype(jnp.bfloat16), 'mp', scatter_dimens...  107 us
    all_gather x4, waiting for transfers between devices, spread_grads(): return lax.all_gather(upstream, 'mp', axis=0, tiled=True)  96.9 us
    reduce_scatter x4, waiting for transfers between devices, branch_total(): lax.psum_scatter(partial_value.astype(jnp.bfloat16), 'mp', scatter_dimens...  95.9 us
    unnamed x36, waiting for transfers between devices  93.2 us
    all_gather x4, waiting for transfers between devices, spread_rows(): return lax.all_gather(normed, 'mp', axis=0, tiled=True)  86.1 us
    reduce_scatter x1, waiting for transfers between devices, body(): lax.psum_scatter(grad_up_one, 'dp', scatter_dimension=0, tiled=True)  55.1 us
    reduce_scatter x1, waiting for transfers between devices, body(): lax.psum_scatter(grad_down_two, 'dp', scatter_dimension=1, tiled=True)  55 us
    reduce_scatter x1, waiting for transfers between devices, body(): lax.psum_scatter(grad_down_one, 'dp', scatter_dimension=1, tiled=True)  54.9 us
  transfers between devices with their start and end apart: 33, of which 29 were waited for; matrix products, arithmetic and copies ran while one was open for 7% of the time, Pallas kernels for 0%

commit v1 on v0

--- a/solution.py
+++ b/solution.py
@@ -76,6 +76,12 @@
 def input_total(partial_value):
     return lax.psum_scatter(
         partial_value.astype(jnp.bfloat16), "mp", scatter_dimension=0, tiled=True
+    ).astype(jnp.float32)
+
+
+def grad_total(partial_value, dimension):
+    return lax.psum_scatter(
+        partial_value.astype(jnp.bfloat16), "dp", scatter_dimension=dimension, tiled=True
     ).astype(jnp.float32)
 
 
@@ -421,17 +427,17 @@
     d_branch, gain_one = norm_back(layer_input, norm_gains[0], input_total(d_normed))
     in_grad = d_first + d_branch
     summed = (
-        lax.psum_scatter(grad_up_one, "dp", scatter_dimension=0, tiled=True),
-        lax.psum_scatter(grad_down_one, "dp", scatter_dimension=1, tiled=True),
-        lax.psum_scatter(grad_attn_in, "dp", scatter_dimension=0, tiled=True),
-        lax.psum_scatter(grad_pos, "dp", scatter_dimension=0, tiled=True),
-        lax.psum_scatter(grad_bias, "dp", scatter_dimension=1, tiled=True),
-        lax.psum_scatter(grad_attn_out, "dp", scatter_dimension=1, tiled=True),
-        lax.psum_scatter(grad_conv_in, "dp", scatter_dimension=0, tiled=True),
-        lax.psum_scatter(grad_kernel, "dp", scatter_dimension=1, tiled=True),
-        lax.psum_scatter(grad_conv_out, "dp", scatter_dimension=1, tiled=True),
-        lax.psum_scatter(grad_up_two, "dp", scatter_dimension=0, tiled=True),
-        lax.psum_scatter(grad_down_two, "dp", scatter_dimension=1, tiled=True),
+        grad_total(grad_up_one, 0),
+        grad_total(grad_down_one, 1),
+        grad_total(grad_attn_in, 0),
+        grad_total(grad_pos, 0),
+        grad_total(grad_bias, 1),
+        grad_total(grad_attn_out, 1),
+        grad_total(grad_conv_in, 0),
+        grad_total(grad_kernel, 1),
+        grad_total(grad_conv_out, 1),
+        grad_total(grad_up_two, 0),
+        grad_total(grad_down_two, 1),
     )
     gain_sum = lax.psum(
         jnp.stack([gain_one, gain_two, gain_three, gain_four, gain_five]), ("dp", "mp")

time: 1320 us -> 1260 us (0.955)
  waiting for transfers between devices: 929 us -> 853 us
    reduce_scatter x8 -> x4, waiting for transfers between devices: 344 us -> 160 us  [grad_total(): lax.psum_scatter(partial_value.astype(jnp.bfloat16), 'dp', scatter_dimens...]
    unnamed x36 -> x40, waiting for transfers between devices: 93.2 us -> 218 us
    all_gather x4, waiting for transfers between devices: 96.9 us -> 79.8 us  [spread_grads(): return lax.all_gather(upstream, 'mp', axis=0, tiled=True)]
    unnamed x132 -> x143, local copies, waits for them, and re-layouts: 33 us -> 41.5 us
  transfers between devices with their start and end apart: 33 -> 33, of which waited for: 29 -> 29; matrix products, arithmetic and copies ran while one was open for 7% -> 9% of each run, Pallas kernels for 0% -> 0%
where the time goes in v1:
time: 1260 us
  waiting for transfers between devices  853 us (68%)
  blocking collectives  129 us (10%)
  local copies, waits for them, and re-layouts  102 us (8%)
  matrix products  89 us (7%)
  other arithmetic  65.8 us (5%)
  between operations  17.6 us (1%)
    unnamed x40, waiting for transfers between devices  218 us
    reduce_scatter x4, waiting for transfers between devices, grad_total(): lax.psum_scatter(partial_value.astype(jnp.bfloat16), 'dp', scatter_dimens...  160 us
    reduce_scatter x4, waiting for transfers between devices, input_total(): lax.psum_scatter(partial_value.astype(jnp.bfloat16), 'mp', scatter_dimens...  107 us
    reduce_scatter x4, waiting for transfers between devices, branch_total(): lax.psum_scatter(partial_value.astype(jnp.bfloat16), 'mp', scatter_dimens...  95.9 us
    all_gather x4, waiting for transfers between devices, spread_rows(): return lax.all_gather(normed, 'mp', axis=0, tiled=True)  86 us
    all_gather x4, waiting for transfers between devices, spread_grads(): return lax.all_gather(upstream, 'mp', axis=0, tiled=True)  79.8 us
    all_gather x2, waiting for transfers between devices, ffn_fetch(): lax.all_gather(w_up, 'dp', axis=0, tiled=True)  54.3 us
    all_gather x2, waiting for transfers between devices, ffn_fetch(): lax.all_gather(w_down, 'dp', axis=1, tiled=True)  51.7 us
  transfers between devices with their start and end apart: 33, of which 29 were waited for; matrix products, arithmetic and copies ran while one was open for 9% of the time, Pallas kernels for 0%

profile of v1, /device:TPU:0, one launch (start us, length us, event | category | flops | bytes accessed | tf_op | source)
XLA Modules:
  0.0 1257.3 jit_solution(1732583593232434804)
XLA Ops:
  13.9 29.3 %all-gather.17.cloned.1.call-done = bf16[512,1024]{1,0:T(8,128)(2,1)} async-done(((bf16[128,1024]{1,0:T(8,128)(2,1)}), bf16[512,1024]{1,0:T(8,128)(2,1)}) %all-gather.17.cloned.1.call-update) | async-done | bytes 1048592 | tf_op jit(solution)/shard_map/all_gather | solution.py:59
  43.2 29.1 %all-gather.19.cloned.1.call-done = bf16[1024,1024]{1,0:T(8,128)(2,1)} async-done(((bf16[128,1024]{1,0:T(8,128)(2,1)}), bf16[1024,1024]{1,0:T(8,128)(2,1)}) %all-gather.19.cloned.1.call-update) | async-done | bytes 2097168 | tf_op jit(solution)/shard_map/all_gather | solution.py:90
  75.5 26.8 %all-gather.21.cloned.1.call-done = bf16[1024,1024]{1,0:T(8,128)(2,1)} async-done(((bf16[1024,128]{1,0:T(8,128)(2,1)}), bf16[1024,1024]{1,0:T(8,128)(2,1)}) %all-gather.21.cloned.1.call-update) | async-done | bytes 2097168 | tf_op jit(solution)/shard_map/all_gather | solution.py:91
  107.1 8.8 all-gather
  115.9 17.7 %reduce-scatter.31.cloned.1.call-done = bf16[128,1024]{1,0:T(8,128)(2,1)} async-done(((bf16[512,1024]{1,0:T(8,128)(2,1)}), bf16[128,1024]{1,0:T(8,128)(2,1)}) %reduce-scatter.31.cloned.1.call-update) | async-done | bytes 262160 | tf_op jit(solution)/shard_map/reduce_scatter | solution.py:67
  137.9 8.1 multiply_sine_fusion
  154.5 9.9 all_gather.86
  164.4 11.2 all_gather.87
  176.4 14.6 %all-gather.23.cloned.1.call-done = bf16[512,1024]{1,0:T(8,128)(2,1)} async-done(((bf16[128,1024]{1,0:T(8,128)(2,1)}), bf16[512,1024]{1,0:T(8,128)(2,1)}) %all-gather.23.cloned.1.call-update) | async-done | bytes 1048592 | tf_op jit(solution)/shard_map/all_gather | solution.py:59
  197.4 9.7 reshape.425
  207.2 7.8 slice.186
  215.0 9.9 reshape.426
  238.3 26.0 %reduce-scatter.33.cloned.1.call-done = bf16[128,1024]{1,0:T(8,128)(2,1)} async-done(((bf16[512,1024]{1,0:T(8,128)(2,1)}), bf16[128,1024]{1,0:T(8,128)(2,1)}) %reduce-scatter.33.cloned.1.call-update) | async-done | bytes 262160 | tf_op jit(solution)/shard_map/reduce_scatter | solution.py:67
  267.3 8.9 all-gather.1
  278.0 13.3 %all-reduce.10 = (bf16[256]{0:T(256)(128)(2,1)S(1)}, bf16[256]{0:T(256)(128)(2,1)S(1)}) all-reduce(bf16[256]{0:T(256)(128)(2,1)S(1)} %dynamic-update-slice.4, bf16[256]{0:T(256)(128)(2,1)S(1)} %dynamic-update-slice.3), channel_id=1, replica_groups=mesh['dp'=8,'mp'=4] {'dp'}, use_global_device_ids=true, to_apply=%add.6 | all-reduce | flops 512 | bytes 2048
  292.6 11.1 all_gather.93
  306.2 12.1 all-gather.27.cloned.1.call-done
  322.9 13.1 %all-reduce.9 = (f32[256]{0:T(256)S(1)}, f32[256]{0:T(256)S(1)}) all-reduce(f32[256]{0:T(256)S(1)} %get-tuple-element.42, f32[256]{0:T(256)S(1)} %get-tuple-element.41), channel_id=1, replica_groups=mesh['dp'=8,'mp'=4] {'dp'}, use_global_device_ids=true, to_apply=%region_11.12 | all-reduce | flops 512 | bytes 4096 | tf_op jit(solution)/shard_map/psum | solution.py:281
  339.5 24.8 %reduce-scatter.35.cloned.1.call-done = bf16[128,1024]{1,0:T(8,128)(2,1)} async-done(((bf16[512,1024]{1,0:T(8,128)(2,1)}), bf16[128,1024]{1,0:T(8,128)(2,1)}) %reduce-scatter.35.cloned.1.call-update) | async-done | bytes 262160 | tf_op jit(solution)/shard_map/reduce_scatter | solution.py:67
  367.3 25.2 %all-gather.33.cloned.1.call-done = bf16[1024,1024]{1,0:T(8,128)(2,1)} async-done(((bf16[128,1024]{1,0:T(8,128)(2,1)}), bf16[1024,1024]{1,0:T(8,128)(2,1)}) %all-gather.33.cloned.1.call-update) | async-done | bytes 2097168 | tf_op jit(solution)/shard_map/all_gather | solution.py:90
  392.5 30.0 %all-gather.31.cloned.1.call-done = bf16[512,1024]{1,0:T(8,128)(2,1)} async-done(((bf16[128,1024]{1,0:T(8,128)(2,1)}), bf16[512,1024]{1,0:T(8,128)(2,1)}) %all-gather.31.cloned.1.call-update) | async-done | bytes 1048592 | tf_op jit(solution)/shard_map/all_gather | solution.py:59
  422.5 4.5 fusion.77
  427.1 24.9 %all-gather.35.cloned.1.call-done = bf16[1024,1024]{1,0:T(8,128)(2,1)} async-done(((bf16[1024,128]{1,0:T(8,128)(2,1)}), bf16[1024,1024]{1,0:T(8,128)(2,1)}) %all-gather.35.cloned.1.call-update) | async-done | bytes 2097168 | tf_op jit(solution)/shard_map/all_gather | solution.py:91
  451.9 4.6 convolution_convert_fusion.8
  456.6 27.4 %reduce-scatter.37.cloned.1.call-done = bf16[128,1024]{1,0:T(8,128)(2,1)} async-done(((bf16[512,1024]{1,0:T(8,128)(2,1)}), bf16[128,1024]{1,0:T(8,128)(2,1)}) %reduce-scatter.37.cloned.1.call-update) | async-done | bytes 262160 | tf_op jit(solution)/shard_map/reduce_scatter | solution.py:67
  489.2 26.6 %all-gather.37.cloned.1.call-done = bf16[512,1024]{1,0:T(8,128)(2,1)} async-done(((bf16[128,1024]{1,0:T(8,128)(2,1)}), bf16[512,1024]{1,0:T(8,128)(2,1)}) %all-gather.37.cloned.1.call-update) | async-done | bytes 1048592 | tf_op jit(solution)/shard_map/all_gather | solution.py:73
  523.5 26.7 %reduce-scatter.39.cloned.1.call-done = bf16[128,1024]{1,0:T(8,128)(2,1)} async-done(((bf16[512,1024]{1,0:T(8,128)(2,1)}), bf16[128,1024]{1,0:T(8,128)(2,1)}) %reduce-scatter.39.cloned.1.call-update) | async-done | bytes 262160 | tf_op jit(solution)/shard_map/reduce_scatter | solution.py:77
  555.0 26.6 %all-gather.39.cloned.1.call-done = bf16[512,1024]{1,0:T(8,128)(2,1)} async-done(((bf16[128,1024]{1,0:T(8,128)(2,1)}), bf16[512,1024]{1,0:T(8,128)(2,1)}) %all-gather.39.cloned.1.call-update) | async-done | bytes 1048592 | tf_op jit(solution)/shard_map/all_gather | solution.py:73
  584.5 13.1 %all-reduce.8 = (f32[256]{0:T(256)S(1)}, f32[256]{0:T(256)S(1)}) all-reduce(f32[256]{0:T(256)S(1)} %get-tuple-element.46, f32[256]{0:T(256)S(1)} %get-tuple-element.45), channel_id=1, replica_groups=mesh['dp'=8,'mp'=4] {'dp'}, use_global_device_ids=true, to_apply=%region_29.30 | all-reduce | flops 512 | bytes 4096 | tf_op jit(solution)/shard_map/psum | solution.py:305
  602.5 25.5 %reduce-scatter.41.cloned.1.call-done = bf16[128,1024]{1,0:T(8,128)(2,1)} async-done(((bf16[512,1024]{1,0:T(8,128)(2,1)}), bf16[128,1024]{1,0:T(8,128)(2,1)}) %reduce-scatter.41.cloned.1.call-update) | async-done | bytes 262160 | tf_op jit(solution)/shard_map/reduce_scatter | solution.py:77
  632.7 26.6 %all-gather.41.cloned.1.call-done = bf16[512,1024]{1,0:T(8,128)(2,1)} async-done(((bf16[128,1024]{1,0:T(8,128)(2,1)}), bf16[512,1024]{1,0:T(8,128)(2,1)}) %all-gather.41.cloned.1.call-update) | async-done | bytes 1048592 | tf_op jit(solution)/shard_map/all_gather | solution.py:73
  671.6 5.1 reshape.468
  687.1 5.1 reshape.431
  697.9 26.4 %reduce-scatter.43.cloned.1.call-done = bf16[128,1024]{1,0:T(8,128)(2,1)} async-done(((bf16[512,1024]{1,0:T(8,128)(2,1)}), bf16[128,1024]{1,0:T(8,128)(2,1)}) %reduce-scatter.43.cloned.1.call-update) | async-done | bytes 262160 | tf_op jit(solution)/shard_map/reduce_scatter | solution.py:77
  729.3 4.5 convolution_convert_fusion
  765.9 4.5 multiply_convert_fusion
  784.3 15.3 %reduce-scatter.65.cloned.1.call-done = bf16[128,1024]{1,0:T(8,128)(2,1)} async-done(((bf16[1024,1024]{1,0:T(8,128)(2,1)}), bf16[128,1024]{1,0:T(8,128)(2,1)}) %reduce-scatter.65.cloned.1.call-update) | async-done | bytes 262160
  801.6 42.5 %reduce-scatter.53.cloned.1.call-done = bf16[128,1024]{1,0:T(8,128)(2,1)} async-done(((bf16[1024,1024]{1,0:T(8,128)(2,1)}), bf16[128,1024]{1,0:T(8,128)(2,1)}) %reduce-scatter.53.cloned.1.call-update) | async-done | bytes 262160 | tf_op jit(solution)/shard_map/reduce_scatter | solution.py:83
  847.0 34.0 %reduce-scatter.61.cloned.1.call-done = bf16[32,5]{1,0:T(8,128)(2,1)} async-done(((bf16[256,5]{1,0:T(8,128)(2,1)}), bf16[32,5]{1,0:T(8,128)(2,1)}) %reduce-scatter.61.cloned.1.call-update) | async-done | bytes 336
  882.4 58.5 %all-reduce.13.cloned.1.call-done = bf16[1024,2,256]{2,1,0:T(2,128)(2,1)} async-done(((bf16[1024,2,256]{2,1,0:T(2,128)(2,1)}), bf16[1024,2,256]{2,1,0:T(2,128)(2,1)}) %all-reduce.13.cloned.1.call-update) | async-done | bytes 1048592
  942.7 34.6 %reduce-scatter.63.cloned.1.call-done = bf16[128,256]{1,0:T(8,128)(2,1)} async-done(((bf16[1024,256]{1,0:T(8,128)(2,1)}), bf16[128,256]{1,0:T(8,128)(2,1)}) %reduce-scatter.63.cloned.1.call-update) | async-done | bytes 65552
  978.9 35.4 %reduce-scatter.57.cloned.1.call-done = bf16[32,2]{1,0:T(8,128)(2,1)} async-done(((bf16[256,2]{1,0:T(8,128)(2,1)}), bf16[32,2]{1,0:T(8,128)(2,1)}) %reduce-scatter.57.cloned.1.call-update) | async-done | bytes 144
  1015.6 36.5 %reduce-scatter.59.cloned.1.call-done = bf16[128,256]{1,0:T(8,128)(2,1)} async-done(((bf16[1024,256]{1,0:T(8,128)(2,1)}), bf16[128,256]{1,0:T(8,128)(2,1)}) %reduce-scatter.59.cloned.1.call-update) | async-done | bytes 65552
  1053.7 36.2 %reduce-scatter.51.cloned.1.call-done = bf16[128,256]{1,0:T(8,128)(2,1)} async-done(((bf16[1024,256]{1,0:T(8,128)(2,1)}), bf16[128,256]{1,0:T(8,128)(2,1)}) %reduce-scatter.51.cloned.1.call-update) | async-done | bytes 65552 | tf_op jit(solution)/shard_map/reduce_scatter | solution.py:83
  1091.4 40.0 %reduce-scatter.49.cloned.1.call-done = bf16[128,3,256]{2,0,1:T(8,128)(2,1)} async-done(((bf16[1024,3,256]{2,0,1:T(8,128)(2,1)}), bf16[128,3,256]{2,0,1:T(8,128)(2,1)}) %reduce-scatter.49.cloned.1.call-update) | async-done | bytes 196624 | tf_op jit(solution)/shard_map/reduce_scatter | solution.py:83
  1133.1 27.9 %reduce-scatter.45.cloned.1.call-done = bf16[128,1024]{1,0:T(8,128)(2,1)} async-done(((bf16[512,1024]{1,0:T(8,128)(2,1)}), bf16[128,1024]{1,0:T(8,128)(2,1)}) %reduce-scatter.45.cloned.1.call-update) | async-done | bytes 262160 | tf_op jit(solution)/shard_map/reduce_scatter | solution.py:77
  1163.6 39.4 %psum.39 = f32[5,1024]{1,0:T(8,128)} all-reduce(f32[5,1024]{1,0:T(8,128)S(1)} %stack.53), channel_id=1, replica_groups=mesh['dp'=8,'mp'=4] {'dp','mp'}, use_global_device_ids=true, to_apply=%region_45.46 | all-reduce | flops 5120 | bytes 40960 | tf_op jit(solution)/shard_map/psum | solution.py:442
  1206.9 41.6 %reduce-scatter.47.cloned.1.call-done = bf16[128,1024]{1,0:T(8,128)(2,1)} async-done(((bf16[1024,1024]{1,0:T(8,128)(2,1)}), bf16[128,1024]{1,0:T(8,128)(2,1)}) %reduce-scatter.47.cloned.1.call-update) | async-done | bytes 262160 | tf_op jit(solution)/shard_map/reduce_scatter | solution.py:83
  (353 shorter events, 198.2 us)
Async XLA Ops:
  7.2 36.0 %all-gather.17.cloned.1.call-start = ((), (), s32[]{:S(2)}) async-start(), calls=%async_computation.18 | async-start | bytes 1310720 | tf_op jit(solution)/shard_map/all_gather | solution.py:59
  12.4 59.9 %all-gather.19.cloned.1.call-start = ((), (), s32[]{:S(2)}) async-start(), calls=%async_computation.19 | async-start | bytes 2359296 | tf_op jit(solution)/shard_map/all_gather | solution.py:90
  13.1 89.2 %all-gather.21.cloned.1.call-start = ((), (), s32[]{:S(2)}) async-start(), calls=%async_computation.20 | async-start | bytes 2359296 | tf_op jit(solution)/shard_map/all_gather | solution.py:91
  13.8 119.8 %reduce-scatter.31.cloned.1.call-start = ((), (), s32[]{:S(2)}) async-start(), calls=%async_computation.21 | async-start | bytes 1310720 | tf_op jit(solution)/shard_map/reduce_scatter | solution.py:67
  75.5 30.7 %copy-start.56 = (f32[512,1024]{1,0:T(8,128)}, f32[512,1024]{1,0:T(8,128)S(1)}, u32[]{:S(2)}) copy-start(f32[512,1024]{1,0:T(8,128)S(1)} %fusion.73) | copy-start | bytes 6291460
  75.5 30.8 %copy-start.38 = (bf16[128,3,256]{2,0,1:T(8,128)(2,1)S(1)}, bf16[128,3,256]{2,0,1:T(8,128)(2,1)}, u32[]{:S(2)}) copy-start(bf16[128,3,256]{2,0,1:T(8,128)(2,1)} %param.25) | copy-start | bytes 589828
  75.5 31.6 %copy-start.44 = (bf16[2,32]{1,0:T(2,128)(2,1)S(1)}, bf16[2,32]{1,0:T(2,128)(2,1)}, u32[]{:S(2)}) copy-start(bf16[2,32]{1,0:T(2,128)(2,1)} %param.27) | copy-start | bytes 388
  75.5 58.1 %copy-start = (bf16[1,128,1024]{2,1,0:T(8,128)(2,1)S(1)}, bf16[1,128,1024]{2,1,0:T(8,128)(2,1)}, u32[]{:S(2)}) copy-start(bf16[1,128,1024]{2,1,0:T(8,128)(2,1)} %param.19) | copy-start | bytes 786436
  106.2 70.2 %all-gather.25.cloned.1.call-start = ((), (), s32[]{:S(2)}) async-start(), calls=%async_computation.23 | async-start | bytes 1769472 | tf_op jit(solution)/shard_map/all_gather | solution.py:97
  107.1 83.9 %all-gather.23.cloned.1.call-start = ((), (), s32[]{:S(2)}) async-start(), calls=%async_computation.22 | async-start | bytes 1310720 | tf_op jit(solution)/shard_map/all_gather | solution.py:59
  137.7 126.6 %reduce-scatter.33.cloned.1.call-start = ((), (), s32[]{:S(2)}) async-start(), calls=%async_computation.24 | async-start | bytes 1310720 | tf_op jit(solution)/shard_map/reduce_scatter | solution.py:67
  232.3 432.5 %copy-start.3 = (f32[2,512,512]{1,2,0:T(8,128)}, f32[2,512,512]{1,2,0:T(8,128)S(1)}, u32[]{:S(2)}) copy-start(f32[2,512,512]{1,2,0:T(8,128)S(1)} %get-tuple-element.101) | copy-start | bytes 6291460
  235.9 29.5 %copy-start.24 = (bf16[2,128,512]{2,1,0:T(8,128)(2,1)}, bf16[2,128,512]{2,1,0:T(8,128)(2,1)S(1)}, u32[]{:S(2)}) copy-start(bf16[2,128,512]{2,1,0:T(8,128)(2,1)S(1)} %convolution_convert_fusion.21) | copy-start | bytes 786436
  237.4 29.8 %copy-start.42 = (bf16[5,32]{1,0:T(8,128)(2,1)S(1)}, bf16[5,32]{1,0:T(8,128)(2,1)}, u32[]{:S(2)}) copy-start(bf16[5,32]{1,0:T(8,128)(2,1)} %param.30) | copy-start | bytes 964
  237.4 38.8 %copy-start.43 = (u32[32]{0:T(128)S(1)}, u32[32]{0:T(128)}, u32[]{:S(2)}) copy-start(u32[32]{0:T(128)} %constant.110) | copy-start | bytes 388
  237.4 40.0 %copy-start.53 = (bf16[32]{0:T(256)(128)(2,1)S(1)}, bf16[32]{0:T(256)(128)(2,1)}, u32[]{:S(2)}) copy-start(bf16[32]{0:T(256)(128)(2,1)} %param.32) | copy-start | bytes 196
  237.4 40.3 %copy-start.54 = (bf16[32]{0:T(256)(128)(2,1)S(1)}, bf16[32]{0:T(256)(128)(2,1)}, u32[]{:S(2)}) copy-start(bf16[32]{0:T(256)(128)(2,1)} %param.31) | copy-start | bytes 196
  237.4 55.1 %copy-start.41 = (bf16[256,128]{1,0:T(8,128)(2,1)S(1)}, bf16[256,128]{1,0:T(8,128)(2,1)}, u32[]{:S(2)}) copy-start(bf16[256,128]{1,0:T(8,128)(2,1)} %param.33) | copy-start | bytes 196612
  237.5 66.2 %all-gather.29.cloned.1.call-start = ((), (), s32[]{:S(2)}) async-start(), calls=%async_computation.26 | async-start | bytes 1179648 | tf_op jit(solution)/shard_map/all_gather | solution.py:106
  238.2 80.1 %all-gather.27.cloned.1.call-start = ((), (), s32[]{:S(2)}) async-start(), calls=%async_computation.25 | async-start | bytes 1310720 | tf_op jit(solution)/shard_map/all_gather | solution.py:59
  266.6 97.8 %reduce-scatter.35.cloned.1.call-start = ((), (), s32[]{:S(2)}) async-start(), calls=%async_computation.27 | async-start | bytes 1310720 | tf_op jit(solution)/shard_map/reduce_scatter | solution.py:67
  338.8 53.8 %all-gather.33.cloned.1.call-start = ((), (), s32[]{:S(2)}) async-start(), calls=%async_computation.29 | async-start | bytes 2359296 | tf_op jit(solution)/shard_map/all_gather | solution.py:90
  339.5 83.0 %all-gather.31.cloned.1.call-start = ((), (), s32[]{:S(2)}) async-start(), calls=%async_computation.28 | async-start | bytes 1310720 | tf_op jit(solution)/shard_map/all_gather | solution.py:59
  366.5 85.4 %all-gather.35.cloned.1.call-start = ((), (), s32[]{:S(2)}) async-start(), calls=%async_computation.30 | async-start | bytes 2359296 | tf_op jit(solution)/shard_map/all_gather | solution.py:91
  367.3 116.7 %reduce-scatter.37.cloned.1.call-start = ((), (), s32[]{:S(2)}) async-start(), calls=%async_computation.31 | async-start | bytes 1310720 | tf_op jit(solution)/shard_map/reduce_scatter | solution.py:67
  456.5 59.3 %all-gather.37.cloned.1.call-start = ((), (), s32[]{:S(2)}) async-start(), calls=%async_computation.32 | async-start | bytes 1310720 | tf_op jit(solution)/shard_map/all_gather | solution.py:73
  489.2 61.1 %reduce-scatter.39.cloned.1.call-start = ((), (), s32[]{:S(2)}) async-start(), calls=%async_computation.33 | async-start | bytes 1310720 | tf_op jit(solution)/shard_map/reduce_scatter | solution.py:77
  523.4 58.2 %all-gather.39.cloned.1.call-start = ((), (), s32[]{:S(2)}) async-start(), calls=%async_computation.34 | async-start | bytes 1310720 | tf_op jit(solution)/shard_map/all_gather | solution.py:73
  555.0 42.7 %copy-start.10 = (f32[512,256]{1,0:T(8,128)S(1)}, f32[512,256]{1,0:T(8,128)}, u32[]{:S(2)}) copy-start(f32[512,256]{1,0:T(8,128)} %copy-done.9) | copy-start | bytes 1572868
  555.0 73.1 %reduce-scatter.41.cloned.1.call-start = ((), (), s32[]{:S(2)}) async-start(), calls=%async_computation.35 | async-start | bytes 1310720 | tf_op jit(solution)/shard_map/reduce_scatter | solution.py:77
  602.5 56.8 %all-gather.41.cloned.1.call-start = ((), (), s32[]{:S(2)}) async-start(), calls=%async_computation.36 | async-start | bytes 1310720 | tf_op jit(solution)/shard_map/all_gather | solution.py:73
  630.5 34.3 %copy-start.7 = (f32[128,1024]{1,0:T(8,128)}, f32[128,1024]{1,0:T(8,128)S(1)}, u32[]{:S(2)}) copy-start(f32[128,1024]{1,0:T(8,128)S(1)} %get-tuple-element.57) | copy-start | bytes 1572868
  632.6 91.7 %reduce-scatter.43.cloned.1.call-start = ((), (), s32[]{:S(2)}) async-start(), calls=%async_computation.37 | async-start | bytes 1310720 | tf_op jit(solution)/shard_map/reduce_scatter | solution.py:77
  697.4 29.4 %copy-start.8 = (f32[128,1024]{1,0:T(8,128)S(1)}, f32[128,1024]{1,0:T(8,128)}, u32[]{:S(2)}) copy-start(f32[128,1024]{1,0:T(8,128)} %copy-done.7) | copy-start | bytes 1572868
  697.5 68.4 %all-gather.43.cloned.1.call-start = ((), (), s32[]{:S(2)}) async-start(), calls=%async_computation.38 | async-start | bytes 1310720 | tf_op jit(solution)/shard_map/all_gather | solution.py:73
  729.2 70.4 %reduce-scatter.65.cloned.1.call-start = ((), (), s32[]{:S(2)}) async-start(), calls=%async_computation.49 | async-start | bytes 2359296
  737.8 106.3 %reduce-scatter.53.cloned.1.call-start = ((), (), s32[]{:S(2)}) async-start(), calls=%async_computation.43 | async-start | bytes 2359296 | tf_op jit(solution)/shard_map/reduce_scatter | solution.py:83
  742.8 138.3 %reduce-scatter.61.cloned.1.call-start = ((), (), s32[]{:S(2)}) async-start(), calls=%async_computation.47 | async-start | bytes 73728
  743.7 197.2 %all-reduce.13.cloned.1.call-start = ((), (), s32[]{:S(2)}) async-start(), calls=%async_computation.50 | async-start | bytes 2097152
  750.5 226.8 %reduce-scatter.63.cloned.1.call-start = ((), (), s32[]{:S(2)}) async-start(), calls=%async_computation.48 | async-start | bytes 589824
  755.3 259.0 %reduce-scatter.57.cloned.1.call-start = ((), (), s32[]{:S(2)}) async-start(), calls=%async_computation.45 | async-start | bytes 73728
  756.1 296.0 %reduce-scatter.59.cloned.1.call-start = ((), (), s32[]{:S(2)}) async-start(), calls=%async_computation.46 | async-start | bytes 589824
  758.9 331.0 %reduce-scatter.51.cloned.1.call-start = ((), (), s32[]{:S(2)}) async-start(), calls=%async_computation.42 | async-start | bytes 589824 | tf_op jit(solution)/shard_map/reduce_scatter | solution.py:83
  762.1 369.3 %reduce-scatter.49.cloned.1.call-start = ((), (), s32[]{:S(2)}) async-start(), calls=%async_computation.41 | async-start | bytes 1769472 | tf_op jit(solution)/shard_map/reduce_scatter | solution.py:83
  765.8 395.3 %reduce-scatter.45.cloned.1.call-start = ((), (), s32[]{:S(2)}) async-start(), calls=%async_computation.39 | async-start | bytes 1310720 | tf_op jit(solution)/shard_map/reduce_scatter | solution.py:77
  773.7 431.2 %reduce-scatter.55.cloned.1.call-start = ((), (), s32[]{:S(2)}) async-start(), calls=%async_computation.44 | async-start | bytes 2359296
  779.5 469.0 %reduce-scatter.47.cloned.1.call-start = ((), (), s32[]{:S(2)}) async-start(), calls=%async_computation.40 | async-start | bytes 2359296 | tf_op jit(solution)/shard_map/reduce_scatter | solution.py:83
  801.6 401.4 %copy-start.20 = (f32[128,1024]{1,0:T(8,128)S(1)}, f32[128,1024]{1,0:T(8,128)}, u32[]{:S(2)}) copy-start(f32[128,1024]{1,0:T(8,128)} %get-tuple-element.55) | copy-start | bytes 1572868
  (46 other events, 220.6 us)
Sparse Core Ops, SparseCore 0:
  12.5 30.6 all-gather.16
  45.1 27.1 all-gather.18
  74.2 28.0 all-gather.20
  106.3 27.2 reduce-scatter.30
  135.9 24.2 all-gather.24
  162.2 28.6 all-gather.22
  237.6 26.6 reduce-scatter.32
  266.2 21.9 all-gather.28
  290.3 27.9 all-gather.26
  338.9 25.3 reduce-scatter.34
  366.2 26.2 all-gather.32
  394.5 27.9 all-gather.30
  424.4 27.4 all-gather.34
  456.6 27.2 reduce-scatter.36
  489.3 26.4 all-gather.36
  523.6 26.6 reduce-scatter.38
  555.1 26.4 all-gather.38
  602.6 25.3 reduce-scatter.40
  632.8 26.4 all-gather.40
  697.6 26.6 reduce-scatter.42
  729.3 26.4 all-gather.42
  759.1 40.4 reduce-scatter.64
  802.9 41.1 reduce-scatter.52
  847.5 33.5 reduce-scatter.60
  884.2 56.6 all-reduce.12
  943.9 33.3 reduce-scatter.62
  980.7 33.5 reduce-scatter.56
  1017.9 34.1 reduce-scatter.58
  1055.8 34.1 reduce-scatter.50
  1093.1 38.3 reduce-scatter.48
  1133.7 27.3 reduce-scatter.44
  1164.4 40.0 reduce-scatter.54
  1207.6 40.9 reduce-scatter.46

commit v2 on v0

--- a/solution.py
+++ b/solution.py
@@ -1,8 +1,11 @@
+import functools
 import math
 
 import jax
 import jax.numpy as jnp
 from jax import lax
+from jax.experimental import pallas as pl
+from jax.experimental.pallas import tpu as pltpu
 from jax.sharding import PartitionSpec as P
 
 HEAD = 128
@@ -55,7 +58,448 @@
     return jnp.stack([jnp.sin(angles), jnp.cos(angles)], axis=-1).reshape(2 * seq_len, model_width)
 
 
+MESH = pl.DeviceIdType.MESH
+VMEM_LIMIT = 60 * 1024 * 1024
+
+
+def neighbour_barrier(axis):
+    me = lax.axis_index(axis)
+    size = lax.axis_size(axis)
+    barrier = pltpu.get_barrier_semaphore()
+
+    @pl.when(me > 0)
+    def _():
+        pl.semaphore_signal(barrier, inc=1, device_id={axis: me - 1}, device_id_type=MESH)
+
+    @pl.when(me < size - 1)
+    def _():
+        pl.semaphore_signal(barrier, inc=1, device_id={axis: me + 1}, device_id_type=MESH)
+
+    peers = jnp.minimum(me, 1) + jnp.minimum(size - 1 - me, 1)
+    pl.semaphore_wait(barrier, peers)
+
+
+def line_copy(src, dst, sems, index, axis, target):
+    return pltpu.make_async_remote_copy(
+        src_ref=src,
+        dst_ref=dst,
+        send_sem=sems.at[0, index],
+        recv_sem=sems.at[1, index],
+        device_id={axis: target},
+        device_id_type=MESH,
+    )
+
+
+def line_gather_kernel(axis, in_ref, out_ref, sems):
+    size = lax.axis_size(axis)
+    me = lax.axis_index(axis)
+    rows = in_ref.shape[0]
+    steps = size - 1
+    neighbour_barrier(axis)
+
+    def piece(index):
+        return out_ref.at[pl.ds(index * rows, rows)]
+
+    def leaving(way, step):
+        index = me - step if way == 0 else me + step
+        return line_copy(
+            in_ref if step == 0 else piece(index), piece(index), sems,
+            way * steps + step, axis, me + 1 if way == 0 else me - 1,
+        )
+
+    def arriving(way, step):
+        index = me - 1 - step if way == 0 else me + 1 + step
+        return line_copy(in_ref, piece(index), sems, way * steps + step, axis, me)
+
+    def go_right(step):
+        return jnp.logical_and(me - step >= 0, me + 1 < size)
+
+    def go_left(step):
+        return jnp.logical_and(me + step < size, me > 0)
+
+    for step in range(steps):
+        if step > 0:
+            @pl.when(me - step >= 0)
+            def _():
+                arriving(0, step - 1).wait_recv()
+
+        @pl.when(go_right(step))
+        def _():
+            leaving(0, step).start()
+
+        if step > 0:
+            @pl.when(me + step < size)
+            def _():
+                arriving(1, step - 1).wait_recv()
+
+        @pl.when(go_left(step))
+        def _():
+            leaving(1, step).start()
+
+        if step == 0:
+            out_ref[pl.ds(pl.multiple_of(me * rows, rows), rows), :] = in_ref[...]
+
+    @pl.when(me - steps >= 0)
+    def _():
+        arriving(0, steps - 1).wait_recv()
+
+    @pl.when(me + steps < size)
+    def _():
+        arriving(1, steps - 1).wait_recv()
+
+    for step in range(steps):
+        @pl.when(go_right(step))
+        def _():
+            leaving(0, step).wait_send()
+
+        @pl.when(go_left(step))
+        def _():
+            leaving(1, step).wait_send()
+
+
+def line_gather(values, axis, collective_id):
+    size = lax.axis_size(axis)
+    rows, width = values.shape
+    return pl.pallas_call(
+        functools.partial(line_gather_kernel, axis),
+        out_shape=jax.ShapeDtypeStruct((size * rows, width), values.dtype),
+        in_specs=[pl.BlockSpec(memory_space=pltpu.VMEM)],
+        out_specs=pl.BlockSpec(memory_space=pltpu.VMEM),
+        scratch_shapes=[pltpu.SemaphoreType.DMA((2, 2 * (size - 1)))],
+        compiler_params=pltpu.CompilerParams(
+            collective_id=collective_id, has_side_effects=True
+        ),
+        name="line_gather",
+    )(values)
+
+
+def line_scatter_kernel(axis, in_ref, out_ref, slots, staged, sems):
+    size = lax.axis_size(axis)
+    me = lax.axis_index(axis)
+    rows = out_ref.shape[0]
+    neighbour_barrier(axis)
+
+    def own(index):
+        return in_ref[index * rows : (index + 1) * rows, :].astype(jnp.float32)
+
+    def copy(way, owner, src):
+        return line_copy(
+            src, slots.at[way, owner], sems, way * size + owner, axis,
+            me + 1 if way == 0 else me - 1,
+        )
+
+    def hop(way, owner):
+        first = me == (0 if way == 0 else size - 1)
+        passes = me < owner if way == 0 else me > owner
+
+        @pl.when(jnp.logical_and(passes, first))
+        def _():
+            copy(way, owner, in_ref.at[owner * rows : (owner + 1) * rows]).start()
+
+        @pl.when(jnp.logical_and(passes, jnp.logical_not(first)))
+        def _():
+            copy(way, owner, staged.at[way, owner]).wait_recv()
+            staged[way, owner] = (own(owner) + slots[way, owner].astype(jnp.float32)).astype(
+                staged.dtype
+            )
+            copy(way, owner, staged.at[way, owner]).start()
+
+    def order(first_way):
+        for index in range(size - 1):
+            owners = (size - 1 - index, index)
+            hop(first_way, owners[first_way])
+            hop(1 - first_way, owners[1 - first_way])
+
+    @pl.when(me < size // 2)
+    def _():
+        order(0)
+
+    @pl.when(me >= size // 2)
+    def _():
+        order(1)
+
+    for owner in range(size):
+        @pl.when(me == owner)
+        def _():
+            total = own(owner)
+            if owner > 0:
+                copy(0, owner, staged.at[0, owner]).wait_recv()
+            if owner < size - 1:
+                copy(1, owner, staged.at[1, owner]).wait_recv()
+            if owner > 0:
+                total = total + slots[0, owner].astype(jnp.float32)
+            if owner < size - 1:
+                total = total + slots[1, owner].astype(jnp.float32)
+            out_ref[...] = total
+
+    for owner in range(size):
+        @pl.when(me < owner)
+        def _():
+            copy(0, owner, staged.at[0, owner]).wait_send()
+
+        @pl.when(me > owner)
+        def _():
+            copy(1, owner, staged.at[1, owner]).wait_send()
+
+
+def line_scatter(values, axis, collective_id):
+    size = lax.axis_size(axis)
+    rows, width = values.shape[0] // size, values.shape[1]
+    return pl.pallas_call(
+        functools.partial(line_scatter_kernel, axis),
+        out_shape=jax.ShapeDtypeStruct((rows, width), jnp.float32),
+        in_specs=[pl.BlockSpec(memory_space=pltpu.VMEM)],
+        out_specs=pl.BlockSpec(memory_space=pltpu.VMEM),
+        scratch_shapes=[
+            pltpu.VMEM((2, size, rows, width), values.dtype),
+            pltpu.VMEM((2, size, rows, width), values.dtype),
+            pltpu.SemaphoreType.DMA((2, 2 * size)),
+        ],
+        compiler_params=pltpu.CompilerParams(
+            collective_id=collective_id, has_side_effects=True
+        ),
+        name="line_scatter",
+    )(values)
+
+
+def bit_of(index, bit):
+    return lax.rem(lax.div(index, bit), 2)
+
+
+def partner(index, bit):
+    return index + bit - 2 * bit * bit_of(index, bit)
+
+
+def cube_bits(size, swap):
+    bits = []
+    bit = 2
+    while bit < size:
+        bits.append(bit)
+        bit *= 2
+    if swap:
+        bits.reverse()
+    return bits + [1]
+
+
+def cube_copy(src, dst, sems, index, axis, target):
+    return line_copy(src, dst, sems, index, axis, target)
+
+
+def cube_barrier(axis):
+    me = lax.axis_index(axis)
+    bits = cube_bits(lax.axis_size(axis), False)
+    barrier = pltpu.get_barrier_semaphore()
+    for bit in bits:
+        pl.semaphore_signal(
+            barrier, inc=1, device_id={axis: partner(me, bit)}, device_id_type=MESH
+        )
+    pl.semaphore_wait(barrier, len(bits))
+
+
+def block_at(ref, dim, index, width):
+    start = pl.multiple_of(index * width, width)
+    return ref.at[pl.ds(start, width)] if dim == 0 else ref.at[:, pl.ds(start, width)]
+
+
+def cube_gather_kernel(axis, dims, ways, *refs):
+    count = len(dims)
+    ins, outs, (sems,) = refs[:count], refs[count : 2 * count], refs[2 * count :]
+    size = lax.axis_size(axis)
+    me = lax.axis_index(axis)
+    stages = len(cube_bits(size, False))
+    cube_barrier(axis)
+    started = []
+    waiting = [None] * count
+    per = size - 1
+    for stage in range(stages):
+        for which in range(count):
+            width = ins[which].shape[dims[which]]
+            bits = cube_bits(size, ways[which])
+            if stage == 0:
+                block_at(outs[which], dims[which], me, width)[...] = ins[which][...]
+            else:
+                for copy in waiting[which]:
+                    copy.wait_recv()
+            held = [me]
+            for bit in bits[:stage]:
+                held = held + [partner(index, bit) for index in held]
+            target = partner(me, bits[stage])
+            new = []
+            for number, index in enumerate(held):
+                place = block_at(outs[which], dims[which], index, width)
+                src = ins[which] if stage == 0 else place
+                copy = cube_copy(
+                    src, place, sems, which * per + 2**stage - 1 + number, axis, target
+                )
+                copy.start()
+                new.append(copy)
+            waiting[which] = new
+            started.extend(new)
+    for which in range(count):
+        for copy in waiting[which]:
+            copy.wait_recv()
+    for copy in started:
+        copy.wait_send()
+
+
+def cube_gather(arrays, dims, ways, axis, collective_id):
+    size = lax.axis_size(axis)
+    count = len(arrays)
+    shapes = []
+    for array, dim in zip(arrays, dims):
+        shape = list(array.shape)
+        shape[dim] *= size
+        shapes.append(jax.ShapeDtypeStruct(tuple(shape), array.dtype))
+    return pl.pallas_call(
+        functools.partial(cube_gather_kernel, axis, dims, ways),
+        out_shape=shapes,
+        in_specs=[pl.BlockSpec(memory_space=pltpu.VMEM)] * count,
+        out_specs=[pl.BlockSpec(memory_space=pltpu.VMEM)] * count,
+        scratch_shapes=[pltpu.SemaphoreType.DMA((2, count * (size - 1)))],
+        compiler_params=pltpu.CompilerParams(
+            collective_id=collective_id, has_side_effects=True, vmem_limit_bytes=VMEM_LIMIT
+        ),
+        name="cube_gather",
+    )(*arrays)
+
+
+def cube_scatter_kernel(axis, dims, ways, *refs):
+    count = len(dims)
+    ins, outs = refs[:count], refs[count : 2 * count]
+    slots, sems = refs[2 * count : 3 * count], refs[3 * count]
+    size = lax.axis_size(axis)
+    me = lax.axis_index(axis)
+    stages = len(cube_bits(size, False))
+    per = size - 1
+    cube_barrier(axis)
+    started = []
+
+    def slot(which, stage, number):
+        return slots[which].at[size - size // 2**stage + number]
+
+    def sets(which, stage):
+        bits = cube_bits(size, ways[which])[::-1]
+        held = [me]
+        for bit in bits[stage + 1 :]:
+            held = held + [partner(index, bit) for index in held]
+        return bits[stage], held
+
+    def send(which, stage):
+        width = outs[which].shape[dims[which]]
+        bit, held = sets(which, stage)
+        target = partner(me, bit)
+        for number, index in enumerate(held):
+            if stage == 0:
+                src = block_at(ins[which], dims[which], partner(index, bit), width)
+            else:
+                src = slot(which, stage - 1, 2 * number + 1)
+            copy = cube_copy(
+                src, slot(which, stage, number), sems,
+                which * per + size - size // 2**stage + number, axis, target,
+            )
+            copy.start()
+            started.append((which, stage, copy))
+
+    def receive(which, stage):
+        width = outs[which].shape[dims[which]]
+        bit, held = sets(which, stage)
+        for copy in [c for w, s, c in started if (w, s) == (which, stage)]:
+            copy.wait_recv()
+        for number, index in enumerate(held):
+            got = slot(which, stage, number)[...].astype(jnp.float32)
+            if stage == 0:
+                mine = block_at(ins[which], dims[which], index, width)[...]
+            else:
+                mine = slot(which, stage - 1, 2 * number)[...]
+            total = got + mine.astype(jnp.float32)
+            if stage == stages - 1:
+                outs[which][...] = total
+            else:
+                slot(which, stage, number)[...] = total.astype(slots[which].dtype)
+
+    for stage in range(stages):
+        for which in range(count):
+            if stage > 0:
+                receive(which, stage - 1)
+            send(which, stage)
+    for which in range(count):
+        receive(which, stages - 1)
+    for which, stage, copy in started:
+        copy.wait_send()
+
+
+def cube_scatter(arrays, dims, ways, axis, collective_id):
+    size = lax.axis_size(axis)
+    count = len(arrays)
+    shapes, slots = [], []
+    for array, dim in zip(arrays, dims):
+        shape = list(array.shape)
+        shape[dim] //= size
+        shapes.append(jax.ShapeDtypeStruct(tuple(shape), jnp.float32))
+        slots.append(pltpu.VMEM((size - 1, *shape), array.dtype))
+    return pl.pallas_call(
+        functools.partial(cube_scatter_kernel, axis, dims, ways),
+        out_shape=shapes,
+        in_specs=[pl.BlockSpec(memory_space=pltpu.VMEM)] * count,
+        out_specs=[pl.BlockSpec(memory_space=pltpu.VMEM)] * count,
+        scratch_shapes=slots + [pltpu.SemaphoreType.DMA((2, count * (size - 1)))],
+        compiler_params=pltpu.CompilerParams(
+            collective_id=collective_id, has_side_effects=True, vmem_limit_bytes=VMEM_LIMIT
+        ),
+        name="cube_scatter",
+    )(*arrays)
+
+
+def all_total_kernel(axis, in_ref, out_ref, slots, sems):
+    size = lax.axis_size(axis)
+    me = lax.axis_index(axis)
+    barrier = pltpu.get_barrier_semaphore()
+    targets = [lax.rem(me + step, size) for step in range(1, size)]
+    for target in targets:
+        pl.semaphore_signal(barrier, inc=1, device_id={axis: target}, device_id_type=MESH)
+    pl.semaphore_wait(barrier, size - 1)
+    copies = []
+    for number, target in enumerate(targets):
+        copy = line_copy(in_ref, slots.at[me], sems, number, axis, target)
+        copy.start()
+        copies.append(copy)
+    slots[me] = in_ref[...]
+    for copy in copies:
+        copy.wait_recv()
+    total = slots[0]
+    for source in range(1, size):
+        total = total + slots[source]
+    out_ref[...] = total
+    for copy in copies:
+        copy.wait_send()
+
+
+def all_total(values, axis, collective_id):
+    size = lax.axis_size(axis)
+    return pl.pallas_call(
+        functools.partial(all_total_kernel, axis),
+        out_shape=jax.ShapeDtypeStruct(values.shape, values.dtype),
+        in_specs=[pl.BlockSpec(memory_space=pltpu.VMEM)],
+        out_specs=pl.BlockSpec(memory_space=pltpu.VMEM),
+        scratch_shapes=[
+            pltpu.VMEM((size, *values.shape), values.dtype),
+            pltpu.SemaphoreType.DMA((2, size - 1)),
+        ],
+        compiler_params=pltpu.CompilerParams(
+            collective_id=collective_id, has_side_effects=True
+        ),
+        name="all_total",
+    )(values)
+
+
+def direct(block):
+    size = lax.axis_size("dp")
+    return size & (size - 1) == 0 and block % 128 == 0
+
+
 def spread_rows(normed):
+    if direct(normed.shape[1] // lax.axis_size("dp")):
+        return line_gather(normed, "mp", 0)
     return lax.all_gather(normed, "mp", axis=0, tiled=True)
 
 
@@ -64,45 +508,62 @@
 
 
 def branch_total(partial_value):
-    return lax.psum_scatter(
-        partial_value.astype(jnp.bfloat16), "mp", scatter_dimension=0, tiled=True
-    ).astype(jnp.float32)
+    partial_value = partial_value.astype(jnp.bfloat16)
+    if direct(partial_value.shape[1] // lax.axis_size("dp")):
+        return line_scatter(partial_value, "mp", 1)
+    return lax.psum_scatter(partial_value, "mp", scatter_dimension=0, tiled=True).astype(
+        jnp.float32
+    )
 
 
 def spread_grads(upstream):
-    return lax.all_gather(upstream, "mp", axis=0, tiled=True)
+    return spread_rows(upstream)
 
 
 def input_total(partial_value):
-    return lax.psum_scatter(
-        partial_value.astype(jnp.bfloat16), "mp", scatter_dimension=0, tiled=True
-    ).astype(jnp.float32)
-
-
-def ffn_fetch(w_up, w_down):
+    return branch_total(partial_value)
+
+
+def dp_total(values):
+    if direct(128):
+        return all_total(values, "dp", 2)
+    return lax.psum(values, "dp")
+
+
+def fetch_now(arrays, dims, small):
+    if direct(arrays[0].shape[dims[0]]):
+        lanes = small.shape[1]
+        packed = jnp.pad(small, ((0, 16 - small.shape[0]), (0, 128 - lanes)))
+        *whole, rows = cube_gather(
+            [*arrays, packed], (*dims, 0), [index % 2 == 1 for index in range(len(dims) + 1)],
+            "dp", 3,
+        )
+        size = lax.axis_size("dp")
+        rows = rows.reshape(size, 16, 128)[:, : small.shape[0], :lanes]
+        return whole, rows.transpose(1, 0, 2).reshape(small.shape[0], size * lanes)
     return (
-        lax.all_gather(w_up, "dp", axis=0, tiled=True),
-        lax.all_gather(w_down, "dp", axis=1, tiled=True),
-    )
-
-
-def attn_fetch(w_in, w_pos, bias_pair, w_out):
-    return (
-        lax.all_gather(w_in, "dp", axis=0, tiled=True),
-        lax.all_gather(w_pos, "dp", axis=0, tiled=True),
-        lax.all_gather(bias_pair, "dp", axis=1, tiled=True),
-        lax.all_gather(w_out, "dp", axis=1, tiled=True),
-    )
-
-
-def conv_fetch(w_in, kernel, bn_gain, bn_bias, w_out):
-    return (
-        lax.all_gather(w_in, "dp", axis=0, tiled=True),
-        lax.all_gather(kernel, "dp", axis=1, tiled=True),
-        lax.all_gather(bn_gain, "dp", axis=0, tiled=True),
-        lax.all_gather(bn_bias, "dp", axis=0, tiled=True),
-        lax.all_gather(w_out, "dp", axis=1, tiled=True),
-    )
+        [lax.all_gather(array, "dp", axis=dim, tiled=True) for array, dim in zip(arrays, dims)],
+        lax.all_gather(small, "dp", axis=1, tiled=True),
+    )
+
+
+def grad_totals(grads, dims, ways, small, gains):
+    dp_size = lax.axis_size("dp")
+    piece_len = small.shape[1] // dp_size
+    grads = [grad.astype(jnp.bfloat16) for grad in grads]
+    if direct(grads[0].shape[dims[0]] // dp_size):
+        totals = cube_scatter(grads, dims, ways, "dp", 4)
+        small = all_total(small, "dp", 5)
+        gains = all_total(all_total(gains, "dp", 6), "mp", 7)
+    else:
+        totals = [
+            lax.psum_scatter(grad, "dp", scatter_dimension=dim, tiled=True).astype(jnp.float32)
+            for grad, dim in zip(grads, dims)
+        ]
+        small = lax.psum(small, "dp")
+        gains = lax.psum(gains, ("dp", "mp"))
+    start = lax.axis_index("dp") * piece_len
+    return totals, lax.dynamic_slice_in_dim(small, start, piece_len, axis=1), gains
 
 
 def ffn_forward(whole, weights):
@@ -272,7 +733,7 @@
 def batch_stats(conved, mask_col, frame_count):
     local_sum = jnp.sum(conved * mask_col, axis=0)
     local_squares = jnp.sum(conved * conved * mask_col, axis=0)
-    total_sum, total_squares = lax.psum((local_sum, local_squares), "dp")
+    total_sum, total_squares = dp_total(jnp.stack([local_sum, local_squares]))
     average = total_sum / frame_count
     variance = total_squares / frame_count - average * average
     return (average, lax.rsqrt(variance + batch_eps))
@@ -296,8 +757,8 @@
     grad_out = contract_rows(active, grad_whole)
     d_normed = contract_cols(grad_whole, w_out) * silu_slope(normed_b)
     centred = (conved - average) * inv_std
-    bias_total, gain_total = lax.psum(
-        (jnp.sum(d_normed, axis=0), jnp.sum(d_normed * centred, axis=0)), "dp"
+    bias_total, gain_total = dp_total(
+        jnp.stack([jnp.sum(d_normed, axis=0), jnp.sum(d_normed * centred, axis=0)])
     )
     d_conved = (
         bn_gain.astype(jnp.float32)
@@ -358,43 +819,59 @@
     mask_col = valid_keys.astype(jnp.float32)[:, None]
     frame_count = jnp.sum(lengths).astype(jnp.float32)
     layer_input = frames_in.reshape(local_rows, model_width).astype(jnp.float32)
-    ffn_first = ffn_fetch(ffn1_up, ffn1_down)
-    after_first = layer_input + 0.5 * branch_total(
-        ffn_forward(enter_block(layer_input, norm_gains[0]), ffn_first)
-    )
-    attn_held = attn_fetch(attn_in, pos_proj, pos_bias, attn_out)
+    (up_one, down_one, pos_whole, attn_out_whole, conv_out_whole), small = fetch_now(
+        [ffn1_up, ffn1_down, pos_proj, attn_out, conv_out],
+        (0, 1, 0, 1, 1),
+        jnp.concatenate([pos_bias, depthwise, bn_scale[None], bn_shift[None]], axis=0),
+    )
+    taps = depthwise.shape[0]
+    ffn_first = (up_one, down_one)
+    attn_held = (
+        lax.all_gather(attn_in, "dp", axis=0, tiled=True),
+        pos_whole,
+        small[:2],
+        attn_out_whole,
+    )
+    conv_held = (
+        lax.all_gather(conv_in, "dp", axis=0, tiled=True),
+        small[2 : 2 + taps],
+        small[2 + taps],
+        small[3 + taps],
+        conv_out_whole,
+    )
+    ffn_second = (
+        lax.all_gather(ffn2_up, "dp", axis=0, tiled=True),
+        lax.all_gather(ffn2_down, "dp", axis=1, tiled=True),
+    )
+    whole_first = enter_block(layer_input, norm_gains[0])
+    after_first = layer_input + 0.5 * branch_total(ffn_forward(whole_first, ffn_first))
+    whole_attn = enter_block(after_first, norm_gains[1])
     after_attn = after_first + branch_total(
-        attention_forward(
-            enter_block(after_first, norm_gains[1]), attn_held, valid_keys, block_rows
-        )
-    )
-    conv_held = conv_fetch(conv_in, depthwise, bn_scale, bn_shift, conv_out)
+        attention_forward(whole_attn, attn_held, valid_keys, block_rows)
+    )
+    whole_conv = enter_block(after_attn, norm_gains[2])
     gate_value, logistic, padded, conved = conv_front(
-        enter_block(after_attn, norm_gains[2]), conv_held[0], conv_held[1], mask_col
+        whole_conv, conv_held[0], conv_held[1], mask_col
     )
     stats = batch_stats(conved, mask_col, frame_count)
     normed_b, active = conv_tail(conved, stats, conv_held[2], conv_held[3])
     after_conv = after_attn + branch_total(matmul(active, conv_held[4]))
-    ffn_second = ffn_fetch(ffn2_up, ffn2_down)
-    after_second = after_conv + 0.5 * branch_total(
-        ffn_forward(enter_block(after_conv, norm_gains[3]), ffn_second)
-    )
+    whole_second = enter_block(after_conv, norm_gains[3])
+    after_second = after_conv + 0.5 * branch_total(ffn_forward(whole_second, ffn_second))
     block_out = layer_norm(after_second, norm_gains[4]).astype(jnp.bfloat16)
     d_second, gain_five = norm_back(
         after_second, norm_gains[4], out_grad.reshape(local_rows, model_width).astype(jnp.float32)
     )
-    ffn_back_two = ffn_fetch(ffn2_up, ffn2_down)
     d_normed, grad_up_two, grad_down_two = ffn_backward(
-        enter_block(after_conv, norm_gains[3]),
-        ffn_back_two,
+        whole_second,
+        ffn_second,
         spread_grads((0.5 * d_second).astype(jnp.bfloat16)),
     )
     d_branch, gain_four = norm_back(after_conv, norm_gains[3], input_total(d_normed))
     d_conv = d_second + d_branch
-    conv_back_held = conv_fetch(conv_in, depthwise, bn_scale, bn_shift, conv_out)
     d_normed, grad_conv_in, grad_kernel, grad_conv_out, gain_total, bias_total = conv_backward(
-        enter_block(after_attn, norm_gains[2]),
-        conv_back_held,
+        whole_conv,
+        conv_held,
         mask_col,
         stats,
         frame_count,
@@ -402,39 +879,52 @@
     )
     d_branch, gain_three = norm_back(after_attn, norm_gains[2], input_total(d_normed))
     d_attn = d_conv + d_branch
-    attn_back_held = attn_fetch(attn_in, pos_proj, pos_bias, attn_out)
     d_normed, grad_attn_in, grad_pos, grad_bias, grad_attn_out = attention_backward(
-        enter_block(after_first, norm_gains[1]),
-        attn_back_held,
+        whole_attn,
+        attn_held,
         valid_keys,
         block_rows,
         spread_grads(d_attn.astype(jnp.bfloat16)),
     )
     d_branch, gain_two = norm_back(after_first, norm_gains[1], input_total(d_normed))
     d_first = d_attn + d_branch
-    ffn_back_one = ffn_fetch(ffn1_up, ffn1_down)
     d_normed, grad_up_one, grad_down_one = ffn_backward(
-        enter_block(layer_input, norm_gains[0]),
-        ffn_back_one,
+        whole_first,
+        ffn_first,
         spread_grads((0.5 * d_first).astype(jnp.bfloat16)),
     )
     d_branch, gain_one = norm_back(layer_input, norm_gains[0], input_total(d_normed))
     in_grad = d_first + d_branch
+    totals, small_grads, gain_sum = grad_totals(
+        [
+            grad_up_two,
+            grad_down_two,
+            grad_conv_in.reshape(model_width, -1),
+            grad_conv_out,
+            grad_attn_in.reshape(model_width, -1),
+            grad_attn_out,
+            grad_pos,
+            grad_up_one,
+            grad_down_one,
+        ],
+        (0, 1, 0, 1, 0, 1, 0, 0, 1),
+        (False, True, True, True, False, True, False, False, True),
+        jnp.concatenate([grad_bias, grad_kernel], axis=0),
+        jnp.stack([gain_one, gain_two, gain_three, gain_four, gain_five]),
+    )
+    block = model_width // lax.axis_size("dp")
     summed = (
-        lax.psum_scatter(grad_up_one, "dp", scatter_dimension=0, tiled=True),
-        lax.psum_scatter(grad_down_one, "dp", scatter_dimension=1, tiled=True),
-        lax.psum_scatter(grad_attn_in, "dp", scatter_dimension=0, tiled=True),
-        lax.psum_scatter(grad_pos, "dp", scatter_dimension=0, tiled=True),
-        lax.psum_scatter(grad_bias, "dp", scatter_dimension=1, tiled=True),
-        lax.psum_scatter(grad_attn_out, "dp", scatter_dimension=1, tiled=True),
-        lax.psum_scatter(grad_conv_in, "dp", scatter_dimension=0, tiled=True),
-        lax.psum_scatter(grad_kernel, "dp", scatter_dimension=1, tiled=True),
-        lax.psum_scatter(grad_conv_out, "dp", scatter_dimension=1, tiled=True),
-        lax.psum_scatter(grad_up_two, "dp", scatter_dimension=0, tiled=True),
-        lax.psum_scatter(grad_down_two, "dp", scatter_dimension=1, tiled=True),
-    )
-    gain_sum = lax.psum(
-        jnp.stack([gain_one, gain_two, gain_three, gain_four, gain_five]), ("dp", "mp")
+        totals[7],
+        totals[8],
+        totals[4].reshape(block, 3, -1),
+        totals[6],
+        small_grads[:2],
+        totals[5],
+        totals[2].reshape(block, 2, -1),
+        small_grads[2:],
+        totals[3],
+        totals[0],
+        totals[1],
     )
     piece_len = bn_scale.shape[0]
     grad_scale = lax.dynamic_slice_in_dim(gain_total, dp_index * piece_len, piece_len)

time: 1320 us -> 728 us (0.55)
  waiting for transfers between devices: 929 us -> 1.93 us
  Pallas kernels: 0 us -> 488 us
  blocking collectives: 129 us -> 0 us
    reduce_scatter x16 -> x0, waiting for transfers between devices: 546 us -> none  [the longest x4 107 us: input_total(): lax.psum_scatter(partial_value.astype(jnp.bfloat16), 'mp', scatter_dimens...]
    pallas_call x0 -> x23, Pallas kernels: none -> 488 us  [the longest x8 184 us: line_scatter(): pl.pallas_call(functools.partial(line_scatter_kernel, axis), out_shape=ja...]
    all_gather x14 -> x4, waiting for transfers between devices: 289 us -> 0.03 us  [the longest x1 0.02 us: body(): lax.all_gather(ffn2_up, 'dp', axis=0, tiled=True)]
    unnamed x36 -> x4, waiting for transfers between devices: 93.2 us -> 1.9 us
    psum x3 -> x0, blocking collectives: 65.6 us -> none  [the longest x1 39.4 us: body(): lax.psum(jnp.stack([gain_one, gain_two, gain_three, gain_four, gain_five]...]
    all_gather x5 -> x0, blocking collectives: 49.8 us -> none  [the longest x1 11.2 us: attn_fetch(): lax.all_gather(w_out, 'dp', axis=1, tiled=True)]
    unnamed x1 -> x0, blocking collectives: 13.3 us -> none
    unnamed x132 -> x138, local copies, waits for them, and re-layouts: 33 us -> 26.7 us
  transfers between devices with their start and end apart: 33 -> 4, of which waited for: 29 -> 0; matrix products, arithmetic and copies ran while one was open for 7% -> 13% of each run, Pallas kernels for 0% -> 28%
where the time goes in v2:
time: 728 us; the launch traced here: 720 us
  Pallas kernels  488 us (67%)
  local copies, waits for them, and re-layouts  87.1 us (12%)
  matrix products  84.3 us (12%)
  other arithmetic  43.2 us (6%)
  between operations  15.6 us (2%)
    pallas_call x8, Pallas kernels, line_scatter(): pl.pallas_call(functools.partial(line_scatter_kernel, axis), out_shape=ja...  184 us
    pallas_call x8, Pallas kernels, line_gather(): pl.pallas_call(functools.partial(line_gather_kernel, axis), out_shape=jax...  168 us
    pallas_call x1, Pallas kernels, cube_scatter(): pl.pallas_call(functools.partial(cube_scatter_kernel, axis, dims, ways),...  65.7 us
    pallas_call x1, Pallas kernels, cube_gather(): pl.pallas_call(functools.partial(cube_gather_kernel, axis, dims, ways), o...  38.7 us
    pallas_call x5, Pallas kernels, all_total(): pl.pallas_call(functools.partial(all_total_kernel, axis), out_shape=jax.S...  32.4 us
    dot_general x9, matrix products, matmul(): return jnp.dot(left, right, preferred_element_type=jnp.float32)  27.3 us
    unnamed x138, local copies, waits for them, and re-layouts  26.7 us
    dot_general x9, matrix products, contract_rows(): lax.dot_general(left, right, (((0,), (0,)), ((), ())), preferred_element_...  20.8 us
  transfers between devices with their start and end apart: 4, of which 0 were waited for; matrix products, arithmetic and copies ran while one was open for 13% of the time, Pallas kernels for 28%

profile of v2, /device:TPU:0, one launch (start us, length us, event | category | flops | bytes accessed | tf_op | source)
XLA Modules:
  0.0 720.2 jit_solution(17314592605521734325)
XLA Ops:
  12.4 38.7 %cube_gather.1 = (bf16[1024,1024]{1,0:T(8,128)(2,1)}, bf16[1024,1024]{1,0:T(8,128)(2,1)}, bf16[1024,256]{1,0:T(8,128)(2,1)}, bf16[256,1024]{1,0:T(8,128)(2,1)}, ...) custom-call(bf16[128,1024]{1,0:T(8,128)(2,1)} %refs_0_.1, bf16[1024,128]{1,0:T(8,128)(2,1)} %refs_1_.1, ...), custom_call_target="tpu_custom_call" | custom-call | tf_op jit(solution)/shard_map/cube_gather/pallas_call | solution.py:353
  55.9 25.6 %line_gather.8 = bf16[512,1024]{1,0:T(8,128)(2,1)} custom-call(bf16[128,1024]{1,0:T(8,128)(2,1)} %fusion.12.in_ref), custom_call_target="tpu_custom_call" | custom-call | tf_op jit(solution)/shard_map/line_gather/pallas_call | solution.py:163
  81.5 8.2 %multiply_sine_fusion = (bf16[1024,512,1]{1,0,2:T(8,128)(2,1)S(1)}, bf16[1024,512,1]{1,0,2:T(8,128)(2,1)S(1)}) fusion(f32[512]{0:T(512)S(1)} %multiply_exponential_fusion, f32[1024]{0:T(1024)S(1)} %subtract_convert_fusion), kind=kLoop, calls=%fused_computation.3 | loop fusion | flops 1572864 | bytes 2103296 | tf_op jit(solution)/shard_map/sin | solution.py:58
  89.9 4.0 copy.93
  93.9 2.8 convert_element_type.286
  97.3 3.3 fusion.76
  104.3 22.8 %line_scatter.8 = f32[128,1024]{1,0:T(8,128)} custom-call(bf16[512,1024]{1,0:T(8,128)(2,1)} %convolution_convert_fusion.11.in_ref), custom_call_target="tpu_custom_call" | custom-call | tf_op jit(solution)/shard_map/line_scatter/pallas_call | solution.py:248
  129.5 20.9 %line_gather.9 = bf16[512,1024]{1,0:T(8,128)(2,1)} custom-call(bf16[128,1024]{1,0:T(8,128)(2,1)} %multiply_convert_fusion.15.in_ref), custom_call_target="tpu_custom_call" | custom-call | tf_op jit(solution)/shard_map/line_gather/pallas_call | solution.py:163
  154.5 3.6 fusion.74
  160.6 2.7 fusion.78
  163.3 9.7 %reshape.472 = f32[2,523776]{1,0:T(2,128)} reshape(f32[2,512,1023]{2,1,0:T(8,128)} %fusion.78) | data formatting | bytes 8380416 | tf_op jit(solution)/shard_map/reshape | solution.py:620
  173.0 7.7 %slice.223 = f32[2,523264]{1,0:T(2,128)} slice(f32[2,523776]{1,0:T(2,128)} %reshape.472), slice={[0:2], [511:523775]} | slice | bytes 8372224 | tf_op jit(solution)/shard_map/slice | solution.py:621
  180.8 10.0 %reshape.473 = f32[2,512,1022]{2,1,0:T(8,128)} reshape(f32[2,523264]{1,0:T(2,128)} %slice.223) | data formatting | bytes 8372224 | tf_op jit(solution)/shard_map/reshape | solution.py:622
  199.0 2.6 convolution_convert_fusion.10.in_ref
  201.6 22.6 %line_scatter.9 = f32[128,1024]{1,0:T(8,128)} custom-call(bf16[512,1024]{1,0:T(8,128)(2,1)} %convolution_convert_fusion.10.in_ref), custom_call_target="tpu_custom_call" | custom-call | tf_op jit(solution)/shard_map/line_scatter/pallas_call | solution.py:248
  226.5 19.3 %line_gather.10 = bf16[512,1024]{1,0:T(8,128)(2,1)} custom-call(bf16[128,1024]{1,0:T(8,128)(2,1)} %multiply_convert_fusion.12.in_ref), custom_call_target="tpu_custom_call" | custom-call | tf_op jit(solution)/shard_map/line_gather/pallas_call | solution.py:163
  249.3 6.0 all_total.5
  258.7 24.0 %line_scatter.10 = f32[128,1024]{1,0:T(8,128)} custom-call(bf16[512,1024]{1,0:T(8,128)(2,1)} %convolution_convert_fusion.9.in_ref), custom_call_target="tpu_custom_call" | custom-call | tf_op jit(solution)/shard_map/line_scatter/pallas_call | solution.py:248
  285.0 20.7 %line_gather.11 = bf16[512,1024]{1,0:T(8,128)(2,1)} custom-call(bf16[128,1024]{1,0:T(8,128)(2,1)} %multiply_convert_fusion.10.in_ref), custom_call_target="tpu_custom_call" | custom-call | tf_op jit(solution)/shard_map/line_gather/pallas_call | solution.py:163
  305.7 4.5 fusion.80
  310.2 4.6 convolution_convert_fusion.8.in_ref
  314.7 23.4 %line_scatter.11 = f32[128,1024]{1,0:T(8,128)} custom-call(bf16[512,1024]{1,0:T(8,128)(2,1)} %convolution_convert_fusion.8.in_ref), custom_call_target="tpu_custom_call" | custom-call | tf_op jit(solution)/shard_map/line_scatter/pallas_call | solution.py:248
  342.4 19.9 %line_gather.12 = bf16[512,1024]{1,0:T(8,128)(2,1)} custom-call(bf16[128,1024]{1,0:T(8,128)(2,1)} %multiply_convert_fusion.8.in_ref), custom_call_target="tpu_custom_call" | custom-call | tf_op jit(solution)/shard_map/line_gather/pallas_call | solution.py:163
  362.4 4.7 convolution_convert_fusion.2.refs_1_
  368.8 2.6 convolution_convert_fusion.3.refs_0_
  373.7 20.5 %line_scatter.12 = f32[128,1024]{1,0:T(8,128)} custom-call(bf16[512,1024]{1,0:T(8,128)(2,1)} %convolution_convert_fusion.7.in_ref), custom_call_target="tpu_custom_call" | custom-call | tf_op jit(solution)/shard_map/line_scatter/pallas_call | solution.py:248
  397.7 19.3 %line_gather.13 = bf16[512,1024]{1,0:T(8,128)(2,1)} custom-call(bf16[128,1024]{1,0:T(8,128)(2,1)} %get-tuple-element.153.in_ref), custom_call_target="tpu_custom_call" | custom-call | tf_op jit(solution)/shard_map/line_gather/pallas_call | solution.py:163
  417.1 2.8 fusion.56
  421.9 5.9 all_total.6
  436.1 22.9 %line_scatter.13 = f32[128,1024]{1,0:T(8,128)} custom-call(bf16[512,1024]{1,0:T(8,128)(2,1)} %convolution_convert_fusion.13.in_ref), custom_call_target="tpu_custom_call" | custom-call | tf_op jit(solution)/shard_map/line_scatter/pallas_call | solution.py:248
  462.5 20.9 %line_gather.14 = bf16[512,1024]{1,0:T(8,128)(2,1)} custom-call(bf16[128,1024]{1,0:T(8,128)(2,1)} %fusion.30.in_ref), custom_call_target="tpu_custom_call" | custom-call | tf_op jit(solution)/shard_map/line_gather/pallas_call | solution.py:163
  483.3 2.6 convolution_convert_fusion.20
  487.2 3.9 convolution_convert_fusion.18
  498.9 5.1 reshape.491
  504.0 3.4 reshape.477
  507.4 4.8 pad.28
  512.2 2.6 reshape.493
  514.8 5.1 reshape.478
  528.7 6.1 all_total.9
  536.7 23.1 %line_scatter.14 = f32[128,1024]{1,0:T(8,128)} custom-call(bf16[512,1024]{1,0:T(8,128)(2,1)} %convolution_convert_fusion.5.in_ref), custom_call_target="tpu_custom_call" | custom-call | tf_op jit(solution)/shard_map/line_scatter/pallas_call | solution.py:248
  563.4 21.0 %line_gather.15 = bf16[512,1024]{1,0:T(8,128)(2,1)} custom-call(bf16[128,1024]{1,0:T(8,128)(2,1)} %get-tuple-element.142.in_ref), custom_call_target="tpu_custom_call" | custom-call | tf_op jit(solution)/shard_map/line_gather/pallas_call | solution.py:163
  584.4 4.3 multiply_convert_fusion
  588.7 2.7 convolution_convert_fusion.refs_8_
  593.7 2.6 convolution_convert_fusion.1.refs_7_
  598.0 24.2 %line_scatter.15 = f32[128,1024]{1,0:T(8,128)} custom-call(bf16[512,1024]{1,0:T(8,128)(2,1)} %convolution_convert_fusion.6.in_ref), custom_call_target="tpu_custom_call" | custom-call | tf_op jit(solution)/shard_map/line_scatter/pallas_call | solution.py:248
  622.3 65.7 %cube_scatter.1 = (f32[128,1024]{1,0:T(8,128)}, f32[1024,128]{1,0:T(8,128)}, f32[128,512]{1,0:T(8,128)}, f32[256,128]{1,0:T(8,128)}, f32[128,768]{1,0:T(8,128)},...) custom-call(bf16[1024,1024]{1,0:T(8,128)(2,1)} %convolution_convert_fusion.3.refs_0_, ...), custom_call_target="tpu_custom_call" | custom-call | tf_op jit(solution)/shard_map/cube_scatter/pallas_call | solution.py:440
  689.2 7.0 all_total.7.in_ref
  696.2 7.5 %all_total.8 = f32[5,1024]{1,0:T(8,128)} custom-call(f32[5,1024]{1,0:T(8,128)} %all_total.7.in_ref), custom_call_target="tpu_custom_call" | custom-call | tf_op jit(solution)/shard_map/all_total/pallas_call | solution.py:479
  (270 shorter events, 105.6 us)
Async XLA Ops:
  7.2 44.9 %copy-start.56 = (s32[8]{0:T(128)S(1)}, s32[8]{0:T(128)}, u32[]{:S(2)}) copy-start(s32[8]{0:T(128)} %param.20) | copy-start | bytes 100
  7.2 46.8 %copy-start = (bf16[1,128,1024]{2,1,0:T(8,128)(2,1)S(1)}, bf16[1,128,1024]{2,1,0:T(8,128)(2,1)}, u32[]{:S(2)}) copy-start(bf16[1,128,1024]{2,1,0:T(8,128)(2,1)} %param.19) | copy-start | bytes 786436
  7.2 47.8 %copy-start.49 = (f32[5,1024]{1,0:T(8,128)S(1)}, f32[5,1024]{1,0:T(8,128)}, u32[]{:S(2)}) copy-start(f32[5,1024]{1,0:T(8,128)} %param.22) | copy-start | bytes 61444
  7.2 144.7 %all-gather.7.cloned.1.call-start = ((), (), s32[]{:S(2)}) async-start(), calls=%async_computation.1 | async-start | bytes 1179648 | tf_op jit(solution)/shard_map/all_gather | solution.py:836
  7.9 146.5 %all-gather.5.cloned.1.call-start = ((), (), s32[]{:S(2)}) async-start(), calls=%async_computation | async-start | bytes 1769472 | tf_op jit(solution)/shard_map/all_gather | solution.py:830
  9.8 295.9 %all-gather.9.cloned.1.call-start = ((), (), s32[]{:S(2)}) async-start(), calls=%async_computation.2 | async-start | bytes 2359296 | tf_op jit(solution)/shard_map/all_gather | solution.py:843
  10.5 299.7 %all-gather.11.cloned.1.call-start = ((), (), s32[]{:S(2)}) async-start(), calls=%async_computation.3 | async-start | bytes 2359296 | tf_op jit(solution)/shard_map/all_gather | solution.py:844
  96.7 53.7 %copy-start.20 = (bf16[1024,1024]{0,1:T(8,128)(2,1)}, bf16[1024,1024]{0,1:T(8,128)(2,1)S(1)}, u32[]{:S(2)}) copy-start(bf16[1024,1024]{0,1:T(8,128)(2,1)S(1)} %convert_element_type.286) | copy-start | bytes 6291460
  97.3 4.7 copy-start.51
  127.1 23.2 %copy-start.55 = (bf16[1024,256]{1,0:T(8,128)(2,1)S(1)}, bf16[1024,256]{1,0:T(8,128)(2,1)}, u32[]{:S(2)}) copy-start(bf16[1024,256]{1,0:T(8,128)(2,1)} %get-tuple-element.46) | copy-start | bytes 1572868
  151.9 2.6 copy-start.29
  158.1 2.5 copy-start.22
  159.0 35.2 %copy-start.12 = (bf16[512,256]{0,1:T(8,128)(2,1)}, bf16[512,256]{0,1:T(8,128)(2,1)S(1)}, u32[]{:S(2)}) copy-start(bf16[512,256]{0,1:T(8,128)(2,1)S(1)} %copy.120) | copy-start | bytes 786436
  160.4 33.8 %copy-start.14 = (bf16[512,256]{0,1:T(8,128)(2,1)}, bf16[512,256]{0,1:T(8,128)(2,1)S(1)}, u32[]{:S(2)}) copy-start(bf16[512,256]{0,1:T(8,128)(2,1)S(1)} %copy.119) | copy-start | bytes 786436
  160.6 2.7 copy-start.16
  199.0 26.5 %copy-start.26 = (bf16[2,128,512]{2,1,0:T(8,128)(2,1)}, bf16[2,128,512]{2,1,0:T(8,128)(2,1)S(1)}, u32[]{:S(2)}) copy-start(bf16[2,128,512]{2,1,0:T(8,128)(2,1)S(1)} %convolution_convert_fusion.21) | copy-start | bytes 786436
  248.3 10.4 %copy-start.5 = (f32[512,256]{1,0:T(8,128)}, f32[512,256]{1,0:T(8,128)S(1)}, u32[]{:S(2)}) copy-start(f32[512,256]{1,0:T(8,128)S(1)} %multiply_multiply_fusion) | copy-start | bytes 1572868
  248.7 34.0 %copy-start.17 = (f32[512,256]{1,0:T(8,128)}, f32[512,256]{1,0:T(8,128)S(1)}, u32[]{:S(2)}) copy-start(f32[512,256]{1,0:T(8,128)S(1)} %get-tuple-element.163) | copy-start | bytes 1572868
  314.7 24.8 %copy-start.37 = (bf16[1,128,1024]{2,1,0:T(8,128)(2,1)S(1)}, bf16[1,128,1024]{2,1,0:T(8,128)(2,1)}, u32[]{:S(2)}) copy-start(bf16[1,128,1024]{2,1,0:T(8,128)(2,1)} %param.21) | copy-start | bytes 786436
  362.4 4.7 copy-start.34
  362.4 4.7 copy-start.53
  362.4 4.7 copy-start.60
  368.8 2.6 copy-start.52
  394.2 2.7 copy-start.8
  396.8 20.2 %copy-start.18 = (f32[512,256]{1,0:T(8,128)S(1)}, f32[512,256]{1,0:T(8,128)}, u32[]{:S(2)}) copy-start(f32[512,256]{1,0:T(8,128)} %copy-done.17) | copy-start | bytes 1572868
  417.1 2.9 copy-start.19
  417.1 2.9 copy-start.33
  419.9 9.7 %copy-start.6 = (f32[512,256]{1,0:T(8,128)S(1)}, f32[512,256]{1,0:T(8,128)}, u32[]{:S(2)}) copy-start(f32[512,256]{1,0:T(8,128)} %copy-done.5) | copy-start | bytes 1572868
  461.6 24.4 %copy-start.9 = (f32[128,1024]{1,0:T(8,128)}, f32[128,1024]{1,0:T(8,128)S(1)}, u32[]{:S(2)}) copy-start(f32[128,1024]{1,0:T(8,128)S(1)} %get-tuple-element.147) | copy-start | bytes 1572868
  461.6 24.3 %copy-start.27 = (bf16[2,128,512]{2,1,0:T(8,128)(2,1)S(1)}, bf16[2,128,512]{2,1,0:T(8,128)(2,1)}, u32[]{:S(2)}) copy-start(bf16[2,128,512]{2,1,0:T(8,128)(2,1)} %copy-done.26) | copy-start | bytes 786436
  483.3 2.6 copy-start.11
  487.2 3.9 copy-start.1
  536.7 25.8 %copy-start.10 = (f32[128,1024]{1,0:T(8,128)S(1)}, f32[128,1024]{1,0:T(8,128)}, u32[]{:S(2)}) copy-start(f32[128,1024]{1,0:T(8,128)} %copy-done.9) | copy-start | bytes 1572868
  584.4 4.3 copy-start.35
  584.4 4.3 copy-start.59
  588.7 2.7 copy-start.50
  593.7 2.7 copy-start.25
  593.7 2.7 copy-start.21
  622.2 65.7 %copy-start.4 = (f32[128,1024]{1,0:T(8,128)S(1)}, f32[128,1024]{1,0:T(8,128)}, u32[]{:S(2)}) copy-start(f32[128,1024]{1,0:T(8,128)} %line_scatter.15) | copy-start | bytes 1572868
  688.0 17.6 %copy-start.42 = (f32[128,768]{1,0:T(8,128)S(1)}, f32[128,768]{1,0:T(8,128)}, u32[]{:S(2)}) copy-start(f32[128,768]{1,0:T(8,128)} %get-tuple-element.51) | copy-start | bytes 1179652
  688.6 19.7 %copy-start.41 = (f32[128,1024]{1,0:T(8,128)S(1)}, f32[128,1024]{1,0:T(8,128)}, u32[]{:S(2)}) copy-start(f32[128,1024]{1,0:T(8,128)} %get-tuple-element.222) | copy-start | bytes 1572868
  703.7 4.0 copy-start.48
  705.5 3.6 copy-start.40
  706.6 3.3 copy-start.47
  706.6 3.9 copy-start.46
  706.6 4.6 copy-start.45
  706.6 5.2 copy-start.39
  707.7 5.0 copy-start.38
  (18 other events, 30.8 us)
Sparse Core Ops, SparseCore 0:
  9.9 30.4 all-gather.6
  42.9 25.7 all-gather.4
  70.6 27.8 all-gather.8
  100.3 27.9 all-gather.10

commit v3 on v2

--- a/solution.py
+++ b/solution.py
@@ -50,12 +50,18 @@
 
 
 def position_table(seq_len, model_width):
-    distance = (seq_len - 1 - jnp.arange(2 * seq_len)).astype(jnp.float32)
-    frequency = jnp.exp(
-        jnp.arange(model_width // 2).astype(jnp.float32) * (-2.0 * math.log(10000.0) / model_width)
-    )
-    angles = distance[:, None] * frequency[None, :]
-    return jnp.stack([jnp.sin(angles), jnp.cos(angles)], axis=-1).reshape(2 * seq_len, model_width)
+    fine = 32
+    lane = jnp.arange(model_width)
+    frequency = jnp.exp((lane // 2).astype(jnp.float32) * (-2.0 * math.log(10000.0) / model_width))
+    coarse = (seq_len - 1 - fine * jnp.arange(2 * seq_len // fine)).astype(jnp.float32)
+    wide = coarse[:, None] * frequency[None, :]
+    small = -jnp.arange(fine).astype(jnp.float32)[:, None] * frequency[None, :]
+    even = (lane % 2 == 0)[None, :]
+    wide_sin, wide_cos = jnp.sin(wide), jnp.cos(wide)
+    high = jnp.where(even, wide_sin, wide_cos)
+    side = jnp.where(even, wide_cos, -wide_sin)
+    table = high[:, None, :] * jnp.cos(small)[None] + side[:, None, :] * jnp.sin(small)[None]
+    return table.reshape(2 * seq_len, model_width)
 
 
 MESH = pl.DeviceIdType.MESH
@@ -582,133 +588,160 @@
     return (contract_cols(d_hidden, w_up), grad_up, grad_down)
 
 
-def attention_setup(whole, weights):
+def place_position(position_ref, block, rows, seq_len):
+    start = pl.multiple_of(seq_len - rows - block * rows, rows)
+    return position_ref.at[pl.ds(start, seq_len + rows)]
+
+
+def attention_kernel(
+    scaling, length_ref, whole_ref, in_ref, bias_ref, position_ref, out_w_ref,
+    partial_ref, probs_ref, context_ref, query_u_ref, query_v_ref, key_ref, value_ref,
+):
+    block = pl.program_id(0)
+    seq_len, local_width = key_ref.shape
+    rows = partial_ref.shape[0]
+
+    @pl.when(block == 0)
+    def _():
+        projected = matmul(whole_ref[...], in_ref[...])
+        queries = projected[:, :local_width]
+        query_u_ref[...] = ((queries + bias_ref[0:1]) * scaling).astype(jnp.bfloat16)
+        query_v_ref[...] = ((queries + bias_ref[1:2]) * scaling).astype(jnp.bfloat16)
+        key_ref[...] = projected[:, local_width : 2 * local_width].astype(jnp.bfloat16)
+        value_ref[...] = projected[:, 2 * local_width :].astype(jnp.bfloat16)
+
+    here = pl.ds(pl.multiple_of(block * rows, rows), rows)
+    valid = lax.broadcasted_iota(jnp.int32, (rows, seq_len), 1) < length_ref[0]
+    nearby = place_position(position_ref, block, rows, seq_len)
+    pieces = []
+    for head in range(local_width // HEAD):
+        lanes = slice(head * HEAD, (head + 1) * HEAD)
+        content = contract_cols(query_u_ref[here, lanes], key_ref[:, lanes])
+        zeds = contract_cols(query_v_ref[here, lanes], nearby[:, lanes])
+        shifted = pltpu.roll(zeds, seq_len + 1, 1, stride=1, stride_axis=0)[:, :seq_len]
+        scores = jnp.where(valid, content + shifted, masked_score)
+        exponent = jnp.exp(scores - jnp.max(scores, axis=-1, keepdims=True))
+        probs = exponent / jnp.sum(exponent, axis=-1, keepdims=True)
+        probs_ref[head] = probs
+        pieces.append(matmul(probs.astype(jnp.bfloat16), value_ref[:, lanes]).astype(jnp.bfloat16))
+    context = jnp.concatenate(pieces, axis=1)
+    context_ref[...] = context
+    partial_ref[...] = matmul(context, out_w_ref[...]).astype(jnp.bfloat16)
+
+
+def attention_forward(whole, weights, position, own_length):
     w_in, w_pos, bias_pair, w_out = weights
     seq_len, model_width = whole.shape
-    local_width = w_in.shape[2]
+    local_width = w_out.shape[0]
     heads_here = local_width // HEAD
-    projected = matmul(whole, w_in.reshape(model_width, 3 * local_width))
-    queries = projected[:, :local_width]
-    key_rows = (
-        projected[:, local_width : 2 * local_width]
-        .astype(jnp.bfloat16)
-        .reshape(seq_len, heads_here, HEAD)
-    )
-    value_rows = (
-        projected[:, 2 * local_width :].astype(jnp.bfloat16).reshape(seq_len, heads_here, HEAD)
-    )
-    scaling = HEAD ** (-0.5)
-    bias_float = bias_pair.astype(jnp.float32)
-    query_u = (
-        ((queries + bias_float[0]) * scaling)
-        .astype(jnp.bfloat16)
-        .reshape(seq_len, heads_here, HEAD)
-    )
-    query_v = (
-        ((queries + bias_float[1]) * scaling)
-        .astype(jnp.bfloat16)
-        .reshape(seq_len, heads_here, HEAD)
-    )
-    table_low = position_table(seq_len, model_width).astype(jnp.bfloat16)
-    position = matmul(table_low, w_pos).astype(jnp.bfloat16).reshape(2 * seq_len, heads_here, HEAD)
-    return (query_u, query_v, key_rows, value_rows, table_low, position)
-
-
-def skew_rows(zeds, block_rows, seq_len):
-    heads_here = zeds.shape[0]
-    window = block_rows + seq_len - 1
-    flat = zeds.reshape(heads_here, block_rows * window)
-    flat = flat[:, block_rows - 1 : block_rows - 1 + block_rows * (window - 1)]
-    return flat.reshape(heads_here, block_rows, window - 1)[:, :, :seq_len]
-
-
-def unskew_rows(grads_in, block_rows, seq_len):
-    heads_here = grads_in.shape[0]
-    window = block_rows + seq_len - 1
-    padded = jnp.pad(grads_in, ((0, 0), (0, 0), (0, window - 1 - seq_len)))
-    flat = padded.reshape(heads_here, block_rows * (window - 1))
-    flat = jnp.pad(flat, ((0, 0), (block_rows - 1, 1)))
-    return flat.reshape(heads_here, block_rows, window)
-
-
-def block_scores(query_u, query_v, key_rows, position, valid_keys, offset, block_rows):
-    seq_len = key_rows.shape[0]
-    window = block_rows + seq_len - 1
-    lowest = seq_len - offset - block_rows
-    nearby = position[lowest : lowest + window]
-    content = jnp.einsum("bhd,jhd->hbj", query_u, key_rows, preferred_element_type=jnp.float32)
-    zeds = jnp.einsum("bhd,whd->hbw", query_v, nearby, preferred_element_type=jnp.float32)
-    scores = jnp.where(
-        valid_keys[None, None, :], content + skew_rows(zeds, block_rows, seq_len), masked_score
-    )
-    top_score = jnp.max(scores, axis=-1, keepdims=True)
-    exponent = jnp.exp(scores - top_score)
-    softmax_out = exponent / jnp.sum(exponent, axis=-1, keepdims=True)
-    return (softmax_out, query_u, query_v, nearby, lowest)
-
-
-def attention_forward(whole, weights, valid_keys, block_rows):
-    seq_len = whole.shape[0]
-    query_u, query_v, key_rows, value_rows, table_low, position = attention_setup(whole, weights)
-    softmax_out, part_u, part_v, nearby, lowest = block_scores(
-        query_u, query_v, key_rows, position, valid_keys, 0, block_rows
-    )
-    contexts = jnp.einsum(
-        "hbj,jhd->bhd",
-        softmax_out.astype(jnp.bfloat16),
-        value_rows,
-        preferred_element_type=jnp.float32,
-    )
-    context = contexts.reshape(seq_len, -1).astype(jnp.bfloat16)
-    return matmul(context, weights[3])
-
-
-def attention_backward(whole, weights, valid_keys, block_rows, grad_whole):
+    rows = 128
+    full = pl.BlockSpec(memory_space=pltpu.VMEM)
+    low = jnp.bfloat16
+    return pl.pallas_call(
+        functools.partial(attention_kernel, HEAD ** (-0.5)),
+        grid=(seq_len // rows,),
+        out_shape=[
+            jax.ShapeDtypeStruct((seq_len, model_width), low),
+            jax.ShapeDtypeStruct((heads_here, seq_len, seq_len), jnp.float32),
+        ]
+        + [jax.ShapeDtypeStruct((seq_len, local_width), low)] * 5,
+        in_specs=[pl.BlockSpec(memory_space=pltpu.SMEM)] + [full] * 5,
+        out_specs=[
+            pl.BlockSpec((rows, model_width), lambda block: (block, 0)),
+            pl.BlockSpec((heads_here, rows, seq_len), lambda block: (0, block, 0)),
+            pl.BlockSpec((rows, local_width), lambda block: (block, 0)),
+        ]
+        + [full] * 4,
+        compiler_params=pltpu.CompilerParams(vmem_limit_bytes=VMEM_LIMIT),
+        name="attention_forward",
+    )(own_length, whole, w_in, bias_pair.astype(jnp.float32), position, w_out)
+
+
+def attention_back_kernel(
+    scaling, grad_ref, out_w_ref, probs_ref, query_u_ref, query_v_ref, key_ref, value_ref,
+    position_ref, d_projected_ref, d_position_ref, bias_ref, d_keys, d_values, d_places,
+):
+    block = pl.program_id(0)
+    seq_len, local_width = key_ref.shape
+    rows = grad_ref.shape[0]
+
+    @pl.when(block == 0)
+    def _():
+        d_keys[...] = jnp.zeros_like(d_keys)
+        d_values[...] = jnp.zeros_like(d_values)
+        d_places[...] = jnp.zeros_like(d_places)
+        bias_ref[...] = jnp.zeros_like(bias_ref)
+
+    here = pl.ds(pl.multiple_of(block * rows, rows), rows)
+    nearby = place_position(position_ref, block, rows, seq_len)
+    d_nearby = place_position(d_places, block, rows, seq_len)
+    upside = (
+        lax.broadcasted_iota(jnp.int32, (rows, rows), 0)
+        + lax.broadcasted_iota(jnp.int32, (rows, rows), 1)
+        == rows - 1
+    ).astype(jnp.bfloat16)
+    d_context_all = contract_cols(grad_ref[...], out_w_ref[...]).astype(jnp.bfloat16)
+    for head in range(local_width // HEAD):
+        lanes = slice(head * HEAD, (head + 1) * HEAD)
+        d_context = d_context_all[:, lanes]
+        probs = probs_ref[head]
+        d_probs = contract_cols(d_context, value_ref[:, lanes])
+        inner = jnp.sum(probs * d_probs, axis=-1, keepdims=True)
+        d_scores = (probs * (d_probs - inner)).astype(jnp.bfloat16)
+        d_values[:, lanes] += contract_rows(probs.astype(jnp.bfloat16), d_context)
+        d_keys[:, lanes] += contract_rows(d_scores, query_u_ref[here, lanes])
+        grad_u = matmul(d_scores, key_ref[:, lanes]) * scaling
+        turned = matmul(upside, d_scores)
+        turned = jnp.concatenate([turned, jnp.zeros((rows, rows), jnp.float32)], axis=1)
+        turned = pltpu.roll(turned, 0, 1, stride=1, stride_axis=0).astype(jnp.bfloat16)
+        d_zeds = matmul(upside, turned).astype(jnp.bfloat16)
+        grad_v = matmul(d_zeds, nearby[:, lanes]) * scaling
+        d_nearby[:, lanes] += contract_rows(d_zeds, query_v_ref[here, lanes])
+        d_projected_ref[here, lanes] = (grad_u + grad_v).astype(jnp.bfloat16)
+        bias_ref[0:1, lanes] += jnp.sum(grad_u, axis=0, keepdims=True)
+        bias_ref[1:2, lanes] += jnp.sum(grad_v, axis=0, keepdims=True)
+
+    @pl.when(block == pl.num_programs(0) - 1)
+    def _():
+        d_projected_ref[:, local_width : 2 * local_width] = d_keys[...].astype(jnp.bfloat16)
+        d_projected_ref[:, 2 * local_width :] = d_values[...].astype(jnp.bfloat16)
+        d_position_ref[...] = d_places[...].astype(jnp.bfloat16)
+
+
+def attention_backward(whole, weights, table_low, position, saved, grad_whole):
     w_in, w_pos, bias_pair, w_out = weights
+    probs, context, query_u, query_v, key_rows, value_rows = saved
     seq_len, model_width = whole.shape
-    query_u, query_v, key_rows, value_rows, table_low, position = attention_setup(whole, weights)
-    heads_here = key_rows.shape[1]
-    local_width = w_in.shape[2]
-    scaling = HEAD ** (-0.5)
-    window = block_rows + seq_len - 1
-    d_context = (
-        contract_cols(grad_whole, w_out).astype(jnp.bfloat16).reshape(seq_len, heads_here, HEAD)
-    )
-    d_position = jnp.zeros(position.shape, jnp.float32)
-    softmax_out, part_u, part_v, nearby, lowest = block_scores(
-        query_u, query_v, key_rows, position, valid_keys, 0, block_rows
-    )
-    soft_low = softmax_out.astype(jnp.bfloat16)
-    contexts = jnp.einsum("hbj,jhd->bhd", soft_low, value_rows, preferred_element_type=jnp.float32)
-    d_soft = jnp.einsum("bhd,jhd->hbj", d_context, value_rows, preferred_element_type=jnp.float32)
-    inner = jnp.sum(softmax_out * d_soft, axis=-1, keepdims=True)
-    d_scores = (softmax_out * (d_soft - inner)).astype(jnp.bfloat16)
-    d_query_u = jnp.einsum("hbj,jhd->bhd", d_scores, key_rows, preferred_element_type=jnp.float32)
-    d_keys = jnp.einsum("hbj,bhd->jhd", d_scores, part_u, preferred_element_type=jnp.float32)
-    d_values = jnp.einsum("hbj,bhd->jhd", soft_low, d_context, preferred_element_type=jnp.float32)
-    d_zeds = unskew_rows(d_scores, block_rows, seq_len)
-    d_query_v = jnp.einsum("hbw,whd->bhd", d_zeds, nearby, preferred_element_type=jnp.float32)
-    d_position = d_position.at[lowest : lowest + window].add(
-        jnp.einsum("hbw,bhd->whd", d_zeds, part_v, preferred_element_type=jnp.float32)
-    )
-    grad_u = d_query_u.reshape(seq_len, local_width) * scaling
-    grad_v = d_query_v.reshape(seq_len, local_width) * scaling
-    d_queries = (grad_u + grad_v).astype(jnp.bfloat16)
-    grad_bias = jnp.stack([jnp.sum(grad_u, axis=0), jnp.sum(grad_v, axis=0)])
-    d_projected = jnp.concatenate(
-        [
-            d_queries,
-            d_keys.reshape(seq_len, local_width).astype(jnp.bfloat16),
-            d_values.reshape(seq_len, local_width).astype(jnp.bfloat16),
+    local_width = w_out.shape[0]
+    heads_here = local_width // HEAD
+    rows = 128
+    full = pl.BlockSpec(memory_space=pltpu.VMEM)
+    d_projected, d_position, grad_bias = pl.pallas_call(
+        functools.partial(attention_back_kernel, HEAD ** (-0.5)),
+        grid=(seq_len // rows,),
+        out_shape=[
+            jax.ShapeDtypeStruct((seq_len, 3 * local_width), jnp.bfloat16),
+            jax.ShapeDtypeStruct((2 * seq_len, local_width), jnp.bfloat16),
+            jax.ShapeDtypeStruct((2, local_width), jnp.float32),
         ],
-        axis=1,
-    )
-    grad_in = contract_rows(whole, d_projected).reshape(model_width, 3, local_width)
-    d_normed = contract_cols(d_projected, w_in.reshape(model_width, 3 * local_width))
-    grad_pos = contract_rows(
-        table_low, d_position.reshape(2 * seq_len, local_width).astype(jnp.bfloat16)
-    )
-    context = contexts.reshape(seq_len, local_width).astype(jnp.bfloat16)
+        in_specs=[
+            pl.BlockSpec((rows, model_width), lambda block: (block, 0)),
+            full,
+            pl.BlockSpec((heads_here, rows, seq_len), lambda block: (0, block, 0)),
+        ]
+        + [full] * 5,
+        out_specs=[full] * 3,
+        scratch_shapes=[
+            pltpu.VMEM((seq_len, local_width), jnp.float32),
+            pltpu.VMEM((seq_len, local_width), jnp.float32),
+            pltpu.VMEM((2 * seq_len, local_width), jnp.float32),
+        ],
+        compiler_params=pltpu.CompilerParams(vmem_limit_bytes=VMEM_LIMIT),
+        name="attention_backward",
+    )(grad_whole, w_out, probs, query_u, query_v, key_rows, value_rows, position)
+    grad_in = contract_rows(whole, d_projected)
+    d_normed = contract_cols(d_projected, w_in)
+    grad_pos = contract_rows(table_low, d_position)
     grad_out = contract_rows(context, grad_whole)
     return (d_normed, grad_in, grad_pos, grad_bias, grad_out)
 
@@ -812,7 +845,6 @@
 ):
     unused, local_rows, model_width = frames_in.shape
     seq_len = local_rows * lax.axis_size("mp")
-    block_rows = min(seq_len, 512)
     dp_index = lax.axis_index("dp")
     own_length = lax.dynamic_slice_in_dim(lengths, dp_index, 1)[0]
     valid_keys = jnp.arange(seq_len) < own_length
@@ -827,7 +859,9 @@
     taps = depthwise.shape[0]
     ffn_first = (up_one, down_one)
     attn_held = (
-        lax.all_gather(attn_in, "dp", axis=0, tiled=True),
+        lax.all_gather(
+            attn_in.reshape(attn_in.shape[0], -1), "dp", axis=0, tiled=True
+        ),
         pos_whole,
         small[:2],
         attn_out_whole,
@@ -846,9 +880,12 @@
     whole_first = enter_block(layer_input, norm_gains[0])
     after_first = layer_input + 0.5 * branch_total(ffn_forward(whole_first, ffn_first))
     whole_attn = enter_block(after_first, norm_gains[1])
-    after_attn = after_first + branch_total(
-        attention_forward(whole_attn, attn_held, valid_keys, block_rows)
-    )
+    table_low = position_table(seq_len, model_width).astype(jnp.bfloat16)
+    position = matmul(table_low, pos_whole).astype(jnp.bfloat16)
+    attn_partial, *attn_saved = attention_forward(
+        whole_attn, attn_held, position, own_length[None]
+    )
+    after_attn = after_first + branch_total(attn_partial)
     whole_conv = enter_block(after_attn, norm_gains[2])
     gate_value, logistic, padded, conved = conv_front(
         whole_conv, conv_held[0], conv_held[1], mask_col
@@ -882,8 +919,9 @@
     d_normed, grad_attn_in, grad_pos, grad_bias, grad_attn_out = attention_backward(
         whole_attn,
         attn_held,
-        valid_keys,
-        block_rows,
+        table_low,
+        position,
+        attn_saved,
         spread_grads(d_attn.astype(jnp.bfloat16)),
     )
     d_branch, gain_two = norm_back(after_first, norm_gains[1], input_total(d_normed))
@@ -901,7 +939,7 @@
             grad_down_two,
             grad_conv_in.reshape(model_width, -1),
             grad_conv_out,
-            grad_attn_in.reshape(model_width, -1),
+            grad_attn_in,
             grad_attn_out,
             grad_pos,
             grad_up_one,

time: 728 us -> 656 us (0.901)
  local copies, waits for them, and re-layouts: 87.1 us -> 24.2 us
  matrix products: 84.3 us -> 59.4 us
  Pallas kernels: 488 us -> 512 us
  other arithmetic: 43.2 us -> 32.8 us
    reshape x7 -> x1, local copies, waits for them, and re-layouts: 28.7 us -> 0.83 us  [body(): attn_in.reshape(attn_in.shape[0], -1)]
    pallas_call x0 -> x2, Pallas kernels: none -> 22.8 us  [the longest x1 12.6 us: attention_backward(): pl.pallas_call(functools.partial(attention_back_kernel, HEAD ** (-0.5)),...]
    dot_general x9 -> x0, matrix products: 16.4 us -> none  [the longest x1 3.85 us: attention_backward(): jnp.einsum('hbj,bhd->jhd', soft_low, d_context, preferred_element_type=jn...]
    unnamed x138 -> x98, local copies, waits for them, and re-layouts: 26.7 us -> 14.3 us
    slice x5 -> x0, local copies, waits for them, and re-layouts: 10.1 us -> none  [the longest x1 7.74 us: skew_rows(): flat = flat[:, block_rows - 1:block_rows - 1 + block_rows * (window - 1)]]
    sin x1 -> x0, other arithmetic: 8.15 us -> none  [position_table(): jnp.sin(angles)]
    dot_general x9 -> x7, matrix products: 27.3 us -> 20.1 us  [matmul(): return jnp.dot(left, right, preferred_element_type=jnp.float32)]
    dot_general x8 -> x7, matrix products: 19.8 us -> 17.3 us  [contract_cols(): lax.dot_general(left, right, (((1,), (1,)), ((), ())), preferred_element_...]
  transfers between devices with their start and end apart: 4 -> 4, of which waited for: 0 -> 0; matrix products, arithmetic and copies ran while one was open for 13% -> 6% of each run, Pallas kernels for 28% -> 33%
where the time goes in v3:
time: 656 us; the launch traced here: 647 us
  Pallas kernels  512 us (78%)
  matrix products  59.4 us (9%)
  other arithmetic  32.8 us (5%)
  local copies, waits for them, and re-layouts  24.2 us (4%)
  between operations  15.6 us (2%)
    pallas_call x8, Pallas kernels, line_scatter(): pl.pallas_call(functools.partial(line_scatter_kernel, axis), out_shape=ja...  182 us
    pallas_call x8, Pallas kernels, line_gather(): pl.pallas_call(functools.partial(line_gather_kernel, axis), out_shape=jax...  171 us
    pallas_call x1, Pallas kernels, cube_scatter(): pl.pallas_call(functools.partial(cube_scatter_kernel, axis, dims, ways),...  65.8 us
    pallas_call x1, Pallas kernels, cube_gather(): pl.pallas_call(functools.partial(cube_gather_kernel, axis, dims, ways), o...  38.7 us
    pallas_call x5, Pallas kernels, all_total(): pl.pallas_call(functools.partial(all_total_kernel, axis), out_shape=jax.S...  32.3 us
    dot_general x9, matrix products, contract_rows(): lax.dot_general(left, right, (((0,), (0,)), ((), ())), preferred_element_...  22 us
    dot_general x7, matrix products, matmul(): return jnp.dot(left, right, preferred_element_type=jnp.float32)  20.1 us
    dot_general x7, matrix products, contract_cols(): lax.dot_general(left, right, (((1,), (1,)), ((), ())), preferred_element_...  17.3 us
  transfers between devices with their start and end apart: 4, of which 0 were waited for; matrix products, arithmetic and copies ran while one was open for 6% of the time, Pallas kernels for 33%

profile of v3, /device:TPU:0, one launch (start us, length us, event | category | flops | bytes accessed | tf_op | source)
XLA Modules:
  0.0 646.5 jit_solution(1963374791029401023)
XLA Ops:
  12.6 38.7 %cube_gather.1 = (bf16[1024,1024]{1,0:T(8,128)(2,1)}, bf16[1024,1024]{1,0:T(8,128)(2,1)}, bf16[1024,256]{1,0:T(8,128)(2,1)}, bf16[256,1024]{1,0:T(8,128)(2,1)}, ...) custom-call(bf16[128,1024]{1,0:T(8,128)(2,1)} %refs_0_.1, bf16[1024,128]{1,0:T(8,128)(2,1)} %refs_1_.1, ...), custom_call_target="tpu_custom_call" | custom-call | tf_op jit(solution)/shard_map/cube_gather/pallas_call | solution.py:359
  56.3 25.5 %line_gather.8 = bf16[512,1024]{1,0:T(8,128)(2,1)} custom-call(bf16[128,1024]{1,0:T(8,128)(2,1)} %fusion.10.in_ref), custom_call_target="tpu_custom_call" | custom-call | tf_op jit(solution)/shard_map/line_gather/pallas_call | solution.py:169
  83.0 2.7 fusion.72
  87.0 2.3 convolution_convert_fusion.10.in_ref
  89.3 22.7 %line_scatter.8 = f32[128,1024]{1,0:T(8,128)} custom-call(bf16[512,1024]{1,0:T(8,128)(2,1)} %convolution_convert_fusion.10.in_ref), custom_call_target="tpu_custom_call" | custom-call | tf_op jit(solution)/shard_map/line_scatter/pallas_call | solution.py:254
  114.3 21.1 %line_gather.9.whole_ref = bf16[512,1024]{1,0:T(8,128)(2,1)} custom-call(bf16[128,1024]{1,0:T(8,128)(2,1)} %multiply_convert_fusion.12.in_ref), custom_call_target="tpu_custom_call" | custom-call | tf_op jit(solution)/shard_map/line_gather/pallas_call | solution.py:169
  138.3 1.5 convolution_convert_fusion.16.position_ref
  141.3 10.3 %attention_forward.1 = (bf16[512,1024]{1,0:T(8,128)(2,1)}, f32[2,512,512]{2,1,0:T(8,128)}, bf16[512,256]{1,0:T(8,128)(2,1)}, bf16[512,256]{1,0:T(8,128)(2,1)}, b...) custom-call(s32[1]{0:T(128)} %dynamic_slice.16.length_ref, ...), custom_call_target="tpu_custom_call" | custom-call | tf_op jit(solution)/shard_map/attention_forward/pallas_call | solution.py:640
  151.6 22.2 %line_scatter.9 = f32[128,1024]{1,0:T(8,128)} custom-call(bf16[512,1024]{1,0:T(8,128)(2,1)} %get-tuple-element.46.in_ref), custom_call_target="tpu_custom_call" | custom-call | tf_op jit(solution)/shard_map/line_scatter/pallas_call | solution.py:254
  176.1 20.3 %line_gather.10 = bf16[512,1024]{1,0:T(8,128)(2,1)} custom-call(bf16[128,1024]{1,0:T(8,128)(2,1)} %multiply_convert_fusion.11.in_ref), custom_call_target="tpu_custom_call" | custom-call | tf_op jit(solution)/shard_map/line_gather/pallas_call | solution.py:169
  196.4 1.9 fusion.73
  199.5 5.9 all_total.5
  206.2 2.6 convolution_convert_fusion.9.in_ref
  208.8 23.4 %line_scatter.10 = f32[128,1024]{1,0:T(8,128)} custom-call(bf16[512,1024]{1,0:T(8,128)(2,1)} %convolution_convert_fusion.9.in_ref), custom_call_target="tpu_custom_call" | custom-call | tf_op jit(solution)/shard_map/line_scatter/pallas_call | solution.py:254
  234.4 21.0 %line_gather.11 = bf16[512,1024]{1,0:T(8,128)(2,1)} custom-call(bf16[128,1024]{1,0:T(8,128)(2,1)} %multiply_convert_fusion.9.in_ref), custom_call_target="tpu_custom_call" | custom-call | tf_op jit(solution)/shard_map/line_gather/pallas_call | solution.py:169
  255.4 4.5 fusion.74
  260.0 4.6 convolution_convert_fusion.8.in_ref
  264.5 23.6 %line_scatter.11 = f32[128,1024]{1,0:T(8,128)} custom-call(bf16[512,1024]{1,0:T(8,128)(2,1)} %convolution_convert_fusion.8.in_ref), custom_call_target="tpu_custom_call" | custom-call | tf_op jit(solution)/shard_map/line_scatter/pallas_call | solution.py:254
  292.5 20.6 %line_gather.12 = bf16[512,1024]{1,0:T(8,128)(2,1)} custom-call(bf16[128,1024]{1,0:T(8,128)(2,1)} %multiply_convert_fusion.7.in_ref), custom_call_target="tpu_custom_call" | custom-call | tf_op jit(solution)/shard_map/line_gather/pallas_call | solution.py:169
  313.2 4.7 convolution_convert_fusion.2.refs_1_
  317.9 1.6 multiply_convert_fusion.1
  319.6 2.6 convolution_convert_fusion.3.refs_0_
  322.2 2.3 convolution_convert_fusion.7.in_ref
  324.5 21.2 %line_scatter.12 = f32[128,1024]{1,0:T(8,128)} custom-call(bf16[512,1024]{1,0:T(8,128)(2,1)} %convolution_convert_fusion.7.in_ref), custom_call_target="tpu_custom_call" | custom-call | tf_op jit(solution)/shard_map/line_scatter/pallas_call | solution.py:254
  349.3 19.4 %line_gather.13 = bf16[512,1024]{1,0:T(8,128)(2,1)} custom-call(bf16[128,1024]{1,0:T(8,128)(2,1)} %get-tuple-element.145.in_ref), custom_call_target="tpu_custom_call" | custom-call | tf_op jit(solution)/shard_map/line_gather/pallas_call | solution.py:169
  368.6 3.0 fusion.57
  373.6 5.9 all_total.6
  380.1 1.7 multiply_reduce_fusion
  383.0 1.7 convolution_convert_fusion.11.refs_2_
  384.8 1.8 convolution_convert_fusion.12.in_ref
  387.1 22.8 %line_scatter.13 = f32[128,1024]{1,0:T(8,128)} custom-call(bf16[512,1024]{1,0:T(8,128)(2,1)} %convolution_convert_fusion.12.in_ref), custom_call_target="tpu_custom_call" | custom-call | tf_op jit(solution)/shard_map/line_scatter/pallas_call | solution.py:254
  413.4 21.6 %line_gather.14.grad_ref = bf16[512,1024]{1,0:T(8,128)(2,1)} custom-call(bf16[128,1024]{1,0:T(8,128)(2,1)} %fusion.24.in_ref), custom_call_target="tpu_custom_call" | custom-call | tf_op jit(solution)/shard_map/line_gather/pallas_call | solution.py:169
  435.0 12.6 %attention_backward.1 = (bf16[512,768]{1,0:T(8,128)(2,1)}, bf16[1024,256]{1,0:T(8,128)(2,1)}, f32[2,256]{1,0:T(2,128)}) custom-call(bf16[512,1024]{1,0:T(8,128)(2,1)} %line_gather.14.grad_ref, bf16[256,1024]{1,0:T(8,128)(2,1)} %get-tuple-element.45.out_w_ref, f32[2,512,512]{2,1,0:T(8,128)} %get-tuple-element.48.probs_ref, ...), custom_call_target="tpu_custom_call" | custom-call | tf_op jit(solution)/shard_map/attention_backward/pallas_call | solution.py:719
  448.9 6.1 all_total.9
  456.9 3.5 convolution_convert_fusion.4.refs_4_
  460.4 2.0 convolution_convert_fusion.5.in_ref
  462.4 21.9 %line_scatter.14 = f32[128,1024]{1,0:T(8,128)} custom-call(bf16[512,1024]{1,0:T(8,128)(2,1)} %convolution_convert_fusion.5.in_ref), custom_call_target="tpu_custom_call" | custom-call | tf_op jit(solution)/shard_map/line_scatter/pallas_call | solution.py:254
  487.9 21.2 %line_gather.15 = bf16[512,1024]{1,0:T(8,128)(2,1)} custom-call(bf16[128,1024]{1,0:T(8,128)(2,1)} %get-tuple-element.134.in_ref), custom_call_target="tpu_custom_call" | custom-call | tf_op jit(solution)/shard_map/line_gather/pallas_call | solution.py:169
  509.1 4.3 multiply_convert_fusion
  513.4 2.6 convolution_convert_fusion.refs_8_
  516.1 2.3 convolution_convert_fusion.6.in_ref
  518.4 2.7 convolution_convert_fusion.1.refs_7_
  522.3 1.6 convolution_convert_fusion.15.refs_6_
  523.9 24.3 %line_scatter.15 = f32[128,1024]{1,0:T(8,128)} custom-call(bf16[512,1024]{1,0:T(8,128)(2,1)} %convolution_convert_fusion.6.in_ref), custom_call_target="tpu_custom_call" | custom-call | tf_op jit(solution)/shard_map/line_scatter/pallas_call | solution.py:254
  548.2 65.8 %cube_scatter.1 = (f32[128,1024]{1,0:T(8,128)}, f32[1024,128]{1,0:T(8,128)}, f32[128,512]{1,0:T(8,128)}, f32[256,128]{1,0:T(8,128)}, f32[128,768]{1,0:T(8,128)},...) custom-call(bf16[1024,1024]{1,0:T(8,128)(2,1)} %convolution_convert_fusion.3.refs_0_, ...), custom_call_target="tpu_custom_call" | custom-call | tf_op jit(solution)/shard_map/cube_scatter/pallas_call | solution.py:446
  615.3 7.0 %all_total.7.in_ref = f32[5,1024]{1,0:T(8,128)} custom-call(f32[5,1024]{1,0:T(8,128)} %stack.47.in_ref), custom_call_target="tpu_custom_call" | custom-call | tf_op jit(solution)/shard_map/all_total/pallas_call | solution.py:485
  622.2 7.5 %all_total.8 = f32[5,1024]{1,0:T(8,128)} custom-call(f32[5,1024]{1,0:T(8,128)} %all_total.7.in_ref), custom_call_target="tpu_custom_call" | custom-call | tf_op jit(solution)/shard_map/all_total/pallas_call | solution.py:485
  629.7 1.8 reshape.440
  (201 shorter events, 58.2 us)
Async XLA Ops:
  7.2 45.3 %copy-start.39 = (s32[8]{0:T(128)S(1)}, s32[8]{0:T(128)}, u32[]{:S(2)}) copy-start(s32[8]{0:T(128)} %param.18) | copy-start | bytes 100
  7.2 47.1 %copy-start = (bf16[1,128,1024]{2,1,0:T(8,128)(2,1)S(1)}, bf16[1,128,1024]{2,1,0:T(8,128)(2,1)}, u32[]{:S(2)}) copy-start(bf16[1,128,1024]{2,1,0:T(8,128)(2,1)} %param.17) | copy-start | bytes 786436
  7.2 48.1 %copy-start.30 = (f32[5,1024]{1,0:T(8,128)S(1)}, f32[5,1024]{1,0:T(8,128)}, u32[]{:S(2)}) copy-start(f32[5,1024]{1,0:T(8,128)} %param.20) | copy-start | bytes 61444
  7.2 132.6 %all-gather.7.cloned.1.call-start = ((), (), s32[]{:S(2)}) async-start(), calls=%async_computation.1 | async-start | bytes 1179648 | tf_op jit(solution)/shard_map/all_gather | solution.py:870
  7.9 133.4 %all-gather.5.cloned.1.call-start = ((), (), s32[]{:S(2)}) async-start(), calls=%async_computation | async-start | bytes 1769472 | tf_op jit(solution)/shard_map/all_gather | solution.py:862
  9.9 245.5 %all-gather.9.cloned.1.call-start = ((), (), s32[]{:S(2)}) async-start(), calls=%async_computation.2 | async-start | bytes 2359296 | tf_op jit(solution)/shard_map/all_gather | solution.py:877
  10.7 249.3 %all-gather.11.cloned.1.call-start = ((), (), s32[]{:S(2)}) async-start(), calls=%async_computation.3 | async-start | bytes 2359296 | tf_op jit(solution)/shard_map/all_gather | solution.py:878
  51.3 31.6 %copy-start.31 = (bf16[1024,1024]{1,0:T(8,128)(2,1)S(1)}, bf16[1024,1024]{1,0:T(8,128)(2,1)}, u32[]{:S(2)}) copy-start(bf16[1024,1024]{1,0:T(8,128)(2,1)} %get-tuple-element.41) | copy-start | bytes 6291460
  83.0 4.0 copy-start.33
  85.6 1.3 copy-start.40
  114.3 24.1 %copy-start.37 = (bf16[1024,256]{1,0:T(8,128)(2,1)S(1)}, bf16[1024,256]{1,0:T(8,128)(2,1)}, u32[]{:S(2)}) copy-start(bf16[1024,256]{1,0:T(8,128)(2,1)} %get-tuple-element.44) | copy-start | bytes 1572868
  137.0 1.3 copy-start.8
  141.3 55.1 %copy-start.17 = (bf16[128,8,2,256]{3,1,2,0:T(8,128)(2,1)}, bf16[128,8,2,256]{3,1,2,0:T(8,128)(2,1)S(1)}, u32[]{:S(2)}) copy-start(bf16[128,8,2,256]{3,1,2,0:T(8,128)(2,1)S(1)} %copy.47) | copy-start | bytes 3145732
  198.9 9.9 %copy-start.6 = (f32[512,256]{1,0:T(8,128)}, f32[512,256]{1,0:T(8,128)S(1)}, u32[]{:S(2)}) copy-start(f32[512,256]{1,0:T(8,128)S(1)} %get-tuple-element.155) | copy-start | bytes 1572868
  288.2 1.5 copy-start.19
  290.9 0.8 copy-start.3
  313.1 4.8 copy-start.15
  313.1 4.8 copy-start.35
  313.1 4.7 copy-start.42
  317.9 1.7 copy-start.13
  319.6 2.6 copy-start.34
  345.7 2.7 copy-start.4
  368.6 3.0 copy-start.7
  368.6 3.0 copy-start.14
  381.8 1.2 copy-start.12
  382.4 2.4 copy-start.18
  435.0 21.9 %copy-start.5 = (bf16[512,1024]{1,0:T(8,128)(2,1)S(1)}, bf16[512,1024]{1,0:T(8,128)(2,1)}, u32[]{:S(2)}) copy-start(bf16[512,1024]{1,0:T(8,128)(2,1)} %line_gather.9.whole_ref) | copy-start | bytes 3145732
  456.9 3.5 copy-start.10
  456.9 3.5 copy-start.36
  509.1 4.3 copy-start.16
  509.1 4.3 copy-start.41
  513.4 2.6 copy-start.32
  516.1 2.3 copy-start.11
  518.4 2.7 copy-start.1
  518.4 2.7 copy-start.25
  518.4 3.9 copy-start.9
  518.4 3.9 copy-start.38
  548.2 65.8 %copy-start.2 = (f32[128,1024]{1,0:T(8,128)S(1)}, f32[128,1024]{1,0:T(8,128)}, u32[]{:S(2)}) copy-start(f32[128,1024]{1,0:T(8,128)} %line_scatter.15) | copy-start | bytes 1572868
  614.0 17.6 %copy-start.24 = (f32[128,768]{1,0:T(8,128)S(1)}, f32[128,768]{1,0:T(8,128)}, u32[]{:S(2)}) copy-start(f32[128,768]{1,0:T(8,128)} %get-tuple-element.58) | copy-start | bytes 1179652
  614.6 19.7 %copy-start.23 = (f32[128,1024]{1,0:T(8,128)S(1)}, f32[128,1024]{1,0:T(8,128)}, u32[]{:S(2)}) copy-start(f32[128,1024]{1,0:T(8,128)} %get-tuple-element.203) | copy-start | bytes 1572868
  629.7 4.0 copy-start.29
  631.6 3.6 copy-start.22
  632.6 3.3 copy-start.28
  632.6 3.9 copy-start.27
  632.6 4.6 copy-start.26
  632.6 5.2 copy-start.21
  633.7 5.0 copy-start.20
Sparse Core Ops, SparseCore 0:
  9.9 30.4 all-gather.6
  42.9 25.5 all-gather.4
  70.4 27.7 all-gather.8
  99.9 28.0 all-gather.10

commit v4 on v3

v4 whole, which is shorter than its diff:
```python
import functools
import math

import jax
import jax.numpy as jnp
from jax import lax
from jax.experimental import pallas as pl
from jax.experimental.pallas import tpu as pltpu
from jax.sharding import PartitionSpec as P

HEAD = 128


norm_eps = 1e-05
batch_eps = 1e-05
masked_score = -1000000000.0


def matmul(left, right):
    return jnp.dot(left, right, preferred_element_type=jnp.float32)


def contract_rows(left, right):
    return lax.dot_general(
        left, right, (((0,), (0,)), ((), ())), preferred_element_type=jnp.float32
    )


def contract_cols(left, right):
    return lax.dot_general(
        left, right, (((1,), (1,)), ((), ())), preferred_element_type=jnp.float32
    )


def layer_norm(values, norm_gain):
    average = jnp.mean(values, axis=-1, keepdims=True)
    centred = values - average
    inv_std = lax.rsqrt(jnp.mean(centred * centred, axis=-1, keepdims=True) + norm_eps)
    return centred * inv_std * norm_gain


def silu_slope(values):
    logistic = jax.nn.sigmoid(values)
    return logistic * (1.0 + values * (1.0 - logistic))


def position_table(seq_len, model_width):
    fine = 32
    lane = jnp.arange(model_width)
    frequency = jnp.exp((lane // 2).astype(jnp.float32) * (-2.0 * math.log(10000.0) / model_width))
    coarse = (seq_len - 1 - fine * jnp.arange(2 * seq_len // fine)).astype(jnp.float32)
    wide = coarse[:, None] * frequency[None, :]
    small = -jnp.arange(fine).astype(jnp.float32)[:, None] * frequency[None, :]
    even = (lane % 2 == 0)[None, :]
    wide_sin, wide_cos = jnp.sin(wide), jnp.cos(wide)
    high = jnp.where(even, wide_sin, wide_cos)
    side = jnp.where(even, wide_cos, -wide_sin)
    table = high[:, None, :] * jnp.cos(small)[None] + side[:, None, :] * jnp.sin(small)[None]
    return table.reshape(2 * seq_len, model_width)


MESH = pl.DeviceIdType.MESH
VMEM_LIMIT = 60 * 1024 * 1024


def line_copy(src, dst, sems, index, axis, target):
    return pltpu.make_async_remote_copy(
        src_ref=src,
        dst_ref=dst,
        send_sem=sems.at[0, index],
        recv_sem=sems.at[1, index],
        device_id={axis: target},
        device_id_type=MESH,
    )


def bit_of(index, bit):
    return lax.rem(lax.div(index, bit), 2)


def partner(index, bit):
    return index + bit - 2 * bit * bit_of(index, bit)


def cube_bits(size, swap):
    bits = []
    bit = 2
    while bit < size:
        bits.append(bit)
        bit *= 2
    if swap:
        bits.reverse()
    return bits + [1]


def block_at(ref, dim, index, width):
    start = pl.multiple_of(index * width, width)
    return ref.at[pl.ds(start, width)] if dim == 0 else ref.at[:, pl.ds(start, width)]


def all_total_kernel(axis, in_ref, out_ref, slots, sems):
    size = lax.axis_size(axis)
    me = lax.axis_index(axis)
    barrier = pltpu.get_barrier_semaphore()
    targets = [lax.rem(me + step, size) for step in range(1, size)]
    for target in targets:
        pl.semaphore_signal(barrier, inc=1, device_id={axis: target}, device_id_type=MESH)
    pl.semaphore_wait(barrier, size - 1)
    copies = []
    for number, target in enumerate(targets):
        copy = line_copy(in_ref, slots.at[me], sems, number, axis, target)
        copy.start()
        copies.append(copy)
    slots[me] = in_ref[...]
    for copy in copies:
        copy.wait_recv()
    total = slots[0]
    for source in range(1, size):
        total = total + slots[source]
    out_ref[...] = total
    for copy in copies:
        copy.wait_send()


def all_total(values, axis, collective_id):
    size = lax.axis_size(axis)
    return pl.pallas_call(
        functools.partial(all_total_kernel, axis),
        out_shape=jax.ShapeDtypeStruct(values.shape, values.dtype),
        in_specs=[pl.BlockSpec(memory_space=pltpu.VMEM)],
        out_specs=pl.BlockSpec(memory_space=pltpu.VMEM),
        scratch_shapes=[
            pltpu.VMEM((size, *values.shape), values.dtype),
            pltpu.SemaphoreType.DMA((2, size - 1)),
        ],
        compiler_params=pltpu.CompilerParams(
            collective_id=collective_id, has_side_effects=True
        ),
        name="all_total",
    )(values)


def line_peers(axis):
    me, size = lax.axis_index(axis), lax.axis_size(axis)
    return jnp.minimum(me, 1) + jnp.minimum(size - 1 - me, 1)


def greet(line_axis, cube_axis, everyone):
    me, size = lax.axis_index(line_axis), lax.axis_size(line_axis)
    barrier = pltpu.get_barrier_semaphore()
    if everyone:
        for axis in (line_axis, cube_axis):
            here, count = lax.axis_index(axis), lax.axis_size(axis)
            for step in range(1, count):
                pl.semaphore_signal(
                    barrier, inc=1, device_id={axis: lax.rem(here + step, count)},
                    device_id_type=MESH,
                )
        pl.semaphore_wait(barrier, size - 1 + lax.axis_size(cube_axis) - 1)
        return

    @pl.when(me > 0)
    def _():
        pl.semaphore_signal(barrier, inc=1, device_id={line_axis: me - 1}, device_id_type=MESH)

    @pl.when(me < size - 1)
    def _():
        pl.semaphore_signal(barrier, inc=1, device_id={line_axis: me + 1}, device_id_type=MESH)

    bits = cube_bits(lax.axis_size(cube_axis), False) if cube_axis else []
    for bit in bits:
        pl.semaphore_signal(
            barrier, inc=1, device_id={cube_axis: partner(lax.axis_index(cube_axis), bit)},
            device_id_type=MESH,
        )
    pl.semaphore_wait(barrier, line_peers(line_axis) + len(bits))


class LineGather:
    def __init__(self, axis, out_ref, sems):
        self.axis, self.out, self.sems = axis, out_ref, sems
        self.size, self.me = lax.axis_size(axis), lax.axis_index(axis)
        self.rows = out_ref.shape[0] // self.size
        self.steps = self.size - 1

    def piece(self, index):
        return self.out.at[pl.ds(pl.multiple_of(index * self.rows, self.rows), self.rows)]

    def copy(self, way, step, index):
        return line_copy(
            self.piece(index), self.piece(index), self.sems, way * self.steps + step, self.axis,
            self.me + 1 if way == 0 else self.me - 1,
        )

    def index(self, way, step):
        return self.me - step if way == 0 else self.me + step

    def held(self, way, step):
        return self.me >= step if way == 0 else self.me + step < self.size

    def onward(self, way):
        return self.me + 1 < self.size if way == 0 else self.me > 0

    def step(self, step):
        for way in range(2):
            if step > 0:
                @pl.when(self.held(way, step))
                def _():
                    self.copy(way, step - 1, self.index(way, step)).wait_recv()

            if step < self.steps:
                @pl.when(jnp.logical_and(self.held(way, step), self.onward(way)))
                def _():
                    self.copy(way, step, self.index(way, step)).start()

    def finish(self):
        for step in range(self.steps):
            for way in range(2):
                @pl.when(jnp.logical_and(self.held(way, step), self.onward(way)))
                def _():
                    self.copy(way, step, self.index(way, step)).wait_send()


class LineScatter:
    def __init__(self, axis, in_ref, total_ref, slots, staged, sems):
        self.axis, self.ins, self.total = axis, in_ref, total_ref
        self.slots, self.staged, self.sems = slots, staged, sems
        self.size, self.me = lax.axis_size(axis), lax.axis_index(axis)
        self.rows = total_ref.shape[0]
        self.first_way = lax.div(self.me, (self.size + 1) // 2)

    def mine(self, owner):
        return self.ins.at[pl.ds(pl.multiple_of(owner * self.rows, self.rows), self.rows)]

    def copy(self, way, owner, src):
        return line_copy(
            src, self.slots.at[way, owner], self.sems, way * self.size + owner, self.axis,
            self.me + 1 - 2 * way,
        )

    def hop(self, way, step):
        owner = (1 - way) * (self.size - 1 - step) + way * step
        distance = (owner - self.me) * (1 - 2 * way)
        behind = (1 - way) * self.me + way * (self.size - 1 - self.me)

        @pl.when(jnp.logical_and(distance > 0, behind == 0))
        def _():
            self.copy(way, owner, self.mine(owner)).start()

        @pl.when(jnp.logical_and(distance > 0, behind > 0))
        def _():
            self.copy(way, owner, self.staged.at[way, owner]).wait_recv()
            self.staged[way, owner] = (
                self.mine(owner)[...].astype(jnp.float32)
                + self.slots[way, owner].astype(jnp.float32)
            ).astype(self.staged.dtype)
            self.copy(way, owner, self.staged.at[way, owner]).start()

    def step(self, step):
        self.hop(self.first_way, step)
        self.hop(1 - self.first_way, step)

    def result(self):
        self.total[...] = self.mine(self.me)[...].astype(jnp.float32)
        for way in range(2):
            @pl.when(self.me > 0 if way == 0 else self.me < self.size - 1)
            def _():
                self.copy(way, self.me, self.staged.at[way, self.me]).wait_recv()
                self.total[...] += self.slots[way, self.me].astype(jnp.float32)

        return self.total[...]

    def finish(self):
        for owner in range(self.size):
            for way in range(2):
                @pl.when(self.me < owner if way == 0 else self.me > owner)
                def _():
                    self.copy(way, owner, self.staged.at[way, owner]).wait_send()


class CubeGather:
    def __init__(self, axis, dims, ways, ins, outs, sems):
        self.axis, self.dims, self.ways = axis, dims, ways
        self.ins, self.outs, self.sems = ins, outs, sems
        self.size, self.me = lax.axis_size(axis), lax.axis_index(axis)
        self.stages = len(cube_bits(self.size, False))
        self.started = []
        self.waiting = [[] for _ in ins]

    def step(self, stage):
        per = self.size - 1
        for which in range(len(self.ins)):
            width = self.ins[which].shape[self.dims[which]]
            bits = cube_bits(self.size, self.ways[which])
            for copy in self.waiting[which]:
                copy.wait_recv()
            self.waiting[which] = []
            if stage == 0:
                block_at(self.outs[which], self.dims[which], self.me, width)[...] = (
                    self.ins[which][...]
                )
            if stage == self.stages:
                continue
            held = [self.me]
            for bit in bits[:stage]:
                held = held + [partner(index, bit) for index in held]
            for number, index in enumerate(held):
                place = block_at(self.outs[which], self.dims[which], index, width)
                copy = line_copy(
                    self.ins[which] if stage == 0 else place, place, self.sems,
                    which * per + 2**stage - 1 + number, self.axis, partner(self.me, bits[stage]),
                )
                copy.start()
                self.waiting[which].append(copy)
            self.started.extend(self.waiting[which])

    def finish(self):
        for copy in self.started:
            copy.wait_send()


class CubeScatter:
    def __init__(self, axis, dims, ways, ins, outs, slots, sems):
        self.axis, self.dims, self.ways = axis, dims, ways
        self.ins, self.outs, self.slots, self.sems = ins, outs, slots, sems
        self.size, self.me = lax.axis_size(axis), lax.axis_index(axis)
        self.stages = len(cube_bits(self.size, False))
        self.started = []

    def slot(self, which, stage, number):
        return self.slots[which].at[self.size - self.size // 2**stage + number]

    def sets(self, which, stage):
        bits = cube_bits(self.size, self.ways[which])[::-1]
        held = [self.me]
        for bit in bits[stage + 1 :]:
            held = held + [partner(index, bit) for index in held]
        return bits[stage], held

    def send(self, which, stage):
        width = self.outs[which].shape[self.dims[which]]
        bit, held = self.sets(which, stage)
        for number, index in enumerate(held):
            if stage == 0:
                src = block_at(self.ins[which], self.dims[which], partner(index, bit), width)
            else:
                src = self.slot(which, stage - 1, 2 * number + 1)
            copy = line_copy(
                src, self.slot(which, stage, number), self.sems,
                which * (self.size - 1) + self.size - self.size // 2**stage + number,
                self.axis, partner(self.me, bit),
            )
            copy.start()
            self.started.append((which, stage, copy))

    def receive(self, which, stage):
        width = self.outs[which].shape[self.dims[which]]
        _, held = self.sets(which, stage)
        for copy in [c for w, s, c in self.started if (w, s) == (which, stage)]:
            copy.wait_recv()
        for number, index in enumerate(held):
            got = self.slot(which, stage, number)
            if stage == 0:
                mine = block_at(self.ins[which], self.dims[which], index, width)
            else:
                mine = self.slot(which, stage - 1, 2 * number)
            total = got[...].astype(jnp.float32) + mine[...].astype(jnp.float32)
            if stage == self.stages - 1:
                self.outs[which][...] = total
            else:
                got[...] = total.astype(self.slots[which].dtype)

    def step(self, stage):
        for which in range(len(self.ins)):
            if stage > 0:
                self.receive(which, stage - 1)
            if stage < self.stages:
                self.send(which, stage)

    def finish(self):
        for _, _, copy in self.started:
            copy.wait_send()


class AllTotal:
    def __init__(self, axis, slots, sems):
        self.axis, self.slots, self.sems = axis, slots, sems
        self.size, self.me = lax.axis_size(axis), lax.axis_index(axis)
        self.copies = []

    def start(self):
        for step in range(1, self.size):
            copy = line_copy(
                self.slots.at[self.me], self.slots.at[self.me], self.sems, step - 1, self.axis,
                lax.rem(self.me + step, self.size),
            )
            copy.start()
            self.copies.append(copy)

    def result(self):
        for copy in self.copies:
            copy.wait_recv()
        total = self.slots[0]
        for source in range(1, self.size):
            total = total + self.slots[source]
        return total

    def finish(self):
        for copy in self.copies:
            copy.wait_send()


def open_kernel(middle, counts, dims, ways, *refs):
    local_count, mid_count = counts
    count = len(dims)
    refs = list(refs)
    take = lambda number: [refs.pop(0) for _ in range(number)]
    locals_, ins = take(local_count), take(count)
    mids, (whole,), outs = take(mid_count), take(1), take(count)
    gather_sems, cube_sems = refs
    fetch = CubeGather("dp", dims, ways, ins, outs, cube_sems)
    rows = LineGather("mp", whole, gather_sems)
    greet("mp", "dp", False)
    fetch.step(0)
    values, normed = middle(None, *[ref[...] for ref in locals_])
    for ref, value in zip(mids, values):
        ref[...] = value
    rows.piece(rows.me)[...] = normed
    rows.step(0)
    fetch.step(1)
    rows.step(1)
    fetch.step(2)
    for step in range(3, fetch.stages + 1):
        fetch.step(step)
        if step <= rows.steps + 1:
            rows.step(step - 1)
    for step in range(max(2, fetch.stages), rows.steps + 1):
        rows.step(step)
    rows.finish()
    fetch.finish()


def between_kernel(middle, counts, gathers, dims, ways, *refs):
    local_count, mid_count = counts
    count = len(dims)
    refs = list(refs)
    take = lambda number: [refs.pop(0) for _ in range(number)]
    (partial,), locals_, ins = take(1), take(local_count), take(count)
    mids, (whole,), outs = take(mid_count), take(1), take(count)
    (total, slots, staged, scatter_sems, gather_sems), refs = refs[:5], refs[5:]
    sums = LineScatter("mp", partial, total, slots, staged, scatter_sems)
    rows = LineGather("mp", whole, gather_sems)
    grads = CubeScatter("dp", dims, ways, ins, outs, refs[:count], refs[count]) if count else None
    greet("mp", "dp" if count else None, False)
    stage = 0
    for step in range(sums.size - 1):
        sums.step(step)
        if count and step in (0, 2):
            grads.step(stage)
            stage += 1
    values, normed = middle(sums.result(), *[ref[...] for ref in locals_])
    rows.piece(rows.me)[...] = normed
    rows.step(0)
    for ref, value in zip(mids, values):
        ref[...] = value
    for step in range(1, rows.steps + 1):
        if count and stage <= grads.stages:
            grads.step(stage)
            stage += 1
        rows.step(step)
    if count:
        for stage in range(stage, grads.stages + 1):
            grads.step(stage)
        grads.finish()
    sums.finish()
    rows.finish()


def close_kernel(middle, counts, dims, ways, *refs):
    local_count, mid_count = counts
    count = len(dims)
    refs = list(refs)
    take = lambda number: [refs.pop(0) for _ in range(number)]
    (partial, small, gains), locals_, ins = take(3), take(local_count), take(count)
    mids, (small_out, gains_out), outs = take(mid_count), take(2), take(count)
    (total, slots, staged, scatter_sems), refs = refs[:4], refs[4:]
    (small_slots, small_sems, gain_slots, gain_sems, last_slots, last_sems), refs = refs[:6], refs[6:]
    sums = LineScatter("mp", partial, total, slots, staged, scatter_sems)
    grads = CubeScatter("dp", dims, ways, ins, outs, refs[:count], refs[count])
    little = AllTotal("dp", small_slots, small_sems)
    near, far = AllTotal("dp", gain_slots, gain_sems), AllTotal("mp", last_slots, last_sems)
    little.slots[little.me] = small[...]
    greet("mp", "dp", True)
    little.start()
    stage = 0
    for step in range(sums.size - 1):
        sums.step(step)
        if step != 1:
            grads.step(stage)
            stage += 1
    values, gain = middle(sums.result(), *[ref[...] for ref in locals_])
    near.slots[near.me] = jnp.concatenate([gains[...], gain], axis=0)
    near.start()
    for ref, value in zip(mids, values):
        ref[...] = value
    grads.step(stage)
    far.slots[far.me] = near.result()
    far.start()
    for stage in range(stage + 1, grads.stages + 1):
        grads.step(stage)
    small_out[...] = little.result()
    gains_out[...] = far.result()
    for task in (grads, sums, little, near, far):
        task.finish()


def shapes_of(arrays):
    return [jax.ShapeDtypeStruct(value.shape, value.dtype) for value in arrays]


def call_step(kernel, inputs, out_shape, scratch, collective_id, name):
    vmem = pl.BlockSpec(memory_space=pltpu.VMEM)
    return pl.pallas_call(
        kernel,
        out_shape=out_shape,
        in_specs=[vmem] * len(inputs),
        out_specs=[vmem] * len(out_shape),
        scratch_shapes=scratch,
        compiler_params=pltpu.CompilerParams(
            collective_id=collective_id, has_side_effects=True, vmem_limit_bytes=VMEM_LIMIT
        ),
        name=name,
    )(*inputs)


def line_scratch(rows, width):
    size = lax.axis_size("mp")
    return [
        pltpu.VMEM((rows, width), jnp.float32),
        pltpu.VMEM((2, size, rows, width), jnp.bfloat16),
        pltpu.VMEM((2, size, rows, width), jnp.bfloat16),
        pltpu.SemaphoreType.DMA((2, 2 * size)),
    ]


def cube_scratch(arrays, dims):
    size = lax.axis_size("dp")
    shapes, slots = [], []
    for array, dim in zip(arrays, dims):
        shape = list(array.shape)
        shape[dim] //= size
        shapes.append(jax.ShapeDtypeStruct(tuple(shape), jnp.float32))
        slots.append(pltpu.VMEM((size - 1, *shape), array.dtype))
    if arrays:
        slots.append(pltpu.SemaphoreType.DMA((2, len(arrays) * (size - 1))))
    return shapes, slots


def plain_totals(grads, dims):
    return [
        lax.psum_scatter(grad, "dp", scatter_dimension=dim, tiled=True).astype(jnp.float32)
        for grad, dim in zip(grads, dims)
    ]


def direct(block):
    size = lax.axis_size("dp")
    return size & (size - 1) == 0 and block % 128 == 0


def open_step(middle, locals_, arrays, dims, small, collective_id):
    if not direct(arrays[0].shape[dims[0]]):
        mids, normed = middle(None, *locals_)
        whole = [
            lax.all_gather(array, "dp", axis=dim, tiled=True) for array, dim in zip(arrays, dims)
        ]
        return (
            mids,
            lax.all_gather(normed, "mp", axis=0, tiled=True),
            whole,
            lax.all_gather(small, "dp", axis=1, tiled=True),
        )
    size, lanes = lax.axis_size("dp"), small.shape[1]
    arrays = [*arrays, jnp.pad(small, ((0, 16 - small.shape[0]), (0, 128 - lanes)))]
    dims = (*dims, 0)
    ways = [index % 2 == 1 for index in range(len(dims))]
    mid_shapes, normed_shape = jax.eval_shape(functools.partial(middle, None), *locals_)
    outs = []
    for array, dim in zip(arrays, dims):
        shape = list(array.shape)
        shape[dim] *= size
        outs.append(jax.ShapeDtypeStruct(tuple(shape), array.dtype))
    rows, width = normed_shape.shape
    whole_shape = jax.ShapeDtypeStruct((rows * lax.axis_size("mp"), width), normed_shape.dtype)
    result = call_step(
        functools.partial(open_kernel, middle, (len(locals_), len(mid_shapes)), dims, ways),
        [*locals_, *arrays],
        [*mid_shapes, whole_shape, *outs],
        [
            pltpu.SemaphoreType.DMA((2, 2 * (lax.axis_size("mp") - 1))),
            pltpu.SemaphoreType.DMA((2, len(arrays) * (size - 1))),
        ],
        collective_id,
        "open_step",
    )
    mids, (whole, *fetched, packed) = result[: len(mid_shapes)], result[len(mid_shapes) :]
    packed = packed.reshape(size, 16, 128)[:, : small.shape[0], :lanes]
    return mids, whole, fetched, packed.transpose(1, 0, 2).reshape(small.shape[0], size * lanes)


def between_step(middle, partial_value, locals_, grads, dims, ways, collective_id):
    partial_value = partial_value.astype(jnp.bfloat16)
    grads = [grad.astype(jnp.bfloat16) for grad in grads]
    size = lax.axis_size("mp")
    rows, width = partial_value.shape[0] // size, partial_value.shape[1]
    if not direct(width // lax.axis_size("dp")):
        total = lax.psum_scatter(partial_value, "mp", scatter_dimension=0, tiled=True)
        mids, normed = middle(total.astype(jnp.float32), *locals_)
        return mids, lax.all_gather(normed, "mp", axis=0, tiled=True), plain_totals(grads, dims)
    total = jax.ShapeDtypeStruct((rows, width), jnp.float32)
    mid_shapes, normed_shape = jax.eval_shape(middle, total, *locals_)
    shapes, slots = cube_scratch(grads, dims)
    count = len(mid_shapes)
    result = call_step(
        functools.partial(between_kernel, middle, (len(locals_), count), True, dims, ways),
        [partial_value, *locals_, *grads],
        [
            *mid_shapes,
            jax.ShapeDtypeStruct((rows * size, width), normed_shape.dtype),
            *shapes,
        ],
        line_scratch(rows, width) + [pltpu.SemaphoreType.DMA((2, 2 * (size - 1)))] + slots,
        collective_id,
        "between_step",
    )
    return result[:count], result[count], result[count + 1 :]


def close_step(middle, partial_value, small, gains, locals_, grads, dims, ways, collective_id):
    partial_value = partial_value.astype(jnp.bfloat16)
    grads = [grad.astype(jnp.bfloat16) for grad in grads]
    size, dp_size = lax.axis_size("mp"), lax.axis_size("dp")
    rows, width = partial_value.shape[0] // size, partial_value.shape[1]
    if not direct(width // dp_size):
        total = lax.psum_scatter(partial_value, "mp", scatter_dimension=0, tiled=True)
        mids, gain = middle(total.astype(jnp.float32), *locals_)
        gains = lax.psum(jnp.concatenate([gains, gain], axis=0), ("dp", "mp"))
        return mids, lax.psum(small, "dp"), gains, plain_totals(grads, dims)
    total = jax.ShapeDtypeStruct((rows, width), jnp.float32)
    mid_shapes, gain_shape = jax.eval_shape(middle, total, *locals_)
    gains_shape = jax.ShapeDtypeStruct((gains.shape[0] + 1, width), jnp.float32)
    shapes, slots = cube_scratch(grads, dims)
    count = len(mid_shapes)
    result = call_step(
        functools.partial(close_kernel, middle, (len(locals_), count), dims, ways),
        [partial_value, small, gains, *locals_, *grads],
        [*mid_shapes, *shapes_of([small]), gains_shape, *shapes],
        line_scratch(rows, width)
        + [
            pltpu.VMEM((dp_size, *small.shape), jnp.float32),
            pltpu.SemaphoreType.DMA((2, dp_size - 1)),
            pltpu.VMEM((dp_size, *gains_shape.shape), jnp.float32),
            pltpu.SemaphoreType.DMA((2, dp_size - 1)),
            pltpu.VMEM((size, *gains_shape.shape), jnp.float32),
            pltpu.SemaphoreType.DMA((2, size - 1)),
        ]
        + slots,
        collective_id,
        "close_step",
    )
    return result[:count], result[count], result[count + 1], result[count + 2 :]


def forward_middle(scale, row, total, residual, norm_gains):
    residual = residual.astype(jnp.float32)
    if total is not None:
        residual = residual + scale * total
    return [residual], layer_norm(residual, norm_gains[row : row + 1]).astype(jnp.bfloat16)


def open_middle(total, frames, norm_gains):
    return [], layer_norm(frames.astype(jnp.float32), norm_gains[0:1]).astype(jnp.bfloat16)


def norm_back(values, norm_gain, upstream):
    centred = values - jnp.mean(values, axis=-1, keepdims=True)
    inv_std = lax.rsqrt(jnp.mean(centred * centred, axis=-1, keepdims=True) + norm_eps)
    normed = centred * inv_std
    scaled = upstream * norm_gain
    d_values = inv_std * (
        scaled
        - jnp.mean(scaled, axis=-1, keepdims=True)
        - normed * jnp.mean(scaled * normed, axis=-1, keepdims=True)
    )
    return d_values, jnp.sum(upstream * normed, axis=0, keepdims=True)


def turn_middle(total, residual, norm_gains, out_grad):
    after = residual + 0.5 * total
    gain = norm_gains[4:5]
    d_after, d_gain = norm_back(after, gain, out_grad.astype(jnp.float32))
    block_out = layer_norm(after, gain).astype(jnp.bfloat16)
    return [block_out, d_after, d_gain], (0.5 * d_after).astype(jnp.bfloat16)


def backward_middle(scale, row, total, values, norm_gains, upstream):
    d_branch, d_gain = norm_back(values.astype(jnp.float32), norm_gains[row : row + 1], total)
    d_values = upstream + d_branch
    return [d_values, d_gain], (scale * d_values).astype(jnp.bfloat16)


def close_middle(total, values, norm_gains, upstream):
    d_branch, d_gain = norm_back(values.astype(jnp.float32), norm_gains[0:1], total)
    return [upstream + d_branch], d_gain


def dp_total(values):
    if direct(128):
        return all_total(values, "dp", 9)
    return lax.psum(values, "dp")


def ffn_forward(whole, weights):
    w_up, w_down = weights
    hidden = matmul(whole, w_up)
    return matmul(jax.nn.silu(hidden).astype(jnp.bfloat16), w_down)


def ffn_backward(whole, weights, grad_whole):
    w_up, w_down = weights
    hidden = matmul(whole, w_up)
    active = jax.nn.silu(hidden).astype(jnp.bfloat16)
    grad_down = contract_rows(active, grad_whole)
    d_hidden = (contract_cols(grad_whole, w_down) * silu_slope(hidden)).astype(jnp.bfloat16)
    grad_up = contract_rows(whole, d_hidden)
    return (contract_cols(d_hidden, w_up), grad_up, grad_down)


def place_position(position_ref, block, rows, seq_len):
    start = pl.multiple_of(seq_len - rows - block * rows, rows)
    return position_ref.at[pl.ds(start, seq_len + rows)]


def attention_kernel(
    scaling, length_ref, whole_ref, in_ref, bias_ref, position_ref, out_w_ref,
    partial_ref, probs_ref, context_ref, query_u_ref, query_v_ref, key_ref, value_ref,
):
    block = pl.program_id(0)
    seq_len, local_width = key_ref.shape
    rows = partial_ref.shape[0]

    @pl.when(block == 0)
    def _():
        projected = matmul(whole_ref[...], in_ref[...])
        queries = projected[:, :local_width]
        query_u_ref[...] = ((queries + bias_ref[0:1]) * scaling).astype(jnp.bfloat16)
        query_v_ref[...] = ((queries + bias_ref[1:2]) * scaling).astype(jnp.bfloat16)
        key_ref[...] = projected[:, local_width : 2 * local_width].astype(jnp.bfloat16)
        value_ref[...] = projected[:, 2 * local_width :].astype(jnp.bfloat16)

    here = pl.ds(pl.multiple_of(block * rows, rows), rows)
    valid = lax.broadcasted_iota(jnp.int32, (rows, seq_len), 1) < length_ref[0]
    nearby = place_position(position_ref, block, rows, seq_len)
    pieces = []
    for head in range(local_width // HEAD):
        lanes = slice(head * HEAD, (head + 1) * HEAD)
        content = contract_cols(query_u_ref[here, lanes], key_ref[:, lanes])
        zeds = contract_cols(query_v_ref[here, lanes], nearby[:, lanes])
        shifted = pltpu.roll(zeds, seq_len + 1, 1, stride=1, stride_axis=0)[:, :seq_len]
        scores = jnp.where(valid, content + shifted, masked_score)
        exponent = jnp.exp(scores - jnp.max(scores, axis=-1, keepdims=True))
        probs = exponent / jnp.sum(exponent, axis=-1, keepdims=True)
        probs_ref[head] = probs
        pieces.append(matmul(probs.astype(jnp.bfloat16), value_ref[:, lanes]).astype(jnp.bfloat16))
    context = jnp.concatenate(pieces, axis=1)
    context_ref[...] = context
    partial_ref[...] = matmul(context, out_w_ref[...]).astype(jnp.bfloat16)


def attention_forward(whole, weights, position, own_length):
    w_in, w_pos, bias_pair, w_out = weights
    seq_len, model_width = whole.shape
    local_width = w_out.shape[0]
    heads_here = local_width // HEAD
    rows = 128
    full = pl.BlockSpec(memory_space=pltpu.VMEM)
    low = jnp.bfloat16
    return pl.pallas_call(
        functools.partial(attention_kernel, HEAD ** (-0.5)),
        grid=(seq_len // rows,),
        out_shape=[
            jax.ShapeDtypeStruct((seq_len, model_width), low),
            jax.ShapeDtypeStruct((heads_here, seq_len, seq_len), jnp.float32),
        ]
        + [jax.ShapeDtypeStruct((seq_len, local_width), low)] * 5,
        in_specs=[pl.BlockSpec(memory_space=pltpu.SMEM)] + [full] * 5,
        out_specs=[
            pl.BlockSpec((rows, model_width), lambda block: (block, 0)),
            pl.BlockSpec((heads_here, rows, seq_len), lambda block: (0, block, 0)),
            pl.BlockSpec((rows, local_width), lambda block: (block, 0)),
        ]
        + [full] * 4,
        compiler_params=pltpu.CompilerParams(vmem_limit_bytes=VMEM_LIMIT),
        name="attention_forward",
    )(own_length, whole, w_in, bias_pair.astype(jnp.float32), position, w_out)


def attention_back_kernel(
    scaling, grad_ref, out_w_ref, probs_ref, query_u_ref, query_v_ref, key_ref, value_ref,
    position_ref, d_projected_ref, d_position_ref, bias_ref, d_keys, d_values, d_places,
):
    block = pl.program_id(0)
    seq_len, local_width = key_ref.shape
    rows = grad_ref.shape[0]

    @pl.when(block == 0)
    def _():
        d_keys[...] = jnp.zeros_like(d_keys)
        d_values[...] = jnp.zeros_like(d_values)
        d_places[...] = jnp.zeros_like(d_places)
        bias_ref[...] = jnp.zeros_like(bias_ref)

    here = pl.ds(pl.multiple_of(block * rows, rows), rows)
    nearby = place_position(position_ref, block, rows, seq_len)
    d_nearby = place_position(d_places, block, rows, seq_len)
    upside = (
        lax.broadcasted_iota(jnp.int32, (rows, rows), 0)
        + lax.broadcasted_iota(jnp.int32, (rows, rows), 1)
        == rows - 1
    ).astype(jnp.bfloat16)
    d_context_all = contract_cols(grad_ref[...], out_w_ref[...]).astype(jnp.bfloat16)
    for head in range(local_width // HEAD):
        lanes = slice(head * HEAD, (head + 1) * HEAD)
        d_context = d_context_all[:, lanes]
        probs = probs_ref[head]
        d_probs = contract_cols(d_context, value_ref[:, lanes])
        inner = jnp.sum(probs * d_probs, axis=-1, keepdims=True)
        d_scores = (probs * (d_probs - inner)).astype(jnp.bfloat16)
        d_values[:, lanes] += contract_rows(probs.astype(jnp.bfloat16), d_context)
        d_keys[:, lanes] += contract_rows(d_scores, query_u_ref[here, lanes])
        grad_u = matmul(d_scores, key_ref[:, lanes]) * scaling
        turned = matmul(upside, d_scores)
        turned = jnp.concatenate([turned, jnp.zeros((rows, rows), jnp.float32)], axis=1)
        turned = pltpu.roll(turned, 0, 1, stride=1, stride_axis=0).astype(jnp.bfloat16)
        d_zeds = matmul(upside, turned).astype(jnp.bfloat16)
        grad_v = matmul(d_zeds, nearby[:, lanes]) * scaling
        d_nearby[:, lanes] += contract_rows(d_zeds, query_v_ref[here, lanes])
        d_projected_ref[here, lanes] = (grad_u + grad_v).astype(jnp.bfloat16)
        bias_ref[0:1, lanes] += jnp.sum(grad_u, axis=0, keepdims=True)
        bias_ref[1:2, lanes] += jnp.sum(grad_v, axis=0, keepdims=True)

    @pl.when(block == pl.num_programs(0) - 1)
    def _():
        d_projected_ref[:, local_width : 2 * local_width] = d_keys[...].astype(jnp.bfloat16)
        d_projected_ref[:, 2 * local_width :] = d_values[...].astype(jnp.bfloat16)
        d_position_ref[...] = d_places[...].astype(jnp.bfloat16)


def attention_backward(whole, weights, table_low, position, saved, grad_whole):
    w_in, w_pos, bias_pair, w_out = weights
    probs, context, query_u, query_v, key_rows, value_rows = saved
    seq_len, model_width = whole.shape
    local_width = w_out.shape[0]
    heads_here = local_width // HEAD
    rows = 128
    full = pl.BlockSpec(memory_space=pltpu.VMEM)
    d_projected, d_position, grad_bias = pl.pallas_call(
        functools.partial(attention_back_kernel, HEAD ** (-0.5)),
        grid=(seq_len // rows,),
        out_shape=[
            jax.ShapeDtypeStruct((seq_len, 3 * local_width), jnp.bfloat16),
            jax.ShapeDtypeStruct((2 * seq_len, local_width), jnp.bfloat16),
            jax.ShapeDtypeStruct((2, local_width), jnp.float32),
        ],
        in_specs=[
            pl.BlockSpec((rows, model_width), lambda block: (block, 0)),
            full,
            pl.BlockSpec((heads_here, rows, seq_len), lambda block: (0, block, 0)),
        ]
        + [full] * 5,
        out_specs=[full] * 3,
        scratch_shapes=[
            pltpu.VMEM((seq_len, local_width), jnp.float32),
            pltpu.VMEM((seq_len, local_width), jnp.float32),
            pltpu.VMEM((2 * seq_len, local_width), jnp.float32),
        ],
        compiler_params=pltpu.CompilerParams(vmem_limit_bytes=VMEM_LIMIT),
        name="attention_backward",
    )(grad_whole, w_out, probs, query_u, query_v, key_rows, value_rows, position)
    grad_in = contract_rows(whole, d_projected)
    d_normed = contract_cols(d_projected, w_in)
    grad_pos = contract_rows(table_low, d_position)
    grad_out = contract_rows(context, grad_whole)
    return (d_normed, grad_in, grad_pos, grad_bias, grad_out)


def conv_front(whole, w_in, kernel, mask_col):
    seq_len, model_width = whole.shape
    local_width = w_in.shape[2]
    glu_in = matmul(whole, w_in.reshape(model_width, 2 * local_width))
    gate_value = glu_in[:, :local_width]
    logistic = jax.nn.sigmoid(glu_in[:, local_width:])
    glu_out = gate_value * logistic * mask_col
    tap_count = kernel.shape[0]
    half_taps = (tap_count - 1) // 2
    padded = jnp.pad(glu_out, ((half_taps, half_taps), (0, 0)))
    kernel_float = kernel.astype(jnp.float32)
    conved = kernel_float[0] * padded[0:seq_len]
    for tap_index in range(1, tap_count):
        conved = conved + kernel_float[tap_index] * padded[tap_index : tap_index + seq_len]
    return (gate_value, logistic, padded, conved)


def batch_stats(conved, mask_col, frame_count):
    local_sum = jnp.sum(conved * mask_col, axis=0)
    local_squares = jnp.sum(conved * conved * mask_col, axis=0)
    total_sum, total_squares = dp_total(jnp.stack([local_sum, local_squares]))
    average = total_sum / frame_count
    variance = total_squares / frame_count - average * average
    return (average, lax.rsqrt(variance + batch_eps))


def conv_tail(conved, stats, bn_gain, bn_bias):
    average, inv_std = stats
    normed_b = (conved - average) * inv_std * bn_gain.astype(jnp.float32) + bn_bias.astype(
        jnp.float32
    )
    return (normed_b, jax.nn.silu(normed_b).astype(jnp.bfloat16))


def conv_backward(whole, weights, mask_col, stats, frame_count, grad_whole):
    w_in, kernel, bn_gain, bn_bias, w_out = weights
    seq_len, model_width = whole.shape
    local_width = w_in.shape[2]
    gate_value, logistic, padded, conved = conv_front(whole, w_in, kernel, mask_col)
    normed_b, active = conv_tail(conved, stats, bn_gain, bn_bias)
    average, inv_std = stats
    grad_out = contract_rows(active, grad_whole)
    d_normed = contract_cols(grad_whole, w_out) * silu_slope(normed_b)
    centred = (conved - average) * inv_std
    bias_total, gain_total = dp_total(
        jnp.stack([jnp.sum(d_normed, axis=0), jnp.sum(d_normed * centred, axis=0)])
    )
    d_conved = (
        bn_gain.astype(jnp.float32)
        * inv_std
        * (d_normed - mask_col * (bias_total + centred * gain_total) / frame_count)
    )
    tap_count = kernel.shape[0]
    half_taps = (tap_count - 1) // 2
    kernel_float = kernel.astype(jnp.float32)
    d_padded = jnp.pad(d_conved, ((half_taps, half_taps), (0, 0)))
    d_glu = kernel_float[0] * d_padded[tap_count - 1 : tap_count - 1 + seq_len]
    for tap_index in range(1, tap_count):
        d_glu = (
            d_glu
            + kernel_float[tap_index]
            * d_padded[tap_count - 1 - tap_index : tap_count - 1 - tap_index + seq_len]
        )
    grad_kernel = jnp.stack(
        [
            jnp.sum(d_conved * padded[tap_index : tap_index + seq_len], axis=0)
            for tap_index in range(tap_count)
        ]
    )
    d_glu = d_glu * mask_col
    d_pair = jnp.concatenate(
        [d_glu * logistic, d_glu * gate_value * logistic * (1.0 - logistic)], axis=1
    ).astype(jnp.bfloat16)
    grad_in = contract_rows(whole, d_pair).reshape(model_width, 2, local_width)
    d_normed_in = contract_cols(d_pair, w_in.reshape(model_width, 2 * local_width))
    return (d_normed_in, grad_in, grad_kernel, grad_out, gain_total, bias_total)


def body(
    frames_in,
    lengths,
    out_grad,
    norm_gains,
    ffn1_up,
    ffn1_down,
    attn_in,
    pos_proj,
    pos_bias,
    attn_out,
    conv_in,
    depthwise,
    bn_scale,
    bn_shift,
    conv_out,
    ffn2_up,
    ffn2_down,
):
    unused, local_rows, model_width = frames_in.shape
    seq_len = local_rows * lax.axis_size("mp")
    dp_index = lax.axis_index("dp")
    own_length = lax.dynamic_slice_in_dim(lengths, dp_index, 1)[0]
    valid_keys = jnp.arange(seq_len) < own_length
    mask_col = valid_keys.astype(jnp.float32)[:, None]
    frame_count = jnp.sum(lengths).astype(jnp.float32)
    frames = frames_in.reshape(local_rows, model_width)
    _, whole_first, fetched, small = open_step(
        open_middle,
        [frames, norm_gains],
        [ffn1_up, ffn1_down, pos_proj, attn_out, conv_out],
        (0, 1, 0, 1, 1),
        jnp.concatenate([pos_bias, depthwise, bn_scale[None], bn_shift[None]], axis=0),
        0,
    )
    up_one, down_one, pos_whole, attn_out_whole, conv_out_whole = fetched
    taps = depthwise.shape[0]
    ffn_first = (up_one, down_one)
    attn_held = (
        lax.all_gather(attn_in.reshape(attn_in.shape[0], -1), "dp", axis=0, tiled=True),
        pos_whole,
        small[:2],
        attn_out_whole,
    )
    conv_held = (
        lax.all_gather(conv_in, "dp", axis=0, tiled=True),
        small[2 : 2 + taps],
        small[2 + taps],
        small[3 + taps],
        conv_out_whole,
    )
    ffn_second = (
        lax.all_gather(ffn2_up, "dp", axis=0, tiled=True),
        lax.all_gather(ffn2_down, "dp", axis=1, tiled=True),
    )
    table_low = position_table(seq_len, model_width).astype(jnp.bfloat16)
    position = matmul(table_low, pos_whole).astype(jnp.bfloat16)
    (after_first,), whole_attn, _ = between_step(
        functools.partial(forward_middle, 0.5, 1),
        ffn_forward(whole_first, ffn_first),
        [frames, norm_gains],
        [],
        (),
        (),
        1,
    )
    attn_partial, *attn_saved = attention_forward(
        whole_attn, attn_held, position, own_length[None]
    )
    (after_attn,), whole_conv, _ = between_step(
        functools.partial(forward_middle, 1.0, 2),
        attn_partial,
        [after_first, norm_gains],
        [],
        (),
        (),
        2,
    )
    gate_value, logistic, padded, conved = conv_front(
        whole_conv, conv_held[0], conv_held[1], mask_col
    )
    stats = batch_stats(conved, mask_col, frame_count)
    normed_b, active = conv_tail(conved, stats, conv_held[2], conv_held[3])
    (after_conv,), whole_second, _ = between_step(
        functools.partial(forward_middle, 1.0, 3),
        matmul(active, conv_held[4]),
        [after_attn, norm_gains],
        [],
        (),
        (),
        3,
    )
    (block_out, d_second, gain_five), whole_grads, _ = between_step(
        turn_middle,
        ffn_forward(whole_second, ffn_second),
        [after_conv, norm_gains, out_grad.reshape(local_rows, model_width)],
        [],
        (),
        (),
        4,
    )
    d_normed, grad_up, grad_down = ffn_backward(whole_second, ffn_second, whole_grads)
    (d_conv, gain_four), whole_grads, (total_up_two, total_down_two) = between_step(
        functools.partial(backward_middle, 1.0, 3),
        d_normed,
        [after_conv, norm_gains, d_second],
        [grad_up, grad_down],
        (0, 1),
        (False, True),
        5,
    )
    d_normed, grad_conv_in, grad_kernel, grad_conv_out, gain_total, bias_total = conv_backward(
        whole_conv, conv_held, mask_col, stats, frame_count, whole_grads
    )
    (d_attn, gain_three), whole_grads, (total_conv_in, total_conv_out) = between_step(
        functools.partial(backward_middle, 1.0, 2),
        d_normed,
        [after_attn, norm_gains, d_conv],
        [grad_conv_in.reshape(model_width, -1), grad_conv_out],
        (0, 1),
        (False, True),
        6,
    )
    d_normed, grad_attn_in, grad_pos, grad_bias, grad_attn_out = attention_backward(
        whole_attn, attn_held, table_low, position, attn_saved, whole_grads
    )
    (d_first, gain_two), whole_grads, (total_attn_in, total_attn_out, total_pos) = between_step(
        functools.partial(backward_middle, 0.5, 1),
        d_normed,
        [after_first, norm_gains, d_attn],
        [grad_attn_in, grad_attn_out, grad_pos],
        (0, 1, 0),
        (False, True, True),
        7,
    )
    d_normed, grad_up, grad_down = ffn_backward(whole_first, ffn_first, whole_grads)
    (in_grad,), small_grads, gains, (total_up_one, total_down_one) = close_step(
        close_middle,
        d_normed,
        jnp.concatenate([grad_bias, grad_kernel], axis=0),
        jnp.concatenate([gain_two, gain_three, gain_four, gain_five], axis=0),
        [frames, norm_gains, d_first],
        [grad_up, grad_down],
        (0, 1),
        (False, True),
        8,
    )
    gain_sum = jnp.concatenate([gains[4:], gains[:4]], axis=0)
    block = model_width // lax.axis_size("dp")
    piece_len = bn_scale.shape[0]
    own = dp_index * piece_len
    small_grads = lax.dynamic_slice_in_dim(small_grads, own, piece_len, axis=1)
    return (
        block_out.reshape(1, local_rows, model_width),
        in_grad.reshape(1, local_rows, model_width),
        gain_sum,
        total_up_one,
        total_down_one,
        total_attn_in.reshape(block, 3, -1),
        total_pos,
        small_grads[:2],
        total_attn_out,
        total_conv_in.reshape(block, 2, -1),
        small_grads[2:],
        lax.dynamic_slice_in_dim(gain_total, own, piece_len),
        lax.dynamic_slice_in_dim(bias_total, own, piece_len),
        total_conv_out,
        total_up_two,
        total_down_two,
    )


def solution(mesh):
    placed = (
        P("dp", "mp", None),
        P(),
        P("dp", "mp", None),
        P(),
        P("dp", "mp"),
        P("mp", "dp"),
        P("dp", None, "mp"),
        P("dp", "mp"),
        P(None, ("mp", "dp")),
        P("mp", "dp"),
        P("dp", None, "mp"),
        P(None, ("mp", "dp")),
        P(("mp", "dp")),
        P(("mp", "dp")),
        P("mp", "dp"),
        P("dp", "mp"),
        P("mp", "dp"),
    )
    return jax.shard_map(
        body,
        mesh=mesh,
        in_specs=placed,
        out_specs=(
            P("dp", "mp", None),
            P("dp", "mp", None),
            P(),
            P("dp", "mp"),
            P("mp", "dp"),
            P("dp", None, "mp"),
            P("dp", "mp"),
            P(None, ("mp", "dp")),
            P("mp", "dp"),
            P("dp", None, "mp"),
            P(None, ("mp", "dp")),
            P(("mp", "dp")),
            P(("mp", "dp")),
            P("mp", "dp"),
            P("dp", "mp"),
            P("mp", "dp"),
        ),
        check_vma=False,
    )
```

time: 656 us -> 558 us (0.85)
  Pallas kernels: 512 us -> 439 us
  other arithmetic: 32.8 us -> 10.2 us
    pallas_call x18 -> x9, Pallas kernels: 457 us -> 404 us  [call_step(): pl.pallas_call(kernel, out_shape=out_shape, in_specs=[vmem] * len(inputs)...]
    pallas_call x5 -> x2, Pallas kernels: 32.3 us -> 12.6 us  [all_total(): pl.pallas_call(functools.partial(all_total_kernel, axis), out_shape=jax.S...]
    reduce_sum x20 -> x0, other arithmetic: 15.6 us -> none  [the longest x5 4.9 us: layer_norm(): average = jnp.mean(values, axis=-1, keepdims=True)]
    convert_element_type x8 -> x0, other arithmetic: 6.86 us -> none  [the longest x4 3.5 us: enter_block(): return spread_rows(layer_norm(residual, norm_gain).astype(jnp.bfloat16))]
    unnamed x98 -> x93, local copies, waits for them, and re-layouts: 14.3 us -> 14.4 us
  transfers between devices with their start and end apart: 4 -> 4, of which waited for: 0 -> 0; matrix products, arithmetic and copies ran while one was open for 6% -> 5% of each run, Pallas kernels for 33% -> 35%
where the time goes in v4:
time: 558 us; the launch traced here: 549 us
  Pallas kernels  439 us (79%)
  matrix products  58.7 us (11%)
  local copies, waits for them, and re-layouts  23.6 us (4%)
  between operations  15.4 us (3%)
  other arithmetic  10.2 us (2%)
    pallas_call x9, Pallas kernels, call_step(): pl.pallas_call(kernel, out_shape=out_shape, in_specs=[vmem] * len(inputs)...  404 us
    dot_general x9, matrix products, contract_rows(): lax.dot_general(left, right, (((0,), (0,)), ((), ())), preferred_element_...  21.8 us
    dot_general x7, matrix products, matmul(): return jnp.dot(left, right, preferred_element_type=jnp.float32)  20.6 us
    dot_general x7, matrix products, contract_cols(): lax.dot_general(left, right, (((1,), (1,)), ((), ())), preferred_element_...  16.3 us
    unnamed x93, local copies, waits for them, and re-layouts  14.4 us
    pallas_call x1, Pallas kernels, attention_backward(): pl.pallas_call(functools.partial(attention_back_kernel, HEAD ** (-0.5)),...  12.7 us
    pallas_call x2, Pallas kernels, all_total(): pl.pallas_call(functools.partial(all_total_kernel, axis), out_shape=jax.S...  12.6 us
  transfers between devices with their start and end apart: 4, of which 0 were waited for; matrix products, arithmetic and copies ran while one was open for 5% of the time, Pallas kernels for 35%

profile of v4, /device:TPU:0, one launch (start us, length us, event | category | flops | bytes accessed | tf_op | source)
XLA Modules:
  0.0 549.2 jit_solution(1214862130657561137)
XLA Ops:
  8.0 1.1 copy.42
  9.1 0.8 copy.43
  11.2 1.3 fusion.20.refs_7_
  12.6 45.5 %open_step.1 = (bf16[512,1024]{1,0:T(8,128)(2,1)}, bf16[1024,1024]{1,0:T(8,128)(2,1)}, bf16[1024,1024]{1,0:T(8,128)(2,1)}, bf16[1024,256]{1,0:T(8,128)(2,1)}, bf...) custom-call(bf16[128,1024]{1,0:T(8,128)(2,1)} %bitcast.73, f32[5,1024]{1,0:T(8,128)} %refs_4_.3, ...), custom_call_target="tpu_custom_call" | custom-call | tf_op jit(solution)/shard_map/open_step/pallas_call | solution.py:523
  62.0 3.3 fusion.37
  65.4 1.4 copy-done.37
  66.7 2.2 convolution_convert_fusion.10.refs_0_
  69.0 48.1 %between_step.7 = (f32[128,1024]{1,0:T(8,128)}, bf16[512,1024]{1,0:T(8,128)(2,1)}) custom-call(bf16[512,1024]{1,0:T(8,128)(2,1)} %convolution_convert_fusion.10.refs_0_, bf16[128,1024]{1,0:T(8,128)(2,1)} %bitcast.74, f32[5,1024]{1,0:T(8,128)} %refs_4_.3), custom_call_target="tpu_custom_call" | custom-call | tf_op jit(solution)/shard_map/between_step/pallas_call | solution.py:523
  117.8 1.0 fusion.5
  119.5 1.4 copy-done.1
  120.9 1.5 convolution_convert_fusion.16.position_ref
  122.4 1.4 copy.47
  123.9 10.2 %attention_forward.1 = (bf16[512,1024]{1,0:T(8,128)(2,1)}, f32[2,512,512]{2,1,0:T(8,128)}, bf16[512,256]{1,0:T(8,128)(2,1)}, bf16[512,256]{1,0:T(8,128)(2,1)}, b...) custom-call(s32[1]{0:T(128)} %dynamic_slice.16.length_ref, ...), custom_call_target="tpu_custom_call" | custom-call | tf_op jit(solution)/shard_map/attention_forward/pallas_call | solution.py:788
  134.2 42.4 %between_step.8 = (f32[128,1024]{1,0:T(8,128)}, bf16[512,1024]{1,0:T(8,128)(2,1)}) custom-call(bf16[512,1024]{1,0:T(8,128)(2,1)} %get-tuple-element.71.refs_0_, f32[128,1024]{1,0:T(8,128)} %get-tuple-element.72.refs_1_, f32[5,1024]{1,0:T(8,128)} %refs_4_.3), custom_call_target="tpu_custom_call" | custom-call | tf_op jit(solution)/shard_map/between_step/pallas_call | solution.py:523
  176.6 1.9 fusion.38
  179.7 6.7 %all_total.2 = f32[2,256]{1,0:T(2,128)} custom-call(f32[2,256]{1,0:T(2,128)} %pad_maximum_fusion.5.in_ref), custom_call_target="tpu_custom_call" | custom-call | tf_op jit(solution)/shard_map/all_total/pallas_call | solution.py:127
  187.1 2.6 convolution_convert_fusion.9.refs_0_
  189.7 41.2 %between_step.9 = (f32[128,1024]{1,0:T(8,128)}, bf16[512,1024]{1,0:T(8,128)(2,1)}) custom-call(bf16[512,1024]{1,0:T(8,128)(2,1)} %convolution_convert_fusion.9.refs_0_, f32[128,1024]{1,0:T(8,128)} %get-tuple-element.75.refs_1_, f32[5,1024]{1,0:T(8,128)} %refs_4_.3), custom_call_target="tpu_custom_call" | custom-call | tf_op jit(solution)/shard_map/between_step/pallas_call | solution.py:523
  230.9 4.5 fusion.39
  235.4 4.5 convolution_convert_fusion.8.refs_0_
  239.9 43.7 %between_step.10 = (bf16[128,1024]{1,0:T(8,128)(2,1)}, f32[128,1024]{1,0:T(8,128)}, f32[1,1024]{1,0:T(1,128)}, bf16[512,1024]{1,0:T(8,128)(2,1)}) custom-call(bf16[512,1024]{1,0:T(8,128)(2,1)} %convolution_convert_fusion.8.refs_0_, f32[128,1024]{1,0:T(8,128)} %get-tuple-element.77.refs_1_, f32[5,1024]{1,0:T(8,128)} %refs_4_.3, bf16[128,1024]{1,0:T(8,128)(2,1)} %bitcast.84), custom_call_target="tpu_custom_call" | custom-call | tf_op jit(solution)/shard_map/between_step/pallas_call | solution.py:523
  283.7 4.6 convolution_convert_fusion.2.refs_5_
  288.4 1.6 multiply_convert_fusion.1
  290.0 2.6 convolution_convert_fusion.3.refs_4_
  292.6 2.3 convolution_convert_fusion.7.refs_0_
  294.9 49.6 %between_step.11 = (f32[128,1024]{1,0:T(8,128)}, f32[1,1024]{1,0:T(1,128)}, bf16[512,1024]{1,0:T(8,128)(2,1)}, f32[128,1024]{1,0:T(8,128)}, f32[1024,128]{1,0:T(8,128)}) custom-call(bf16[512,1024]{1,0:T(8,128)(2,1)} %convolution_convert_fusion.7.refs_0_, f32[128,1024]{1,0:T(8,128)} %get-tuple-element.77.refs_1_, f32[5,1024]{1,0:T(8,128)} %refs_4_.3, ...), custom_call_target="tpu_custom_call" | custom-call | tf_op jit(solution)/shard_map/between_step/pallas_call | solution.py:523
  344.5 2.7 fusion.33
  347.2 1.3 convolution_convert_fusion.14.refs_5_
  349.1 5.9 %all_total.3 = f32[2,256]{1,0:T(2,128)} custom-call(f32[2,256]{1,0:T(2,128)} %pad_maximum_fusion.6.in_ref), custom_call_target="tpu_custom_call" | custom-call | tf_op jit(solution)/shard_map/all_total/pallas_call | solution.py:127
  355.8 1.5 multiply_reduce_fusion
  358.6 1.7 convolution_convert_fusion.11.refs_4_
  360.3 1.7 convolution_convert_fusion.12.refs_0_
  362.0 42.7 %between_step.12 = (f32[128,1024]{1,0:T(8,128)}, f32[1,1024]{1,0:T(1,128)}, bf16[512,1024]{1,0:T(8,128)(2,1)}, f32[128,512]{1,0:T(8,128)}, f32[256,128]{1,0:T(8,128)}) custom-call(bf16[512,1024]{1,0:T(8,128)(2,1)} %convolution_convert_fusion.12.refs_0_, f32[128,1024]{1,0:T(8,128)} %get-tuple-element.75.refs_1_, f32[5,1024]{1,0:T(8,128)} %refs_4_.3, ...), custom_call_target="tpu_custom_call" | custom-call | tf_op jit(solution)/shard_map/between_step/pallas_call | solution.py:523
  404.7 12.7 %attention_backward.1 = (bf16[512,768]{1,0:T(8,128)(2,1)}, bf16[1024,256]{1,0:T(8,128)(2,1)}, f32[2,256]{1,0:T(2,128)}) custom-call(bf16[512,1024]{1,0:T(8,128)(2,1)} %get-tuple-element.83.grad_ref, bf16[256,1024]{1,0:T(8,128)(2,1)} %get-tuple-element.70.out_w_ref, f32[2,512,512]{2,1,0:T(8,128)} %get-tuple-element.84.probs_ref, ...), custom_call_target="tpu_custom_call" | custom-call | tf_op jit(solution)/shard_map/attention_backward/pallas_call | solution.py:867
  417.4 2.8 convolution_convert_fusion.15.refs_6_
  420.2 1.3 convolution_convert_fusion.13.refs_5_
  421.5 2.2 convolution_convert_fusion.4.refs_4_
  423.7 2.0 convolution_convert_fusion.5.refs_0_
  425.6 46.2 %between_step.13 = (f32[128,1024]{1,0:T(8,128)}, f32[1,1024]{1,0:T(1,128)}, bf16[512,1024]{1,0:T(8,128)(2,1)}, f32[128,768]{1,0:T(8,128)}, f32[256,128]{1,0:T(8,128)}, /*index=5*/f32[128,256]{1,0:T(8,128)}) custom-call(bf16[512,1024]{1,0:T(8,128)(2,1)} %convolution_convert_fusion.5.refs_0_, f32[128,1024]{1,0:T(8,128)} %get-tuple-element.72.refs_1_, ...), custom_call_target="tpu_custom_call" | custom-call | tf_op jit(solution)/shard_map/between_step/pallas_call | solution.py:523
  471.9 3.7 multiply_convert_fusion
  475.6 2.3 convolution_convert_fusion.6.refs_0_
  477.9 2.6 convolution_convert_fusion.1.refs_6_
  480.5 2.7 convolution_convert_fusion.refs_7_
  485.1 44.3 %close_step.1 = (f32[128,1024]{1,0:T(8,128)}, f32[7,256]{1,0:T(8,128)}, f32[5,1024]{1,0:T(8,128)}, f32[128,1024]{1,0:T(8,128)}, f32[1024,128]{1,0:T(8,128)}) custom-call(bf16[512,1024]{1,0:T(8,128)(2,1)} %convolution_convert_fusion.6.refs_0_, f32[7,256]{1,0:T(8,128)} %concatenate.18.refs_1_, f32[4,1024]{1,0:T(4,128)} %pad_maximum_fusion.4.refs_2_, ...), custom_call_target="tpu_custom_call" | custom-call | tf_op jit(solution)/shard_map/close_step/pallas_call | solution.py:523
  529.4 0.8 constant_dynamic-slice_fusion.2
  532.9 0.9 reshape.293
  534.0 0.9 copy.45
  536.2 0.8 copy.60
  (137 shorter events, 22.5 us)
Async XLA Ops:
  7.2 51.9 %copy-start.36 = (s32[8]{0:T(128)S(1)}, s32[8]{0:T(128)}, u32[]{:S(2)}) copy-start(s32[8]{0:T(128)} %param.18) | copy-start | bytes 100
  7.2 115.2 %all-gather.7.cloned.1.call-start = ((), (), s32[]{:S(2)}) async-start(), calls=%async_computation.1 | async-start | bytes 1179648 | tf_op jit(solution)/shard_map/all_gather | solution.py:1020
  7.9 116.0 %all-gather.5.cloned.1.call-start = ((), (), s32[]{:S(2)}) async-start(), calls=%async_computation | async-start | bytes 1769472 | tf_op jit(solution)/shard_map/all_gather | solution.py:1014
  9.9 221.0 %all-gather.9.cloned.1.call-start = ((), (), s32[]{:S(2)}) async-start(), calls=%async_computation.2 | async-start | bytes 2359296 | tf_op jit(solution)/shard_map/all_gather | solution.py:1027
  10.7 224.8 %all-gather.11.cloned.1.call-start = ((), (), s32[]{:S(2)}) async-start(), calls=%async_computation.3 | async-start | bytes 2359296 | tf_op jit(solution)/shard_map/all_gather | solution.py:1028
  62.0 4.7 copy-start.23
  65.4 1.4 copy-start.37
  69.0 51.9 %copy-start.35 = (bf16[1024,256]{1,0:T(8,128)(2,1)S(1)}, bf16[1024,256]{1,0:T(8,128)(2,1)}, u32[]{:S(2)}) copy-start(bf16[1024,256]{1,0:T(8,128)(2,1)} %get-tuple-element.69) | copy-start | bytes 1572868
  119.5 1.4 copy-start.1
  283.7 4.7 copy-start.26
  283.7 4.7 copy-start.32
  283.7 4.7 copy-start.39
  288.3 1.6 copy-start.29
  290.0 2.6 copy-start.25
  294.9 49.6 %copy-start.34 = (bf16[256,1024]{1,0:T(8,128)(2,1)S(1)}, bf16[256,1024]{1,0:T(8,128)(2,1)}, u32[]{:S(2)}) copy-start(bf16[256,1024]{1,0:T(8,128)(2,1)} %get-tuple-element.74) | copy-start | bytes 1572868
  344.5 2.7 copy-start.31
  357.3 1.2 copy-start.28
  404.7 12.7 %copy-start.2 = (bf16[32,32,1024]{2,1,0:T(8,128)(2,1)S(1)}, bf16[32,32,1024]{2,1,0:T(8,128)(2,1)}, u32[]{:S(2)}) copy-start(bf16[32,32,1024]{2,1,0:T(8,128)(2,1)} %copy-done.1) | copy-start | bytes 6291460
  417.4 2.8 copy-start
  417.4 2.8 copy-start.11
  417.4 4.1 copy-start.4
  417.4 4.0 copy-start.33
  421.5 2.2 copy-start.3
  425.6 46.2 %copy-start.24 = (bf16[1024,1024]{1,0:T(8,128)(2,1)S(1)}, bf16[1024,1024]{1,0:T(8,128)(2,1)}, u32[]{:S(2)}) copy-start(bf16[1024,1024]{1,0:T(8,128)(2,1)} %get-tuple-element.67) | copy-start | bytes 6291460
  471.9 3.7 copy-start.22
  475.6 2.3 copy-start.27
  477.9 2.6 copy-start.30
  477.9 2.6 copy-start.38
  480.5 3.3 copy-start.17
  480.5 3.3 copy-start.18
  480.5 3.3 copy-start.19
  480.5 3.3 copy-start.20
  480.5 3.9 copy-start.21
  485.1 47.9 %copy-start.13 = (f32[128,512]{1,0:T(8,128)S(1)}, f32[128,512]{1,0:T(8,128)}, u32[]{:S(2)}) copy-start(f32[128,512]{1,0:T(8,128)} %get-tuple-element.108) | copy-start | bytes 786436
  485.1 48.7 %copy-start.10 = (f32[128,768]{1,0:T(8,128)S(1)}, f32[128,768]{1,0:T(8,128)}, u32[]{:S(2)}) copy-start(f32[128,768]{1,0:T(8,128)} %get-tuple-element.104) | copy-start | bytes 1179652
  529.4 6.1 %copy-start.12 = (bf16[128,1024]{1,0:T(8,128)(2,1)S(1)}, bf16[128,1024]{1,0:T(8,128)(2,1)}, u32[]{:S(2)}) copy-start(bf16[128,1024]{1,0:T(8,128)(2,1)} %get-tuple-element.78) | copy-start | bytes 786436
  529.4 6.8 %copy-start.9 = (f32[128,1024]{1,0:T(8,128)S(1)}, f32[128,1024]{1,0:T(8,128)}, u32[]{:S(2)}) copy-start(f32[128,1024]{1,0:T(8,128)} %get-tuple-element.100) | copy-start | bytes 1572868
  529.4 7.6 %copy-start.8 = (f32[128,1024]{1,0:T(8,128)S(1)}, f32[128,1024]{1,0:T(8,128)}, u32[]{:S(2)}) copy-start(f32[128,1024]{1,0:T(8,128)} %get-tuple-element.213) | copy-start | bytes 1572868
  533.8 4.0 copy-start.7
  534.0 4.7 copy-start.16
  534.9 4.4 copy-start.15
  535.5 4.4 copy-start.14
  535.5 5.1 copy-start.6
  537.0 4.4 copy-start.5
Sparse Core Ops, SparseCore 0:
  9.9 30.4 all-gather.6
  42.9 25.5 all-gather.4
  70.4 27.7 all-gather.8
  99.9 28.1 all-gather.10

commit v5 on v4

--- a/solution.py
+++ b/solution.py
@@ -61,6 +61,7 @@
 
 MESH = pl.DeviceIdType.MESH
 VMEM_LIMIT = 60 * 1024 * 1024
+CHUNKS = 2
 
 
 def line_copy(src, dst, sems, index, axis, target):
@@ -177,18 +178,21 @@
 
 
 class LineGather:
-    def __init__(self, axis, out_ref, sems):
-        self.axis, self.out, self.sems = axis, out_ref, sems
+    def __init__(self, axis, out_ref, sems, chunks):
+        self.axis, self.out, self.sems, self.chunks = axis, out_ref, sems, chunks
         self.size, self.me = lax.axis_size(axis), lax.axis_index(axis)
         self.rows = out_ref.shape[0] // self.size
+        self.part = self.rows // chunks
         self.steps = self.size - 1
 
-    def piece(self, index):
-        return self.out.at[pl.ds(pl.multiple_of(index * self.rows, self.rows), self.rows)]
-
-    def copy(self, way, step, index):
+    def piece(self, index, chunk):
+        start = pl.multiple_of(index * self.rows + chunk * self.part, self.part)
+        return self.out.at[pl.ds(start, self.part)]
+
+    def copy(self, way, step, index, chunk):
+        place = self.piece(index, chunk)
         return line_copy(
-            self.piece(index), self.piece(index), self.sems, way * self.steps + step, self.axis,
+            place, place, self.sems, (way * self.steps + step) * self.chunks + chunk, self.axis,
             self.me + 1 if way == 0 else self.me - 1,
         )
 
@@ -201,81 +205,108 @@
     def onward(self, way):
         return self.me + 1 < self.size if way == 0 else self.me > 0
 
-    def step(self, step):
+    def step(self, step, chunk):
         for way in range(2):
             if step > 0:
                 @pl.when(self.held(way, step))
                 def _():
-                    self.copy(way, step - 1, self.index(way, step)).wait_recv()
+                    self.copy(way, step - 1, self.index(way, step), chunk).wait_recv()
 
             if step < self.steps:
                 @pl.when(jnp.logical_and(self.held(way, step), self.onward(way)))
                 def _():
-                    self.copy(way, step, self.index(way, step)).start()
+                    self.copy(way, step, self.index(way, step), chunk).start()
 
     def finish(self):
-        for step in range(self.steps):
-            for way in range(2):
-                @pl.when(jnp.logical_and(self.held(way, step), self.onward(way)))
-                def _():
-                    self.copy(way, step, self.index(way, step)).wait_send()
+        for chunk in range(self.chunks):
+            for step in range(self.steps):
+                for way in range(2):
+                    @pl.when(jnp.logical_and(self.held(way, step), self.onward(way)))
+                    def _():
+                        self.copy(way, step, self.index(way, step), chunk).wait_send()
 
 
 class LineScatter:
-    def __init__(self, axis, in_ref, total_ref, slots, staged, sems):
-        self.axis, self.ins, self.total = axis, in_ref, total_ref
+    def __init__(self, axis, in_ref, total_ref, slots, staged, sems, chunks):
+        self.axis, self.ins, self.total, self.chunks = axis, in_ref, total_ref, chunks
         self.slots, self.staged, self.sems = slots, staged, sems
         self.size, self.me = lax.axis_size(axis), lax.axis_index(axis)
         self.rows = total_ref.shape[0]
+        self.part = self.rows // chunks
         self.first_way = lax.div(self.me, (self.size + 1) // 2)
 
-    def mine(self, owner):
-        return self.ins.at[pl.ds(pl.multiple_of(owner * self.rows, self.rows), self.rows)]
-
-    def copy(self, way, owner, src):
+    def mine(self, owner, chunk):
+        start = pl.multiple_of(owner * self.rows + chunk * self.part, self.part)
+        return self.ins.at[pl.ds(start, self.part)]
+
+    def lines(self, chunk):
+        return slice(chunk * self.part, (chunk + 1) * self.part)
+
+    def copy(self, way, owner, chunk, src):
         return line_copy(
-            src, self.slots.at[way, owner], self.sems, way * self.size + owner, self.axis,
+            src, self.slots.at[way, owner, self.lines(chunk)], self.sems,
+            (way * self.size + owner) * self.chunks + chunk, self.axis,
             self.me + 1 - 2 * way,
         )
 
-    def hop(self, way, step):
+    def arrived(self, way, owner, chunk):
+        return self.copy(way, owner, chunk, self.staged.at[way, owner, self.lines(chunk)])
+
+    def place(self, way, step):
         owner = (1 - way) * (self.size - 1 - step) + way * step
         distance = (owner - self.me) * (1 - 2 * way)
         behind = (1 - way) * self.me + way * (self.size - 1 - self.me)
-
-        @pl.when(jnp.logical_and(distance > 0, behind == 0))
-        def _():
-            self.copy(way, owner, self.mine(owner)).start()
+        return owner, distance, behind
+
+    def lead(self, step, chunk):
+        for way in range(2):
+            owner, distance, behind = self.place(way, step)
+
+            @pl.when(jnp.logical_and(distance > 0, behind == 0))
+            def _():
+                self.copy(way, owner, chunk, self.mine(owner, chunk)).start()
+
+    def hop(self, way, step, chunk):
+        owner, distance, behind = self.place(way, step)
 
         @pl.when(jnp.logical_and(distance > 0, behind > 0))
         def _():
-            self.copy(way, owner, self.staged.at[way, owner]).wait_recv()
-            self.staged[way, owner] = (
-                self.mine(owner)[...].astype(jnp.float32)
-                + self.slots[way, owner].astype(jnp.float32)
+            lines = self.lines(chunk)
+            self.arrived(way, owner, chunk).wait_recv()
+            self.staged[way, owner, lines] = (
+                self.mine(owner, chunk)[...].astype(jnp.float32)
+                + self.slots[way, owner, lines].astype(jnp.float32)
             ).astype(self.staged.dtype)
-            self.copy(way, owner, self.staged.at[way, owner]).start()
-
-    def step(self, step):
-        self.hop(self.first_way, step)
-        self.hop(1 - self.first_way, step)
-
-    def result(self):
-        self.total[...] = self.mine(self.me)[...].astype(jnp.float32)
+            self.arrived(way, owner, chunk).start()
+
+    def run(self):
+        marks = [(step, chunk) for step in range(self.size - 1) for chunk in range(self.chunks)]
+        for mark in marks:
+            self.lead(*mark)
+        for number in range(len(marks) + self.chunks):
+            if number < len(marks):
+                self.hop(self.first_way, *marks[number])
+            if number >= self.chunks:
+                self.hop(1 - self.first_way, *marks[number - self.chunks])
+
+    def result(self, chunk):
+        lines = self.lines(chunk)
+        self.total[lines] = self.mine(self.me, chunk)[...].astype(jnp.float32)
         for way in range(2):
             @pl.when(self.me > 0 if way == 0 else self.me < self.size - 1)
             def _():
-                self.copy(way, self.me, self.staged.at[way, self.me]).wait_recv()
-                self.total[...] += self.slots[way, self.me].astype(jnp.float32)
-
-        return self.total[...]
+                self.arrived(way, self.me, chunk).wait_recv()
+                self.total[lines] += self.slots[way, self.me, lines].astype(jnp.float32)
+
+        return self.total[lines]
 
     def finish(self):
-        for owner in range(self.size):
-            for way in range(2):
-                @pl.when(self.me < owner if way == 0 else self.me > owner)
-                def _():
-                    self.copy(way, owner, self.staged.at[way, owner]).wait_send()
+        for chunk in range(self.chunks):
+            for owner in range(self.size):
+                for way in range(2):
+                    @pl.when(self.me < owner if way == 0 else self.me > owner)
+                    def _():
+                        self.arrived(way, owner, chunk).wait_send()
 
 
 class CubeGather:
@@ -410,7 +441,7 @@
             copy.wait_send()
 
 
-def open_kernel(middle, counts, dims, ways, *refs):
+def open_kernel(middle, counts, chunks, dims, ways, *refs):
     local_count, mid_count = counts
     count = len(dims)
     refs = list(refs)
@@ -419,28 +450,27 @@
     mids, (whole,), outs = take(mid_count), take(1), take(count)
     gather_sems, cube_sems = refs
     fetch = CubeGather("dp", dims, ways, ins, outs, cube_sems)
-    rows = LineGather("mp", whole, gather_sems)
+    rows = LineGather("mp", whole, gather_sems, chunks)
     greet("mp", "dp", False)
     fetch.step(0)
     values, normed = middle(None, *[ref[...] for ref in locals_])
     for ref, value in zip(mids, values):
         ref[...] = value
-    rows.piece(rows.me)[...] = normed
-    rows.step(0)
-    fetch.step(1)
-    rows.step(1)
-    fetch.step(2)
-    for step in range(3, fetch.stages + 1):
-        fetch.step(step)
-        if step <= rows.steps + 1:
-            rows.step(step - 1)
-    for step in range(max(2, fetch.stages), rows.steps + 1):
-        rows.step(step)
+    for chunk in range(chunks):
+        part = rows.part
+        rows.piece(rows.me, chunk)[...] = normed[chunk * part : (chunk + 1) * part]
+        rows.step(0, chunk)
+    for step in range(1, max(rows.steps, fetch.stages) + 1):
+        if step <= fetch.stages:
+            fetch.step(step)
+        if step <= rows.steps:
+            for chunk in range(chunks):
+                rows.step(step, chunk)
     rows.finish()
     fetch.finish()
 
 
-def between_kernel(middle, counts, gathers, dims, ways, *refs):
+def between_kernel(middle, counts, chunks, fetches, dims, ways, *refs):
     local_count, mid_count = counts
     count = len(dims)
     refs = list(refs)
@@ -448,35 +478,49 @@
     (partial,), locals_, ins = take(1), take(local_count), take(count)
     mids, (whole,), outs = take(mid_count), take(1), take(count)
     (total, slots, staged, scatter_sems, gather_sems), refs = refs[:5], refs[5:]
-    sums = LineScatter("mp", partial, total, slots, staged, scatter_sems)
-    rows = LineGather("mp", whole, gather_sems)
-    grads = CubeScatter("dp", dims, ways, ins, outs, refs[:count], refs[count]) if count else None
+    sums = LineScatter("mp", partial, total, slots, staged, scatter_sems, chunks)
+    rows = LineGather("mp", whole, gather_sems, chunks)
+    beside, stages = None, 0
+    if count:
+        if fetches:
+            beside = CubeGather("dp", dims, ways, ins, outs, refs[0])
+        else:
+            beside = CubeScatter("dp", dims, ways, ins, outs, refs[:count], refs[count])
+        stages = beside.stages + 1
     greet("mp", "dp" if count else None, False)
     stage = 0
-    for step in range(sums.size - 1):
-        sums.step(step)
-        if count and step in (0, 2):
-            grads.step(stage)
+    if stages:
+        beside.step(0)
+        stage = 1
+    sums.run()
+    for chunk in range(chunks):
+        lines = sums.lines(chunk)
+        picked = [ref[lines] if ref.shape[0] == sums.rows else ref[...] for ref in locals_]
+        values, normed = middle(sums.result(chunk), *picked)
+        rows.piece(rows.me, chunk)[...] = normed
+        rows.step(0, chunk)
+        for ref, value in zip(mids, values):
+            if ref.shape[0] == sums.rows:
+                ref[lines] = value
+            elif chunk == 0:
+                ref[...] = value
+            else:
+                ref[...] += value
+    for step in range(1, rows.steps + 1):
+        if stage < stages:
+            beside.step(stage)
             stage += 1
-    values, normed = middle(sums.result(), *[ref[...] for ref in locals_])
-    rows.piece(rows.me)[...] = normed
-    rows.step(0)
-    for ref, value in zip(mids, values):
-        ref[...] = value
-    for step in range(1, rows.steps + 1):
-        if count and stage <= grads.stages:
-            grads.step(stage)
-            stage += 1
-        rows.step(step)
+        for chunk in range(chunks):
+            rows.step(step, chunk)
+    for stage in range(stage, stages):
+        beside.step(stage)
     if count:
-        for stage in range(stage, grads.stages + 1):
-            grads.step(stage)
-        grads.finish()
+        beside.finish()
     sums.finish()
     rows.finish()
 
 
-def close_kernel(middle, counts, dims, ways, *refs):
+def close_kernel(middle, counts, chunks, dims, ways, *refs):
     local_count, mid_count = counts
     count = len(dims)
     refs = list(refs)
@@ -485,28 +529,26 @@
     mids, (small_out, gains_out), outs = take(mid_count), take(2), take(count)
     (total, slots, staged, scatter_sems), refs = refs[:4], refs[4:]
     (small_slots, small_sems, gain_slots, gain_sems, last_slots, last_sems), refs = refs[:6], refs[6:]
-    sums = LineScatter("mp", partial, total, slots, staged, scatter_sems)
+    sums = LineScatter("mp", partial, total, slots, staged, scatter_sems, chunks)
     grads = CubeScatter("dp", dims, ways, ins, outs, refs[:count], refs[count])
     little = AllTotal("dp", small_slots, small_sems)
     near, far = AllTotal("dp", gain_slots, gain_sems), AllTotal("mp", last_slots, last_sems)
     little.slots[little.me] = small[...]
     greet("mp", "dp", True)
     little.start()
-    stage = 0
-    for step in range(sums.size - 1):
-        sums.step(step)
-        if step != 1:
-            grads.step(stage)
-            stage += 1
-    values, gain = middle(sums.result(), *[ref[...] for ref in locals_])
+    grads.step(0)
+    sums.run()
+    grads.step(1)
+    total_rows = jnp.concatenate([sums.result(chunk) for chunk in range(chunks)], axis=0)
+    values, gain = middle(total_rows, *[ref[...] for ref in locals_])
     near.slots[near.me] = jnp.concatenate([gains[...], gain], axis=0)
     near.start()
     for ref, value in zip(mids, values):
         ref[...] = value
-    grads.step(stage)
+    grads.step(2)
     far.slots[far.me] = near.result()
     far.start()
-    for stage in range(stage + 1, grads.stages + 1):
+    for stage in range(3, grads.stages + 1):
         grads.step(stage)
     small_out[...] = little.result()
     gains_out[...] = far.result()
@@ -533,13 +575,13 @@
     )(*inputs)
 
 
-def line_scratch(rows, width):
+def line_scratch(rows, width, chunks):
     size = lax.axis_size("mp")
     return [
         pltpu.VMEM((rows, width), jnp.float32),
         pltpu.VMEM((2, size, rows, width), jnp.bfloat16),
         pltpu.VMEM((2, size, rows, width), jnp.bfloat16),
-        pltpu.SemaphoreType.DMA((2, 2 * size)),
+        pltpu.SemaphoreType.DMA((2, 2 * size * chunks)),
     ]
 
 
@@ -568,47 +610,55 @@
     return size & (size - 1) == 0 and block % 128 == 0
 
 
-def open_step(middle, locals_, arrays, dims, small, collective_id):
-    if not direct(arrays[0].shape[dims[0]]):
-        mids, normed = middle(None, *locals_)
-        whole = [
-            lax.all_gather(array, "dp", axis=dim, tiled=True) for array, dim in zip(arrays, dims)
-        ]
-        return (
-            mids,
-            lax.all_gather(normed, "mp", axis=0, tiled=True),
-            whole,
-            lax.all_gather(small, "dp", axis=1, tiled=True),
-        )
-    size, lanes = lax.axis_size("dp"), small.shape[1]
-    arrays = [*arrays, jnp.pad(small, ((0, 16 - small.shape[0]), (0, 128 - lanes)))]
-    dims = (*dims, 0)
-    ways = [index % 2 == 1 for index in range(len(dims))]
-    mid_shapes, normed_shape = jax.eval_shape(functools.partial(middle, None), *locals_)
-    outs = []
+def fetched_shapes(arrays, dims):
+    size, shapes = lax.axis_size("dp"), []
     for array, dim in zip(arrays, dims):
         shape = list(array.shape)
         shape[dim] *= size
-        outs.append(jax.ShapeDtypeStruct(tuple(shape), array.dtype))
+        shapes.append(jax.ShapeDtypeStruct(tuple(shape), array.dtype))
+    return shapes
+
+
+def plain_fetch(arrays, dims):
+    return [lax.all_gather(array, "dp", axis=dim, tiled=True) for array, dim in zip(arrays, dims)]
+
+
+def packed_rows(small):
+    return jnp.pad(small, ((0, 16 - small.shape[0]), (0, 128 - small.shape[1])))
+
+
+def whole_rows(packed, small):
+    size, (count, lanes) = lax.axis_size("dp"), small.shape
+    packed = packed.reshape(size, 16, 128)[:, :count, :lanes]
+    return packed.transpose(1, 0, 2).reshape(count, size * lanes)
+
+
+def open_step(middle, locals_, arrays, dims, collective_id):
+    if not direct(arrays[0].shape[dims[0]]):
+        mids, normed = middle(None, *locals_)
+        return mids, lax.all_gather(normed, "mp", axis=0, tiled=True), plain_fetch(arrays, dims)
+    ways = [index % 2 == 1 for index in range(len(dims))]
+    mid_shapes, normed_shape = jax.eval_shape(functools.partial(middle, None), *locals_)
     rows, width = normed_shape.shape
     whole_shape = jax.ShapeDtypeStruct((rows * lax.axis_size("mp"), width), normed_shape.dtype)
+    count = len(mid_shapes)
     result = call_step(
-        functools.partial(open_kernel, middle, (len(locals_), len(mid_shapes)), dims, ways),
+        functools.partial(open_kernel, middle, (len(locals_), count), CHUNKS, dims, ways),
         [*locals_, *arrays],
-        [*mid_shapes, whole_shape, *outs],
+        [*mid_shapes, whole_shape, *fetched_shapes(arrays, dims)],
         [
-            pltpu.SemaphoreType.DMA((2, 2 * (lax.axis_size("mp") - 1))),
-            pltpu.SemaphoreType.DMA((2, len(arrays) * (size - 1))),
+            pltpu.SemaphoreType.DMA((2, 2 * (lax.axis_size("mp") - 1) * CHUNKS)),
+            pltpu.SemaphoreType.DMA((2, len(arrays) * (lax.axis_size("dp") - 1))),
         ],
         collective_id,
         "open_step",
     )
-    mids, (whole, *fetched, packed) = result[: len(mid_shapes)], result[len(mid_shapes) :]
-    packed = packed.reshape(size, 16, 128)[:, : small.shape[0], :lanes]
-    return mids, whole, fetched, packed.transpose(1, 0, 2).reshape(small.shape[0], size * lanes)
-
-
-def between_step(middle, partial_value, locals_, grads, dims, ways, collective_id):
+    return result[:count], result[count], result[count + 1 :]
+
+
+def between_step(
+    middle, partial_value, locals_, collective_id, grads=(), fetch=(), dims=(), ways=()
+):
     partial_value = partial_value.astype(jnp.bfloat16)
     grads = [grad.astype(jnp.bfloat16) for grad in grads]
     size = lax.axis_size("mp")
@@ -616,20 +666,29 @@
     if not direct(width // lax.axis_size("dp")):
         total = lax.psum_scatter(partial_value, "mp", scatter_dimension=0, tiled=True)
         mids, normed = middle(total.astype(jnp.float32), *locals_)
-        return mids, lax.all_gather(normed, "mp", axis=0, tiled=True), plain_totals(grads, dims)
+        others = plain_fetch(fetch, dims) if fetch else plain_totals(grads, dims)
+        return mids, lax.all_gather(normed, "mp", axis=0, tiled=True), others
     total = jax.ShapeDtypeStruct((rows, width), jnp.float32)
     mid_shapes, normed_shape = jax.eval_shape(middle, total, *locals_)
-    shapes, slots = cube_scratch(grads, dims)
+    if fetch:
+        shapes = fetched_shapes(fetch, dims)
+        scratch = [pltpu.SemaphoreType.DMA((2, len(fetch) * (lax.axis_size("dp") - 1)))]
+    else:
+        shapes, scratch = cube_scratch(grads, dims)
     count = len(mid_shapes)
     result = call_step(
-        functools.partial(between_kernel, middle, (len(locals_), count), True, dims, ways),
-        [partial_value, *locals_, *grads],
+        functools.partial(
+            between_kernel, middle, (len(locals_), count), CHUNKS, bool(fetch), dims, ways
+        ),
+        [partial_value, *locals_, *grads, *fetch],
         [
             *mid_shapes,
             jax.ShapeDtypeStruct((rows * size, width), normed_shape.dtype),
             *shapes,
         ],
-        line_scratch(rows, width) + [pltpu.SemaphoreType.DMA((2, 2 * (size - 1)))] + slots,
+        line_scratch(rows, width, CHUNKS)
+        + [pltpu.SemaphoreType.DMA((2, 2 * (size - 1) * CHUNKS))]
+        + scratch,
         collective_id,
         "between_step",
     )
@@ -652,10 +711,10 @@
     shapes, slots = cube_scratch(grads, dims)
     count = len(mid_shapes)
     result = call_step(
-        functools.partial(close_kernel, middle, (len(locals_), count), dims, ways),
+        functools.partial(close_kernel, middle, (len(locals_), count), CHUNKS, dims, ways),
         [partial_value, small, gains, *locals_, *grads],
         [*mid_shapes, *shapes_of([small]), gains_shape, *shapes],
-        line_scratch(rows, width)
+        line_scratch(rows, width, CHUNKS)
         + [
             pltpu.VMEM((dp_size, *small.shape), jnp.float32),
             pltpu.SemaphoreType.DMA((2, dp_size - 1)),
@@ -999,45 +1058,46 @@
     mask_col = valid_keys.astype(jnp.float32)[:, None]
     frame_count = jnp.sum(lengths).astype(jnp.float32)
     frames = frames_in.reshape(local_rows, model_width)
-    _, whole_first, fetched, small = open_step(
-        open_middle,
+    _, whole_first, ffn_first = open_step(
+        open_middle, [frames, norm_gains], [ffn1_up, ffn1_down], (0, 1), 0
+    )
+    ffn_second = (
+        lax.all_gather(ffn2_up, "dp", axis=0, tiled=True),
+        lax.all_gather(ffn2_down, "dp", axis=1, tiled=True),
+    )
+    attn_in_whole = lax.all_gather(
+        attn_in.reshape(attn_in.shape[0], -1), "dp", axis=0, tiled=True
+    )
+    conv_in_whole = lax.all_gather(conv_in, "dp", axis=0, tiled=True)
+    small = jnp.concatenate([pos_bias, depthwise, bn_scale[None], bn_shift[None]], axis=0)
+    table_low = position_table(seq_len, model_width).astype(jnp.bfloat16)
+    if direct(model_width // lax.axis_size("dp")):
+        packed = packed_rows(small)
+    else:
+        packed = small.T
+    (after_first,), whole_attn, (pos_whole, attn_out_whole, conv_out_whole, packed) = between_step(
+        functools.partial(forward_middle, 0.5, 1),
+        ffn_forward(whole_first, ffn_first),
         [frames, norm_gains],
-        [ffn1_up, ffn1_down, pos_proj, attn_out, conv_out],
-        (0, 1, 0, 1, 1),
-        jnp.concatenate([pos_bias, depthwise, bn_scale[None], bn_shift[None]], axis=0),
-        0,
-    )
-    up_one, down_one, pos_whole, attn_out_whole, conv_out_whole = fetched
+        1,
+        fetch=[pos_proj, attn_out, conv_out, packed],
+        dims=(0, 1, 1, 0),
+        ways=(False, True, False, True),
+    )
+    if direct(model_width // lax.axis_size("dp")):
+        small = whole_rows(packed, small)
+    else:
+        small = packed.T
     taps = depthwise.shape[0]
-    ffn_first = (up_one, down_one)
-    attn_held = (
-        lax.all_gather(attn_in.reshape(attn_in.shape[0], -1), "dp", axis=0, tiled=True),
-        pos_whole,
-        small[:2],
-        attn_out_whole,
-    )
+    attn_held = (attn_in_whole, pos_whole, small[:2], attn_out_whole)
     conv_held = (
-        lax.all_gather(conv_in, "dp", axis=0, tiled=True),
+        conv_in_whole,
         small[2 : 2 + taps],
         small[2 + taps],
         small[3 + taps],
         conv_out_whole,
     )
-    ffn_second = (
-        lax.all_gather(ffn2_up, "dp", axis=0, tiled=True),
-        lax.all_gather(ffn2_down, "dp", axis=1, tiled=True),
-    )
-    table_low = position_table(seq_len, model_width).astype(jnp.bfloat16)
     position = matmul(table_low, pos_whole).astype(jnp.bfloat16)
-    (after_first,), whole_attn, _ = between_step(
-        functools.partial(forward_middle, 0.5, 1),
-        ffn_forward(whole_first, ffn_first),
-        [frames, norm_gains],
-        [],
-        (),
-        (),
-        1,
-    )
     attn_partial, *attn_saved = attention_forward(
         whole_attn, attn_held, position, own_length[None]
     )
@@ -1045,9 +1105,6 @@
         functools.partial(forward_middle, 1.0, 2),
         attn_partial,
         [after_first, norm_gains],
-        [],
-        (),
-        (),
         2,
     )
     gate_value, logistic, padded, conved = conv_front(
@@ -1059,18 +1116,12 @@
         functools.partial(forward_middle, 1.0, 3),
         matmul(active, conv_held[4]),
         [after_attn, norm_gains],
-        [],
-        (),
-        (),
         3,
     )
     (block_out, d_second, gain_five), whole_grads, _ = between_step(
         turn_middle,
         ffn_forward(whole_second, ffn_second),
         [after_conv, norm_gains, out_grad.reshape(local_rows, model_width)],
-        [],
-        (),
-        (),
         4,
     )
     d_normed, grad_up, grad_down = ffn_backward(whole_second, ffn_second, whole_grads)
@@ -1078,10 +1129,10 @@
         functools.partial(backward_middle, 1.0, 3),
         d_normed,
         [after_conv, norm_gains, d_second],
-        [grad_up, grad_down],
-        (0, 1),
-        (False, True),
         5,
+        grads=[grad_up, grad_down],
+        dims=(0, 1),
+        ways=(False, True),
     )
     d_normed, grad_conv_in, grad_kernel, grad_conv_out, gain_total, bias_total = conv_backward(
         whole_conv, conv_held, mask_col, stats, frame_count, whole_grads
@@ -1090,10 +1141,10 @@
         functools.partial(backward_middle, 1.0, 2),
         d_normed,
         [after_attn, norm_gains, d_conv],
-        [grad_conv_in.reshape(model_width, -1), grad_conv_out],
-        (0, 1),
-        (False, True),
         6,
+        grads=[grad_conv_in.reshape(model_width, -1), grad_conv_out],
+        dims=(0, 1),
+        ways=(False, True),
     )
     d_normed, grad_attn_in, grad_pos, grad_bias, grad_attn_out = attention_backward(
         whole_attn, attn_held, table_low, position, attn_saved, whole_grads
@@ -1102,10 +1153,10 @@
         functools.partial(backward_middle, 0.5, 1),
         d_normed,
         [after_first, norm_gains, d_attn],
-        [grad_attn_in, grad_attn_out, grad_pos],
-        (0, 1, 0),
-        (False, True, True),
         7,
+        grads=[grad_attn_in, grad_attn_out, grad_pos],
+        dims=(0, 1, 0),
+        ways=(False, True, True),
     )
     d_normed, grad_up, grad_down = ffn_backward(whole_first, ffn_first, whole_grads)
     (in_grad,), small_grads, gains, (total_up_one, total_down_one) = close_step(

time: 558 us -> 512 us (0.918); the launches traced: 549 us -> 509 us
  Pallas kernels: 439 us -> 401 us
    pallas_call x9, Pallas kernels: 404 us -> 365 us  [call_step(): pl.pallas_call(kernel, out_shape=out_shape, in_specs=[vmem] * len(inputs)...]
    unnamed x93 -> x101, local copies, waits for them, and re-layouts: 14.4 us -> 13.1 us
  transfers between devices with their start and end apart: 4 -> 4, of which waited for: 0 -> 0; matrix products, arithmetic and copies ran while one was open for 5% -> 5% of each run, Pallas kernels for 35% -> 33%
where the time goes in v5:
time: 512 us; the launch traced here: 509 us
  Pallas kernels  401 us (78%)
  matrix products  58.9 us (12%)
  local copies, waits for them, and re-layouts  22.3 us (4%)
  between operations  15.2 us (3%)
  other arithmetic  9.43 us (2%)
    pallas_call x9, Pallas kernels, call_step(): pl.pallas_call(kernel, out_shape=out_shape, in_specs=[vmem] * len(inputs)...  365 us
    dot_general x9, matrix products, contract_rows(): lax.dot_general(left, right, (((0,), (0,)), ((), ())), preferred_element_...  21.9 us
    dot_general x7, matrix products, matmul(): return jnp.dot(left, right, preferred_element_type=jnp.float32)  20.7 us
    dot_general x7, matrix products, contract_cols(): lax.dot_general(left, right, (((1,), (1,)), ((), ())), preferred_element_...  16.4 us
    unnamed x101, local copies, waits for them, and re-layouts  13.1 us
    pallas_call x2, Pallas kernels, all_total(): pl.pallas_call(functools.partial(all_total_kernel, axis), out_shape=jax.S...  13.1 us
    pallas_call x1, Pallas kernels, attention_backward(): pl.pallas_call(functools.partial(attention_back_kernel, HEAD ** (-0.5)),...  12.7 us
    pallas_call x1, Pallas kernels, attention_forward(): pl.pallas_call(functools.partial(attention_kernel, HEAD ** (-0.5)), grid=...  10.4 us
  transfers between devices with their start and end apart: 4, of which 0 were waited for; matrix products, arithmetic and copies ran while one was open for 5% of the time, Pallas kernels for 33%

profile of v5, /device:TPU:0, one launch (start us, length us, event | category | flops | bytes accessed | tf_op | source)
XLA Modules:
  0.0 508.9 jit_solution(10056376552010109947)
XLA Ops:
  8.0 1.1 copy.42
  9.0 0.8 copy.43
  11.2 36.2 %open_step.1 = (bf16[512,1024]{1,0:T(8,128)(2,1)}, bf16[1024,1024]{1,0:T(8,128)(2,1)}, bf16[1024,1024]{1,0:T(8,128)(2,1)}) custom-call(bf16[128,1024]{1,0:T(8,128)(2,1)} %bitcast.73, f32[5,1024]{1,0:T(8,128)} %refs_4_.3, bf16[128,1024]{1,0:T(8,128)(2,1)} %refs_2_.8, bf16[1024,128]{1,0:T(8,128)(2,1)} %refs_3_.2), custom_call_target="tpu_custom_call" | custom-call | tf_op jit(solution)/shard_map/open_step/pallas_call | solution.py:565
  47.4 3.4 fusion.37
  50.9 2.3 convolution_convert_fusion.10.refs_0_
  53.8 39.5 %between_step.7 = (f32[128,1024]{1,0:T(8,128)}, bf16[512,1024]{1,0:T(8,128)(2,1)}, bf16[1024,256]{1,0:T(8,128)(2,1)}, bf16[256,1024]{1,0:T(8,128)(2,1)}, bf16[25...) custom-call(bf16[512,1024]{1,0:T(8,128)(2,1)} %convolution_convert_fusion.10.refs_0_, bf16[128,1024]{1,0:T(8,128)(2,1)} %bitcast.74, ...), custom_call_target="tpu_custom_call" | custom-call | tf_op jit(solution)/shard_map/between_step/pallas_call | solution.py:565
  93.3 0.8 copy.49
  98.0 1.0 fusion.5
  99.6 1.4 copy-done.1
  101.0 1.5 convolution_convert_fusion.16.position_ref
  102.5 1.4 copy.47
  104.0 10.4 %attention_forward.1 = (bf16[512,1024]{1,0:T(8,128)(2,1)}, f32[2,512,512]{2,1,0:T(8,128)}, bf16[512,256]{1,0:T(8,128)(2,1)}, bf16[512,256]{1,0:T(8,128)(2,1)}, b...) custom-call(s32[1]{0:T(128)} %dynamic_slice.16.length_ref, ...), custom_call_target="tpu_custom_call" | custom-call | tf_op jit(solution)/shard_map/attention_forward/pallas_call | solution.py:847
  114.4 35.8 %between_step.8 = (f32[128,1024]{1,0:T(8,128)}, bf16[512,1024]{1,0:T(8,128)(2,1)}) custom-call(bf16[512,1024]{1,0:T(8,128)(2,1)} %get-tuple-element.71.refs_0_, f32[128,1024]{1,0:T(8,128)} %get-tuple-element.72.refs_1_, f32[5,1024]{1,0:T(8,128)} %refs_4_.3), custom_call_target="tpu_custom_call" | custom-call | tf_op jit(solution)/shard_map/between_step/pallas_call | solution.py:565
  150.2 1.9 fusion.38
  153.3 7.2 %all_total.2 = f32[2,256]{1,0:T(2,128)} custom-call(f32[2,256]{1,0:T(2,128)} %pad_maximum_fusion.5.in_ref), custom_call_target="tpu_custom_call" | custom-call | tf_op jit(solution)/shard_map/all_total/pallas_call | solution.py:128
  161.2 2.6 convolution_convert_fusion.9.refs_0_
  163.7 37.9 %between_step.9 = (f32[128,1024]{1,0:T(8,128)}, bf16[512,1024]{1,0:T(8,128)(2,1)}) custom-call(bf16[512,1024]{1,0:T(8,128)(2,1)} %convolution_convert_fusion.9.refs_0_, f32[128,1024]{1,0:T(8,128)} %get-tuple-element.75.refs_1_, f32[5,1024]{1,0:T(8,128)} %refs_4_.3), custom_call_target="tpu_custom_call" | custom-call | tf_op jit(solution)/shard_map/between_step/pallas_call | solution.py:565
  201.7 4.5 fusion.39
  206.2 4.5 convolution_convert_fusion.8.refs_0_
  210.7 38.1 %between_step.10 = (bf16[128,1024]{1,0:T(8,128)(2,1)}, f32[128,1024]{1,0:T(8,128)}, f32[1,1024]{1,0:T(1,128)}, bf16[512,1024]{1,0:T(8,128)(2,1)}) custom-call(bf16[512,1024]{1,0:T(8,128)(2,1)} %convolution_convert_fusion.8.refs_0_, f32[128,1024]{1,0:T(8,128)} %get-tuple-element.77.refs_1_, f32[5,1024]{1,0:T(8,128)} %refs_4_.3, bf16[128,1024]{1,0:T(8,128)(2,1)} %bitcast.84), custom_call_target="tpu_custom_call" | custom-call | tf_op jit(solution)/shard_map/between_step/pallas_call | solution.py:565
  248.9 4.6 convolution_convert_fusion.2.refs_5_
  253.6 1.6 multiply_convert_fusion.1
  255.2 2.6 convolution_convert_fusion.3.refs_4_
  257.8 2.3 convolution_convert_fusion.7.refs_0_
  260.2 55.7 %between_step.11 = (f32[128,1024]{1,0:T(8,128)}, f32[1,1024]{1,0:T(1,128)}, bf16[512,1024]{1,0:T(8,128)(2,1)}, f32[128,1024]{1,0:T(8,128)}, f32[1024,128]{1,0:T(8,128)}) custom-call(bf16[512,1024]{1,0:T(8,128)(2,1)} %convolution_convert_fusion.7.refs_0_, f32[128,1024]{1,0:T(8,128)} %get-tuple-element.77.refs_1_, f32[5,1024]{1,0:T(8,128)} %refs_4_.3, ...), custom_call_target="tpu_custom_call" | custom-call | tf_op jit(solution)/shard_map/between_step/pallas_call | solution.py:565
  315.9 2.7 fusion.33
  318.6 1.3 convolution_convert_fusion.14.refs_5_
  320.5 5.9 %all_total.3 = f32[2,256]{1,0:T(2,128)} custom-call(f32[2,256]{1,0:T(2,128)} %pad_maximum_fusion.6.in_ref), custom_call_target="tpu_custom_call" | custom-call | tf_op jit(solution)/shard_map/all_total/pallas_call | solution.py:128
  327.2 1.5 multiply_reduce_fusion
  329.9 1.7 convolution_convert_fusion.11.refs_4_
  331.7 1.8 convolution_convert_fusion.12.refs_0_
  333.4 39.7 %between_step.12 = (f32[128,1024]{1,0:T(8,128)}, f32[1,1024]{1,0:T(1,128)}, bf16[512,1024]{1,0:T(8,128)(2,1)}, f32[128,512]{1,0:T(8,128)}, f32[256,128]{1,0:T(8,128)}) custom-call(bf16[512,1024]{1,0:T(8,128)(2,1)} %convolution_convert_fusion.12.refs_0_, f32[128,1024]{1,0:T(8,128)} %get-tuple-element.75.refs_1_, f32[5,1024]{1,0:T(8,128)} %refs_4_.3, ...), custom_call_target="tpu_custom_call" | custom-call | tf_op jit(solution)/shard_map/between_step/pallas_call | solution.py:565
  373.1 12.7 %attention_backward.1 = (bf16[512,768]{1,0:T(8,128)(2,1)}, bf16[1024,256]{1,0:T(8,128)(2,1)}, f32[2,256]{1,0:T(2,128)}) custom-call(bf16[512,1024]{1,0:T(8,128)(2,1)} %get-tuple-element.83.grad_ref, bf16[256,1024]{1,0:T(8,128)(2,1)} %get-tuple-element.70.out_w_ref, f32[2,512,512]{2,1,0:T(8,128)} %get-tuple-element.84.probs_ref, ...), custom_call_target="tpu_custom_call" | custom-call | tf_op jit(solution)/shard_map/attention_backward/pallas_call | solution.py:926
  385.9 2.8 convolution_convert_fusion.15.refs_6_
  388.6 1.3 convolution_convert_fusion.13.refs_5_
  389.9 2.2 convolution_convert_fusion.4.refs_4_
  392.1 2.0 convolution_convert_fusion.5.refs_0_
  394.1 41.9 %between_step.13 = (f32[128,1024]{1,0:T(8,128)}, f32[1,1024]{1,0:T(1,128)}, bf16[512,1024]{1,0:T(8,128)(2,1)}, f32[128,768]{1,0:T(8,128)}, f32[256,128]{1,0:T(8,128)}, /*index=5*/f32[128,256]{1,0:T(8,128)}) custom-call(bf16[512,1024]{1,0:T(8,128)(2,1)} %convolution_convert_fusion.5.refs_0_, f32[128,1024]{1,0:T(8,128)} %get-tuple-element.72.refs_1_, ...), custom_call_target="tpu_custom_call" | custom-call | tf_op jit(solution)/shard_map/between_step/pallas_call | solution.py:565
  436.0 3.7 multiply_convert_fusion
  439.7 2.3 convolution_convert_fusion.6.refs_0_
  442.0 2.6 convolution_convert_fusion.1.refs_6_
  444.7 2.7 convolution_convert_fusion.refs_7_
  449.2 40.1 %close_step.1 = (f32[128,1024]{1,0:T(8,128)}, f32[7,256]{1,0:T(8,128)}, f32[5,1024]{1,0:T(8,128)}, f32[128,1024]{1,0:T(8,128)}, f32[1024,128]{1,0:T(8,128)}) custom-call(bf16[512,1024]{1,0:T(8,128)(2,1)} %convolution_convert_fusion.6.refs_0_, f32[7,256]{1,0:T(8,128)} %concatenate.18.refs_1_, f32[4,1024]{1,0:T(4,128)} %pad_maximum_fusion.4.refs_2_, ...), custom_call_target="tpu_custom_call" | custom-call | tf_op jit(solution)/shard_map/close_step/pallas_call | solution.py:565
  489.4 0.9 constant_dynamic-slice_fusion.2
  492.9 0.9 reshape.293
  494.0 0.9 copy.45
  496.2 0.8 copy.60
  497.0 0.8 copy.61
  (145 shorter events, 21.5 us)
Async XLA Ops:
  7.2 95.4 %all-gather.7.cloned.1.call-start = ((), (), s32[]{:S(2)}) async-start(), calls=%async_computation.1 | async-start | bytes 1179648 | tf_op jit(solution)/shard_map/all_gather | solution.py:1071
  7.9 96.1 %all-gather.5.cloned.1.call-start = ((), (), s32[]{:S(2)}) async-start(), calls=%async_computation | async-start | bytes 1769472 | tf_op jit(solution)/shard_map/all_gather | solution.py:1068
  9.9 191.8 %all-gather.9.cloned.1.call-start = ((), (), s32[]{:S(2)}) async-start(), calls=%async_computation.2 | async-start | bytes 2359296 | tf_op jit(solution)/shard_map/all_gather | solution.py:1065
  10.6 195.6 %all-gather.11.cloned.1.call-start = ((), (), s32[]{:S(2)}) async-start(), calls=%async_computation.3 | async-start | bytes 2359296 | tf_op jit(solution)/shard_map/all_gather | solution.py:1066
  47.4 3.4 copy-start.27
  50.8 2.3 copy-start.41
  50.8 2.3 copy-start.22
  50.8 2.3 copy-start.23
  50.8 2.3 copy-start.24
  50.9 2.3 copy-start.25
  50.9 43.4 %copy-start.40 = (s32[8]{0:T(128)S(1)}, s32[8]{0:T(128)}, u32[]{:S(2)}) copy-start(s32[8]{0:T(128)} %param.18) | copy-start | bytes 100
  93.3 7.8 %copy-start.39 = (bf16[1024,256]{1,0:T(8,128)(2,1)S(1)}, bf16[1024,256]{1,0:T(8,128)(2,1)}, u32[]{:S(2)}) copy-start(bf16[1024,256]{1,0:T(8,128)(2,1)} %get-tuple-element.69) | copy-start | bytes 1572868
  99.6 1.4 copy-start.1
  248.9 4.7 copy-start.30
  248.9 4.7 copy-start.36
  248.9 4.7 copy-start.43
  253.6 1.6 copy-start.33
  255.2 2.6 copy-start.29
  260.2 55.7 %copy-start.38 = (bf16[256,1024]{1,0:T(8,128)(2,1)S(1)}, bf16[256,1024]{1,0:T(8,128)(2,1)}, u32[]{:S(2)}) copy-start(bf16[256,1024]{1,0:T(8,128)(2,1)} %get-tuple-element.74) | copy-start | bytes 1572868
  315.9 2.7 copy-start.35
  328.7 1.2 copy-start.32
  373.1 12.7 %copy-start.2 = (bf16[32,32,1024]{2,1,0:T(8,128)(2,1)S(1)}, bf16[32,32,1024]{2,1,0:T(8,128)(2,1)}, u32[]{:S(2)}) copy-start(bf16[32,32,1024]{2,1,0:T(8,128)(2,1)} %copy-done.1) | copy-start | bytes 6291460
  385.8 2.8 copy-start
  385.8 2.8 copy-start.11
  385.8 4.1 copy-start.4
  385.8 4.0 copy-start.37
  389.9 2.2 copy-start.3
  394.1 41.9 %copy-start.28 = (bf16[1024,1024]{1,0:T(8,128)(2,1)S(1)}, bf16[1024,1024]{1,0:T(8,128)(2,1)}, u32[]{:S(2)}) copy-start(bf16[1024,1024]{1,0:T(8,128)(2,1)} %get-tuple-element.66) | copy-start | bytes 6291460
  436.0 3.7 copy-start.26
  439.7 2.3 copy-start.31
  442.0 2.7 copy-start.34
  442.0 2.7 copy-start.42
  444.6 3.3 copy-start.17
  444.6 3.3 copy-start.18
  444.6 3.3 copy-start.19
  444.6 3.3 copy-start.20
  444.7 3.9 copy-start.21
  449.2 43.7 %copy-start.13 = (f32[128,512]{1,0:T(8,128)S(1)}, f32[128,512]{1,0:T(8,128)}, u32[]{:S(2)}) copy-start(f32[128,512]{1,0:T(8,128)} %get-tuple-element.108) | copy-start | bytes 786436
  449.2 44.6 %copy-start.10 = (f32[128,768]{1,0:T(8,128)S(1)}, f32[128,768]{1,0:T(8,128)}, u32[]{:S(2)}) copy-start(f32[128,768]{1,0:T(8,128)} %get-tuple-element.104) | copy-start | bytes 1179652
  489.4 6.2 %copy-start.12 = (bf16[128,1024]{1,0:T(8,128)(2,1)S(1)}, bf16[128,1024]{1,0:T(8,128)(2,1)}, u32[]{:S(2)}) copy-start(bf16[128,1024]{1,0:T(8,128)(2,1)} %get-tuple-element.78) | copy-start | bytes 786436
  489.4 6.9 %copy-start.9 = (f32[128,1024]{1,0:T(8,128)S(1)}, f32[128,1024]{1,0:T(8,128)}, u32[]{:S(2)}) copy-start(f32[128,1024]{1,0:T(8,128)} %get-tuple-element.100) | copy-start | bytes 1572868
  489.4 7.7 %copy-start.8 = (f32[128,1024]{1,0:T(8,128)S(1)}, f32[128,1024]{1,0:T(8,128)}, u32[]{:S(2)}) copy-start(f32[128,1024]{1,0:T(8,128)} %get-tuple-element.213) | copy-start | bytes 1572868
  493.8 4.0 copy-start.7
  494.0 4.7 copy-start.16
  494.9 4.4 copy-start.15
  495.5 4.4 copy-start.14
  495.5 5.1 copy-start.6
  497.0 4.4 copy-start.5
Sparse Core Ops, SparseCore 0:
  9.9 28.9 all-gather.6
  41.3 26.0 all-gather.4
  69.3 28.3 all-gather.8
  99.5 28.1 all-gather.10

commit v6 on v5

--- a/solution.py
+++ b/solution.py
@@ -60,7 +60,7 @@
 
 
 MESH = pl.DeviceIdType.MESH
-VMEM_LIMIT = 60 * 1024 * 1024
+VMEM_LIMIT = 24 * 1024 * 1024
 CHUNKS = 2
 
 
@@ -279,11 +279,13 @@
             ).astype(self.staged.dtype)
             self.arrived(way, owner, chunk).start()
 
-    def run(self):
+    def run(self, halfway=None):
         marks = [(step, chunk) for step in range(self.size - 1) for chunk in range(self.chunks)]
         for mark in marks:
             self.lead(*mark)
         for number in range(len(marks) + self.chunks):
+            if halfway and number == len(marks) // 2 + 1:
+                halfway()
             if number < len(marks):
                 self.hop(self.first_way, *marks[number])
             if number >= self.chunks:
@@ -491,8 +493,10 @@
     stage = 0
     if stages:
         beside.step(0)
-        stage = 1
-    sums.run()
+        sums.run(lambda: beside.step(1))
+        stage = 2
+    else:
+        sums.run()
     for chunk in range(chunks):
         lines = sums.lines(chunk)
         picked = [ref[lines] if ref.shape[0] == sums.rows else ref[...] for ref in locals_]
@@ -537,8 +541,7 @@
     greet("mp", "dp", True)
     little.start()
     grads.step(0)
-    sums.run()
-    grads.step(1)
+    sums.run(lambda: grads.step(1))
     total_rows = jnp.concatenate([sums.result(chunk) for chunk in range(chunks)], axis=0)
     values, gain = middle(total_rows, *[ref[...] for ref in locals_])
     near.slots[near.me] = jnp.concatenate([gains[...], gain], axis=0)
@@ -955,8 +958,8 @@
 
 def conv_front(whole, w_in, kernel, mask_col):
     seq_len, model_width = whole.shape
-    local_width = w_in.shape[2]
-    glu_in = matmul(whole, w_in.reshape(model_width, 2 * local_width))
+    local_width = w_in.shape[1] // 2
+    glu_in = matmul(whole, w_in)
     gate_value = glu_in[:, :local_width]
     logistic = jax.nn.sigmoid(glu_in[:, local_width:])
     glu_out = gate_value * logistic * mask_col
@@ -990,7 +993,6 @@
 def conv_backward(whole, weights, mask_col, stats, frame_count, grad_whole):
     w_in, kernel, bn_gain, bn_bias, w_out = weights
     seq_len, model_width = whole.shape
-    local_width = w_in.shape[2]
     gate_value, logistic, padded, conved = conv_front(whole, w_in, kernel, mask_col)
     normed_b, active = conv_tail(conved, stats, bn_gain, bn_bias)
     average, inv_std = stats
@@ -1026,8 +1028,8 @@
     d_pair = jnp.concatenate(
         [d_glu * logistic, d_glu * gate_value * logistic * (1.0 - logistic)], axis=1
     ).astype(jnp.bfloat16)
-    grad_in = contract_rows(whole, d_pair).reshape(model_width, 2, local_width)
-    d_normed_in = contract_cols(d_pair, w_in.reshape(model_width, 2 * local_width))
+    grad_in = contract_rows(whole, d_pair)
+    d_normed_in = contract_cols(d_pair, w_in)
     return (d_normed_in, grad_in, grad_kernel, grad_out, gain_total, bias_total)
 
 
@@ -1061,28 +1063,20 @@
     _, whole_first, ffn_first = open_step(
         open_middle, [frames, norm_gains], [ffn1_up, ffn1_down], (0, 1), 0
     )
-    ffn_second = (
-        lax.all_gather(ffn2_up, "dp", axis=0, tiled=True),
-        lax.all_gather(ffn2_down, "dp", axis=1, tiled=True),
-    )
-    attn_in_whole = lax.all_gather(
-        attn_in.reshape(attn_in.shape[0], -1), "dp", axis=0, tiled=True
-    )
-    conv_in_whole = lax.all_gather(conv_in, "dp", axis=0, tiled=True)
     small = jnp.concatenate([pos_bias, depthwise, bn_scale[None], bn_shift[None]], axis=0)
     table_low = position_table(seq_len, model_width).astype(jnp.bfloat16)
     if direct(model_width // lax.axis_size("dp")):
         packed = packed_rows(small)
     else:
         packed = small.T
-    (after_first,), whole_attn, (pos_whole, attn_out_whole, conv_out_whole, packed) = between_step(
+    (after_first,), whole_attn, (attn_in_whole, pos_whole, attn_out_whole, packed) = between_step(
         functools.partial(forward_middle, 0.5, 1),
         ffn_forward(whole_first, ffn_first),
         [frames, norm_gains],
         1,
-        fetch=[pos_proj, attn_out, conv_out, packed],
-        dims=(0, 1, 1, 0),
-        ways=(False, True, False, True),
+        fetch=[attn_in.reshape(attn_in.shape[0], -1), pos_proj, attn_out, packed],
+        dims=(0, 0, 1, 0),
+        ways=(False, True, True, True),
     )
     if direct(model_width // lax.axis_size("dp")):
         small = whole_rows(packed, small)
@@ -1090,34 +1084,40 @@
         small = packed.T
     taps = depthwise.shape[0]
     attn_held = (attn_in_whole, pos_whole, small[:2], attn_out_whole)
-    conv_held = (
-        conv_in_whole,
+    conv_small = (
         small[2 : 2 + taps],
         small[2 + taps],
         small[3 + taps],
-        conv_out_whole,
     )
     position = matmul(table_low, pos_whole).astype(jnp.bfloat16)
     attn_partial, *attn_saved = attention_forward(
         whole_attn, attn_held, position, own_length[None]
     )
-    (after_attn,), whole_conv, _ = between_step(
+    (after_attn,), whole_conv, (conv_in_whole, conv_out_whole, down_two) = between_step(
         functools.partial(forward_middle, 1.0, 2),
         attn_partial,
         [after_first, norm_gains],
         2,
-    )
+        fetch=[conv_in.reshape(conv_in.shape[0], -1), conv_out, ffn2_down],
+        dims=(0, 1, 1),
+        ways=(False, False, True),
+    )
+    conv_held = (conv_in_whole, *conv_small, conv_out_whole)
     gate_value, logistic, padded, conved = conv_front(
         whole_conv, conv_held[0], conv_held[1], mask_col
     )
     stats = batch_stats(conved, mask_col, frame_count)
     normed_b, active = conv_tail(conved, stats, conv_held[2], conv_held[3])
-    (after_conv,), whole_second, _ = between_step(
+    (after_conv,), whole_second, (up_two,) = between_step(
         functools.partial(forward_middle, 1.0, 3),
         matmul(active, conv_held[4]),
         [after_attn, norm_gains],
         3,
-    )
+        fetch=[ffn2_up],
+        dims=(0,),
+        ways=(True,),
+    )
+    ffn_second = (up_two, down_two)
     (block_out, d_second, gain_five), whole_grads, _ = between_step(
         turn_middle,
         ffn_forward(whole_second, ffn_second),
@@ -1142,7 +1142,7 @@
         d_normed,
         [after_attn, norm_gains, d_conv],
         6,
-        grads=[grad_conv_in.reshape(model_width, -1), grad_conv_out],
+        grads=[grad_conv_in, grad_conv_out],
         dims=(0, 1),
         ways=(False, True),
     )

time: 512 us -> 442 us (0.86)
  Pallas kernels: 401 us -> 360 us
  matrix products: 58.9 us -> 31.5 us
  between operations: 15.2 us -> 2.43 us
  local copies, waits for them, and re-layouts: 22.3 us -> 27.9 us
    pallas_call x9, Pallas kernels: 365 us -> 331 us  [call_step(): pl.pallas_call(kernel, out_shape=out_shape, in_specs=[vmem] * len(inputs)...]
    dot_general x7, matrix products: 20.7 us -> 9.84 us  [matmul(): return jnp.dot(left, right, preferred_element_type=jnp.float32)]
    dot_general x9, matrix products: 21.9 us -> 11.7 us  [contract_rows(): lax.dot_general(left, right, (((0,), (0,)), ((), ())), preferred_element_...]
    unnamed x101 -> x155, local copies, waits for them, and re-layouts: 13.1 us -> 21.5 us
    dot_general x7, matrix products: 16.4 us -> 9.98 us  [contract_cols(): lax.dot_general(left, right, (((1,), (1,)), ((), ())), preferred_element_...]
  transfers between devices with their start and end apart: 4 -> 0, of which waited for: 0 -> 0; matrix products, arithmetic and copies ran while one was open for 5% -> 0% of each run, Pallas kernels for 33% -> 0%
where the time goes in v6:
time: 442 us; the launch traced here: 434 us
  Pallas kernels  360 us (81%)
  matrix products  31.5 us (7%)
  local copies, waits for them, and re-layouts  27.9 us (6%)
  other arithmetic  13 us (3%)
    pallas_call x9, Pallas kernels, call_step(): pl.pallas_call(kernel, out_shape=out_shape, in_specs=[vmem] * len(inputs)...  331 us
    unnamed x155, local copies, waits for them, and re-layouts  21.5 us
    pallas_call x2, Pallas kernels, all_total(): pl.pallas_call(functools.partial(all_total_kernel, axis), out_shape=jax.S...  11.8 us
    dot_general x9, matrix products, contract_rows(): lax.dot_general(left, right, (((0,), (0,)), ((), ())), preferred_element_...  11.7 us
    dot_general x7, matrix products, contract_cols(): lax.dot_general(left, right, (((1,), (1,)), ((), ())), preferred_element_...  9.98 us
    dot_general x7, matrix products, matmul(): return jnp.dot(left, right, preferred_element_type=jnp.float32)  9.84 us
    pallas_call x1, Pallas kernels, attention_backward(): pl.pallas_call(functools.partial(attention_back_kernel, HEAD ** (-0.5)),...  9.8 us

profile of v6, /device:TPU:0, one launch (start us, length us, event | category | flops | bytes accessed | tf_op | source)
XLA Modules:
  0.0 434.3 jit_solution(10527090407716748405)
XLA Ops:
  0.7 1.3 reduce_sum.92
  2.6 1.2 dynamic_slice.16.length_ref
  5.3 1.6 copy.42
  7.0 1.1 copy.36
  8.0 0.8 copy.37.refs_3_
  8.9 1.0 fusion.5
  9.9 2.0 add_convert_fusion
  11.9 30.2 %open_step.1 = (bf16[512,1024]{1,0:T(8,128)(2,1)S(1)}, bf16[1024,1024]{1,0:T(8,128)(2,1)S(1)}, bf16[1024,1024]{1,0:T(8,128)(2,1)S(1)}) custom-call(bf16[128,1024]{1,0:T(8,128)(2,1)S(1)} %bitcast.73, f32[5,1024]{1,0:T(8,128)S(1)} %copy-done, bf16[128,1024]{1,0:T(8,128)(2,1)S(1)} %copy-done.22, bf16[1024,128]{1,0:T(8,128)(2,1)S(1)} %copy-done.23), custom_call_target="tpu_custom_call" | custom-call | tf_op jit(solution)/shard_map/open_step/pallas_call | solution.py:568
  42.2 1.2 fusion.37
  44.5 1.4 copy-done.69
  45.8 1.3 convolution_convert_fusion.10.refs_0_
  47.1 36.6 %between_step.7 = (f32[128,1024]{1,0:T(8,128)S(1)}, bf16[512,1024]{1,0:T(8,128)(2,1)S(1)}, bf16[1024,768]{1,0:T(8,128)(2,1)S(1)}, bf16[1024,256]{1,0:T(8,128)(2,...) custom-call(bf16[512,1024]{1,0:T(8,128)(2,1)S(1)} %convolution_convert_fusion.10.refs_0_, ...), custom_call_target="tpu_custom_call" | custom-call | tf_op jit(solution)/shard_map/between_step/pallas_call | solution.py:568
  83.7 1.1 copy-done.4
  86.4 2.5 convolution_convert_fusion.16.position_ref
  89.0 7.0 %attention_forward.1 = (bf16[512,1024]{1,0:T(8,128)(2,1)S(1)}, f32[2,512,512]{2,1,0:T(8,128)S(1)}, bf16[512,256]{1,0:T(8,128)(2,1)S(1)}, bf16[512,256]{1,0:T(8,1...) custom-call(s32[1]{0:T(128)} %dynamic_slice.16.length_ref, ...), custom_call_target="tpu_custom_call" | custom-call | tf_op jit(solution)/shard_map/attention_forward/pallas_call | solution.py:850
  96.0 1.3 copy-done.2
  98.7 38.7 %between_step.8 = (f32[128,1024]{1,0:T(8,128)S(1)}, bf16[512,1024]{1,0:T(8,128)(2,1)S(1)}, bf16[1024,512]{1,0:T(8,128)(2,1)S(1)}, bf16[256,1024]{1,0:T(8,128)(2,1)S(1)}, bf16[1024,1024]{1,0:T(8,128)(2,1)S(1)}) custom-call(bf16[512,1024]{1,0:T(8,128)(2,1)S(1)} %get-tuple-element.76.refs_0_, f32[128,1024]{1,0:T(8,128)S(1)} %get-tuple-element.77.refs_1_, ...), custom_call_target="tpu_custom_call" | custom-call | tf_op jit(solution)/shard_map/between_step/pallas_call | solution.py:568
  139.6 1.2 multiply_reduce_fusion.7
  141.3 5.9 %all_total.2 = f32[2,256]{1,0:T(2,128)} custom-call(f32[2,256]{1,0:T(2,128)} %pad_maximum_fusion.5.in_ref), custom_call_target="tpu_custom_call" | custom-call | tf_op jit(solution)/shard_map/all_total/pallas_call | solution.py:128
  148.0 1.6 convolution_convert_fusion.9.refs_0_
  149.6 38.5 %between_step.9 = (f32[128,1024]{1,0:T(8,128)S(1)}, bf16[512,1024]{1,0:T(8,128)(2,1)S(1)}, bf16[1024,1024]{1,0:T(8,128)(2,1)S(1)}) custom-call(bf16[512,1024]{1,0:T(8,128)(2,1)S(1)} %convolution_convert_fusion.9.refs_0_, f32[128,1024]{1,0:T(8,128)S(1)} %get-tuple-element.81.refs_1_, f32[5,1024]{1,0:T(8,128)S(1)} %copy-done, bf16[128,1024]{1,0:T(8,128)(2,1)S(1)} %copy-done.24), custom_call_target="tpu_custom_call" | custom-call | tf_op jit(solution)/shard_map/between_step/pallas_call | solution.py:568
  188.1 1.3 fusion.39
  189.7 1.3 convolution_convert_fusion.8.refs_0_
  191.0 34.8 %between_step.10 = (bf16[128,1024]{1,0:T(8,128)(2,1)S(1)}, f32[128,1024]{1,0:T(8,128)S(1)}, f32[1,1024]{1,0:T(1,128)S(1)}, bf16[512,1024]{1,0:T(8,128)(2,1)S(1)}) custom-call(bf16[512,1024]{1,0:T(8,128)(2,1)S(1)} %convolution_convert_fusion.8.refs_0_, f32[128,1024]{1,0:T(8,128)S(1)} %get-tuple-element.85.refs_1_, f32[5,1024]{1,0:T(8,128)S(1)} %copy-done, ...), custom_call_target="tpu_custom_call" | custom-call | tf_op jit(solution)/shard_map/between_step/pallas_call | solution.py:568
  225.8 1.6 multiply_convert_fusion.1
  227.5 1.3 convolution_convert_fusion.7.refs_0_
  228.8 1.3 convolution_convert_fusion.3.refs_4_
  230.1 1.3 convolution_convert_fusion.2.refs_5_
  231.5 40.8 %between_step.11 = (f32[128,1024]{1,0:T(8,128)S(1)}, f32[1,1024]{1,0:T(1,128)S(1)}, bf16[512,1024]{1,0:T(8,128)(2,1)S(1)}, f32[128,1024]{1,0:T(8,128)S(1)}, f32[1024,128]{1,0:T(8,128)S(1)}) custom-call(bf16[512,1024]{1,0:T(8,128)(2,1)S(1)} %convolution_convert_fusion.7.refs_0_, f32[128,1024]{1,0:T(8,128)S(1)} %get-tuple-element.85.refs_1_, ...), custom_call_target="tpu_custom_call" | custom-call | tf_op jit(solution)/shard_map/between_step/pallas_call | solution.py:568
  272.3 1.4 fusion.33
  273.6 1.3 convolution_convert_fusion.14.refs_5_
  275.6 5.9 %all_total.3 = f32[2,256]{1,0:T(2,128)} custom-call(f32[2,256]{1,0:T(2,128)} %pad_maximum_fusion.6.in_ref), custom_call_target="tpu_custom_call" | custom-call | tf_op jit(solution)/shard_map/all_total/pallas_call | solution.py:128
  282.2 2.8 multiply_reduce_fusion
  288.6 37.3 %between_step.12 = (f32[128,1024]{1,0:T(8,128)S(1)}, f32[1,1024]{1,0:T(1,128)S(1)}, bf16[512,1024]{1,0:T(8,128)(2,1)S(1)}, f32[128,512]{1,0:T(8,128)S(1)}, f32[256,128]{1,0:T(8,128)S(1)}) custom-call(bf16[512,1024]{1,0:T(8,128)(2,1)S(1)} %convolution_convert_fusion.12.refs_0_, f32[128,1024]{1,0:T(8,128)S(1)} %get-tuple-element.81.refs_1_, ...), custom_call_target="tpu_custom_call" | custom-call | tf_op jit(solution)/shard_map/between_step/pallas_call | solution.py:568
  327.5 9.8 %attention_backward.1 = (bf16[512,768]{1,0:T(8,128)(2,1)S(1)}, bf16[1024,256]{1,0:T(8,128)(2,1)S(1)}, f32[2,256]{1,0:T(2,128)S(1)}) custom-call(bf16[512,1024]{1,0:T(8,128)(2,1)S(1)} %get-tuple-element.91.grad_ref, bf16[256,1024]{1,0:T(8,128)(2,1)S(1)} %get-tuple-element.75.out_w_ref, f32[2,512,512]{2,1,0:T(8,128)S(1)} %copy-done.3, ...), custom_call_target="tpu_custom_call" | custom-call | tf_op jit(solution)/shard_map/attention_backward/pallas_call | solution.py:929
  337.3 2.0 convolution_convert_fusion.5.refs_0_
  339.3 1.6 convolution_convert_fusion.15.refs_6_
  340.9 0.9 reshape.291
  342.3 2.3 convolution_convert_fusion.4.refs_4_
  344.7 36.9 %between_step.13 = (f32[128,1024]{1,0:T(8,128)S(1)}, f32[1,1024]{1,0:T(1,128)S(1)}, bf16[512,1024]{1,0:T(8,128)(2,1)S(1)}, f32[128,768]{1,0:T(8,128)S(1)}, f32[2...) custom-call(bf16[512,1024]{1,0:T(8,128)(2,1)S(1)} %copy-done.9, f32[128,1024]{1,0:T(8,128)S(1)} %get-tuple-element.77.refs_1_, ...), custom_call_target="tpu_custom_call" | custom-call | tf_op jit(solution)/shard_map/between_step/pallas_call | solution.py:568
  381.6 1.6 multiply_convert_fusion
  383.3 1.3 convolution_convert_fusion.6.refs_0_
  384.6 1.3 convolution_convert_fusion.1.refs_6_
  385.9 1.3 convolution_convert_fusion.refs_7_
  387.3 37.1 %close_step.1 = (f32[128,1024]{1,0:T(8,128)S(1)}, f32[7,256]{1,0:T(8,128)S(1)}, f32[5,1024]{1,0:T(8,128)S(1)}, f32[128,1024]{1,0:T(8,128)S(1)}, f32[1024,128]{1,0:T(8,128)S(1)}) custom-call(bf16[512,1024]{1,0:T(8,128)(2,1)S(1)} %convolution_convert_fusion.6.refs_0_, f32[7,256]{1,0:T(8,128)S(1)} %concatenate.18.refs_1_, ...), custom_call_target="tpu_custom_call" | custom-call | tf_op jit(solution)/shard_map/close_step/pallas_call | solution.py:568
  426.5 0.9 copy.40
  432.5 0.8 copy.61
  433.3 0.8 copy.62
  (187 shorter events, 23.3 us)
Async XLA Ops:
  5.3 6.6 %copy-start = (f32[5,1024]{1,0:T(8,128)S(1)}, f32[5,1024]{1,0:T(8,128)}, u32[]{:S(2)}) copy-start(f32[5,1024]{1,0:T(8,128)} %refs_4_.5) | copy-start | bytes 61444
  5.3 6.6 %copy-start.1 = (bf16[1,128,1024]{2,1,0:T(8,128)(2,1)S(1)}, bf16[1,128,1024]{2,1,0:T(8,128)(2,1)}, u32[]{:S(2)}) copy-start(bf16[1,128,1024]{2,1,0:T(8,128)(2,1)} %param.17) | copy-start | bytes 786436
  5.3 6.6 %copy-start.22 = (bf16[128,1024]{1,0:T(8,128)(2,1)S(1)}, bf16[128,1024]{1,0:T(8,128)(2,1)}, u32[]{:S(2)}) copy-start(bf16[128,1024]{1,0:T(8,128)(2,1)} %refs_2_.8) | copy-start | bytes 786436
  5.3 6.6 %copy-start.23 = (bf16[1024,128]{1,0:T(8,128)(2,1)S(1)}, bf16[1024,128]{1,0:T(8,128)(2,1)}, u32[]{:S(2)}) copy-start(bf16[1024,128]{1,0:T(8,128)(2,1)} %refs_3_.2) | copy-start | bytes 786436
  42.1 2.0 copy-start.52
  42.2 2.3 copy-start.56
  84.9 4.0 copy-start.7
  86.4 2.5 copy-start.5
  88.9 9.8 %copy-start.17 = (bf16[16,8,2,256]{3,1,2,0:T(8,128)(2,1)S(1)}, bf16[16,8,2,256]{3,1,2,0:T(8,128)(2,1)}, u32[]{:S(2)}) copy-start(bf16[16,8,2,256]{3,1,2,0:T(8,128)(2,1)} %copy.42) | copy-start | bytes 393220
  89.0 9.8 %copy-start.40 = (bf16[1024,128]{1,0:T(8,128)(2,1)S(1)}, bf16[1024,128]{1,0:T(8,128)(2,1)}, u32[]{:S(2)}) copy-start(bf16[1024,128]{1,0:T(8,128)(2,1)} %refs_5_.3) | copy-start | bytes 786436
  89.0 9.8 %copy-start.49 = (bf16[256,128]{1,0:T(8,128)(2,1)S(1)}, bf16[256,128]{1,0:T(8,128)(2,1)}, u32[]{:S(2)}) copy-start(bf16[256,128]{1,0:T(8,128)(2,1)} %refs_4_.4) | copy-start | bytes 196612
  98.7 39.5 %copy-start.30 = (bf16[512,256]{1,0:T(8,128)(2,1)}, bf16[512,256]{1,0:T(8,128)(2,1)S(1)}, u32[]{:S(2)}) copy-start(bf16[512,256]{1,0:T(8,128)(2,1)S(1)} %get-tuple-element.94.query_v_ref) | copy-start | bytes 786436
  98.7 39.5 %copy-start.32 = (bf16[512,256]{1,0:T(8,128)(2,1)}, bf16[512,256]{1,0:T(8,128)(2,1)S(1)}, u32[]{:S(2)}) copy-start(bf16[512,256]{1,0:T(8,128)(2,1)S(1)} %get-tuple-element.95.key_ref) | copy-start | bytes 786436
  98.7 39.5 %copy-start.34 = (bf16[512,256]{1,0:T(8,128)(2,1)}, bf16[512,256]{1,0:T(8,128)(2,1)S(1)}, u32[]{:S(2)}) copy-start(bf16[512,256]{1,0:T(8,128)(2,1)S(1)} %get-tuple-element.96.value_ref) | copy-start | bytes 786436
  137.4 1.4 copy-start.54
  137.5 1.8 copy-start.58
  137.5 2.1 copy-start.60
  138.2 2.5 copy-start.64
  140.7 8.8 %copy-start.24 = (bf16[128,1024]{1,0:T(8,128)(2,1)S(1)}, bf16[128,1024]{1,0:T(8,128)(2,1)}, u32[]{:S(2)}) copy-start(bf16[128,1024]{1,0:T(8,128)(2,1)} %refs_3_.3) | copy-start | bytes 786436
  188.1 1.6 copy-start.55
  225.8 1.7 copy-start.36
  231.4 40.8 %copy-start.67 = (f32[512,256]{1,0:T(8,128)S(1)}, f32[512,256]{1,0:T(8,128)}, u32[]{:S(2)}) copy-start(f32[512,256]{1,0:T(8,128)} %get-tuple-element.167) | copy-start | bytes 1572868
  275.0 10.6 %copy-start.65 = (f32[512,512]{1,0:T(8,128)S(1)}, f32[512,512]{1,0:T(8,128)}, u32[]{:S(2)}) copy-start(f32[512,512]{1,0:T(8,128)} %copy-done.64) | copy-start | bytes 3145732
  288.6 38.8 %copy-start.3 = (f32[2,512,512]{2,1,0:T(8,128)S(1)}, f32[2,512,512]{2,1,0:T(8,128)}, u32[]{:S(2)}) copy-start(f32[2,512,512]{2,1,0:T(8,128)} %copy-done.2) | copy-start | bytes 6291460
  288.6 38.8 %copy-start.29 = (bf16[512,256]{1,0:T(8,128)(2,1)S(1)}, bf16[512,256]{1,0:T(8,128)(2,1)}, u32[]{:S(2)}) copy-start(bf16[512,256]{1,0:T(8,128)(2,1)} %copy-done.28) | copy-start | bytes 786436
  288.6 38.8 %copy-start.31 = (bf16[512,256]{1,0:T(8,128)(2,1)S(1)}, bf16[512,256]{1,0:T(8,128)(2,1)}, u32[]{:S(2)}) copy-start(bf16[512,256]{1,0:T(8,128)(2,1)} %copy-done.30) | copy-start | bytes 786436
  288.6 38.8 %copy-start.33 = (bf16[512,256]{1,0:T(8,128)(2,1)S(1)}, bf16[512,256]{1,0:T(8,128)(2,1)}, u32[]{:S(2)}) copy-start(bf16[512,256]{1,0:T(8,128)(2,1)} %copy-done.32) | copy-start | bytes 786436
  288.6 38.8 %copy-start.35 = (bf16[512,256]{1,0:T(8,128)(2,1)S(1)}, bf16[512,256]{1,0:T(8,128)(2,1)}, u32[]{:S(2)}) copy-start(bf16[512,256]{1,0:T(8,128)(2,1)} %copy-done.34) | copy-start | bytes 786436
  327.4 9.9 %copy-start.41 = (f32[256,128]{1,0:T(8,128)}, f32[256,128]{1,0:T(8,128)S(1)}, u32[]{:S(2)}) copy-start(f32[256,128]{1,0:T(8,128)S(1)} %get-tuple-element.215) | copy-start | bytes 393220
  327.5 9.8 %copy-start.6 = (bf16[1024,768]{1,0:T(8,128)(2,1)S(1)}, bf16[1024,768]{1,0:T(8,128)(2,1)}, u32[]{:S(2)}) copy-start(bf16[1024,768]{1,0:T(8,128)(2,1)} %copy-done.4) | copy-start | bytes 4718596
  337.3 3.6 copy-start.62
  337.3 2.0 copy-start.68
  339.3 1.6 copy-start.39
  339.3 2.5 copy-start.27
  342.3 2.3 copy-start.9
  342.3 2.3 copy-start.15
  342.3 2.3 copy-start.16
  344.7 36.9 %copy-start.53 = (bf16[1024,1024]{1,0:T(8,128)(2,1)S(1)}, bf16[1024,1024]{1,0:T(8,128)(2,1)}, u32[]{:S(2)}) copy-start(bf16[1024,1024]{1,0:T(8,128)(2,1)} %copy-done.52) | copy-start | bytes 6291460
  344.7 36.9 %copy-start.70 = (f32[512,1024]{1,0:T(8,128)S(1)}, f32[512,1024]{1,0:T(8,128)}, u32[]{:S(2)}) copy-start(f32[512,1024]{1,0:T(8,128)} %copy-done.69) | copy-start | bytes 6291460
  381.6 1.7 copy-start.43
  381.6 1.7 copy-start.45
  381.6 1.7 copy-start.51
  387.3 40.1 %copy-start.37 = (bf16[128,1024]{1,0:T(8,128)(2,1)S(1)}, bf16[128,1024]{1,0:T(8,128)(2,1)}, u32[]{:S(2)}) copy-start(bf16[128,1024]{1,0:T(8,128)(2,1)} %copy-done.36) | copy-start | bytes 786436
  426.5 4.0 copy-start.46
  427.4 3.8 copy-start.44
  427.4 4.4 %copy-start.42 = (f32[256,128]{1,0:T(8,128)S(1)}, f32[256,128]{1,0:T(8,128)}, u32[]{:S(2)}) copy-start(f32[256,128]{1,0:T(8,128)} %copy-done.41) | copy-start | bytes 393220
  427.4 5.1 %copy-start.21 = (f32[128,1024]{1,0:T(8,128)S(1)}, f32[128,1024]{1,0:T(8,128)}, u32[]{:S(2)}) copy-start(f32[128,1024]{1,0:T(8,128)} %copy-done.20) | copy-start | bytes 1572868
  428.9 4.4 %copy-start.19 = (f32[1024,128]{1,0:T(8,128)S(1)}, f32[1024,128]{1,0:T(8,128)}, u32[]{:S(2)}) copy-start(f32[1024,128]{1,0:T(8,128)} %copy-done.18) | copy-start | bytes 1572868
  (23 other events, 26.9 us)

commit v7 on v6

--- a/solution.py
+++ b/solution.py
@@ -61,7 +61,7 @@
 
 MESH = pl.DeviceIdType.MESH
 VMEM_LIMIT = 24 * 1024 * 1024
-CHUNKS = 2
+CHUNKS = 4
 
 
 def line_copy(src, dst, sems, index, axis, target):
@@ -776,6 +776,31 @@
     return [upstream + d_branch], d_gain
 
 
+def store_kernel(*refs):
+    count = len(refs) // 2
+    ins, outs, sems = refs[:count], refs[count : 2 * count], refs[2 * count]
+    copies = [
+        pltpu.make_async_copy(ins[number], outs[number], sems.at[number])
+        for number in range(count)
+    ]
+    for copy in copies:
+        copy.start()
+    for copy in copies:
+        copy.wait()
+
+
+def store_all(arrays):
+    return pl.pallas_call(
+        store_kernel,
+        out_shape=shapes_of(arrays),
+        in_specs=[pl.BlockSpec(memory_space=pltpu.VMEM)] * len(arrays),
+        out_specs=[pl.BlockSpec(memory_space=pl.ANY)] * len(arrays),
+        scratch_shapes=[pltpu.SemaphoreType.DMA((len(arrays),))],
+        compiler_params=pltpu.CompilerParams(vmem_limit_bytes=VMEM_LIMIT),
+        name="store_all",
+    )(*arrays)
+
+
 def dp_total(values):
     if direct(128):
         return all_total(values, "dp", 9)
@@ -1171,6 +1196,30 @@
         8,
     )
     gain_sum = jnp.concatenate([gains[4:], gains[:4]], axis=0)
+    if direct(model_width // lax.axis_size("dp")):
+        (
+            block_out,
+            in_grad,
+            total_up_one,
+            total_down_one,
+            total_pos,
+            total_attn_out,
+            total_conv_out,
+            total_up_two,
+            total_down_two,
+        ) = store_all(
+            [
+                block_out,
+                in_grad,
+                total_up_one,
+                total_down_one,
+                total_pos,
+                total_attn_out,
+                total_conv_out,
+                total_up_two,
+                total_down_two,
+            ]
+        )
     block = model_width // lax.axis_size("dp")
     piece_len = bn_scale.shape[0]
     own = dp_index * piece_len

time: 442 us -> 430 us (0.973)
  Pallas kernels: 360 us -> 353 us
  local copies, waits for them, and re-layouts: 27.9 us -> 21.2 us
    pallas_call x9, Pallas kernels: 331 us -> 323 us  [call_step(): pl.pallas_call(kernel, out_shape=out_shape, in_specs=[vmem] * len(inputs)...]
    unnamed x155 -> x138, local copies, waits for them, and re-layouts: 21.5 us -> 14.8 us
where the time goes in v7:
time: 430 us; the launch traced here: 422 us
  Pallas kernels  353 us (82%)
  matrix products  31.5 us (7%)
  local copies, waits for them, and re-layouts  21.2 us (5%)
  other arithmetic  13 us (3%)
    pallas_call x9, Pallas kernels, call_step(): pl.pallas_call(kernel, out_shape=out_shape, in_specs=[vmem] * len(inputs)...  323 us
    unnamed x138, local copies, waits for them, and re-layouts  14.8 us
    pallas_call x2, Pallas kernels, all_total(): pl.pallas_call(functools.partial(all_total_kernel, axis), out_shape=jax.S...  11.8 us
    dot_general x9, matrix products, contract_rows(): lax.dot_general(left, right, (((0,), (0,)), ((), ())), preferred_element_...  11.7 us
    dot_general x7, matrix products, contract_cols(): lax.dot_general(left, right, (((1,), (1,)), ((), ())), preferred_element_...  9.97 us
    dot_general x7, matrix products, matmul(): return jnp.dot(left, right, preferred_element_type=jnp.float32)  9.84 us
    pallas_call x1, Pallas kernels, attention_backward(): pl.pallas_call(functools.partial(attention_back_kernel, HEAD ** (-0.5)),...  9.79 us

profile of v7, /device:TPU:0, one launch (start us, length us, event | category | flops | bytes accessed | tf_op | source)
XLA Modules:
  0.0 421.6 jit_solution(14378837298846596764)
XLA Ops:
  0.7 1.3 reduce_sum.92
  2.6 1.2 dynamic_slice.16.length_ref
  5.3 1.6 copy.42
  7.0 1.1 copy.36
  8.0 0.8 copy.37.refs_3_
  8.9 1.0 fusion.5
  9.9 2.0 add_convert_fusion
  11.9 30.4 %open_step.1 = (bf16[512,1024]{1,0:T(8,128)(2,1)S(1)}, bf16[1024,1024]{1,0:T(8,128)(2,1)S(1)}, bf16[1024,1024]{1,0:T(8,128)(2,1)S(1)}) custom-call(bf16[128,1024]{1,0:T(8,128)(2,1)S(1)} %bitcast.73, f32[5,1024]{1,0:T(8,128)S(1)} %copy-done, bf16[128,1024]{1,0:T(8,128)(2,1)S(1)} %copy-done.22, bf16[1024,128]{1,0:T(8,128)(2,1)S(1)} %copy-done.23), custom_call_target="tpu_custom_call" | custom-call | tf_op jit(solution)/shard_map/open_step/pallas_call | solution.py:568
  42.4 1.3 fusion.37
  44.6 1.3 copy-done.65
  46.0 1.3 convolution_convert_fusion.10.refs_0_
  47.3 35.8 %between_step.7 = (f32[128,1024]{1,0:T(8,128)S(1)}, bf16[512,1024]{1,0:T(8,128)(2,1)S(1)}, bf16[1024,768]{1,0:T(8,128)(2,1)S(1)}, bf16[1024,256]{1,0:T(8,128)(2,...) custom-call(bf16[512,1024]{1,0:T(8,128)(2,1)S(1)} %convolution_convert_fusion.10.refs_0_, ...), custom_call_target="tpu_custom_call" | custom-call | tf_op jit(solution)/shard_map/between_step/pallas_call | solution.py:568
  83.1 1.1 copy-done.4
  85.8 2.5 convolution_convert_fusion.16.position_ref
  88.3 7.0 %attention_forward.1 = (bf16[512,1024]{1,0:T(8,128)(2,1)S(1)}, f32[2,512,512]{2,1,0:T(8,128)S(1)}, bf16[512,256]{1,0:T(8,128)(2,1)S(1)}, bf16[512,256]{1,0:T(8,1...) custom-call(s32[1]{0:T(128)} %dynamic_slice.16.length_ref, ...), custom_call_target="tpu_custom_call" | custom-call | tf_op jit(solution)/shard_map/attention_forward/pallas_call | solution.py:875
  95.3 1.3 copy-done.2
  98.1 37.6 %between_step.8 = (f32[128,1024]{1,0:T(8,128)S(1)}, bf16[512,1024]{1,0:T(8,128)(2,1)S(1)}, bf16[1024,512]{1,0:T(8,128)(2,1)S(1)}, bf16[256,1024]{1,0:T(8,128)(2,1)S(1)}, bf16[1024,1024]{1,0:T(8,128)(2,1)S(1)}) custom-call(bf16[512,1024]{1,0:T(8,128)(2,1)S(1)} %get-tuple-element.85.refs_0_, f32[128,1024]{1,0:T(8,128)S(1)} %get-tuple-element.86.refs_1_, ...), custom_call_target="tpu_custom_call" | custom-call | tf_op jit(solution)/shard_map/between_step/pallas_call | solution.py:568
  137.8 1.2 multiply_reduce_fusion.7
  139.6 5.9 %all_total.2 = f32[2,256]{1,0:T(2,128)} custom-call(f32[2,256]{1,0:T(2,128)} %pad_maximum_fusion.5.in_ref), custom_call_target="tpu_custom_call" | custom-call | tf_op jit(solution)/shard_map/all_total/pallas_call | solution.py:128
  146.3 1.6 convolution_convert_fusion.9.refs_0_
  147.8 37.3 %between_step.9 = (f32[128,1024]{1,0:T(8,128)S(1)}, bf16[512,1024]{1,0:T(8,128)(2,1)S(1)}, bf16[1024,1024]{1,0:T(8,128)(2,1)S(1)}) custom-call(bf16[512,1024]{1,0:T(8,128)(2,1)S(1)} %convolution_convert_fusion.9.refs_0_, f32[128,1024]{1,0:T(8,128)S(1)} %get-tuple-element.90.refs_1_, f32[5,1024]{1,0:T(8,128)S(1)} %copy-done, bf16[128,1024]{1,0:T(8,128)(2,1)S(1)} %copy-done.24), custom_call_target="tpu_custom_call" | custom-call | tf_op jit(solution)/shard_map/between_step/pallas_call | solution.py:568
  185.2 1.3 fusion.39
  186.8 1.3 convolution_convert_fusion.8.refs_0_
  188.1 34.0 %between_step.10 = (bf16[128,1024]{1,0:T(8,128)(2,1)S(1)}, f32[128,1024]{1,0:T(8,128)S(1)}, f32[1,1024]{1,0:T(1,128)S(1)}, bf16[512,1024]{1,0:T(8,128)(2,1)S(1)}) custom-call(bf16[512,1024]{1,0:T(8,128)(2,1)S(1)} %convolution_convert_fusion.8.refs_0_, f32[128,1024]{1,0:T(8,128)S(1)} %get-tuple-element.94.refs_1_, f32[5,1024]{1,0:T(8,128)S(1)} %copy-done, ...), custom_call_target="tpu_custom_call" | custom-call | tf_op jit(solution)/shard_map/between_step/pallas_call | solution.py:568
  222.1 1.6 multiply_convert_fusion.1
  223.7 1.3 convolution_convert_fusion.7.refs_0_
  225.0 1.3 convolution_convert_fusion.3.refs_4_
  226.4 1.3 convolution_convert_fusion.2.refs_5_
  227.7 40.0 %between_step.11 = (f32[128,1024]{1,0:T(8,128)S(1)}, f32[1,1024]{1,0:T(1,128)S(1)}, bf16[512,1024]{1,0:T(8,128)(2,1)S(1)}, f32[128,1024]{1,0:T(8,128)S(1)}, f32[1024,128]{1,0:T(8,128)S(1)}) custom-call(bf16[512,1024]{1,0:T(8,128)(2,1)S(1)} %convolution_convert_fusion.7.refs_0_, f32[128,1024]{1,0:T(8,128)S(1)} %get-tuple-element.94.refs_1_, ...), custom_call_target="tpu_custom_call" | custom-call | tf_op jit(solution)/shard_map/between_step/pallas_call | solution.py:568
  267.7 1.4 fusion.33
  269.1 1.3 convolution_convert_fusion.14.refs_5_
  271.0 5.9 %all_total.3 = f32[2,256]{1,0:T(2,128)} custom-call(f32[2,256]{1,0:T(2,128)} %pad_maximum_fusion.6.in_ref), custom_call_target="tpu_custom_call" | custom-call | tf_op jit(solution)/shard_map/all_total/pallas_call | solution.py:128
  277.6 2.8 multiply_reduce_fusion
  284.0 35.8 %between_step.12 = (f32[128,1024]{1,0:T(8,128)S(1)}, f32[1,1024]{1,0:T(1,128)S(1)}, bf16[512,1024]{1,0:T(8,128)(2,1)S(1)}, f32[128,512]{1,0:T(8,128)S(1)}, f32[256,128]{1,0:T(8,128)S(1)}) custom-call(bf16[512,1024]{1,0:T(8,128)(2,1)S(1)} %convolution_convert_fusion.12.refs_0_, f32[128,1024]{1,0:T(8,128)S(1)} %get-tuple-element.90.refs_1_, ...), custom_call_target="tpu_custom_call" | custom-call | tf_op jit(solution)/shard_map/between_step/pallas_call | solution.py:568
  319.8 0.8 copy-done.18
  321.3 9.8 %attention_backward.1 = (bf16[512,768]{1,0:T(8,128)(2,1)S(1)}, bf16[1024,256]{1,0:T(8,128)(2,1)S(1)}, f32[2,256]{1,0:T(2,128)S(1)}) custom-call(bf16[512,1024]{1,0:T(8,128)(2,1)S(1)} %get-tuple-element.100.grad_ref, bf16[256,1024]{1,0:T(8,128)(2,1)S(1)} %get-tuple-element.84.out_w_ref, f32[2,512,512]{2,1,0:T(8,128)S(1)} %copy-done.3, ...), custom_call_target="tpu_custom_call" | custom-call | tf_op jit(solution)/shard_map/attention_backward/pallas_call | solution.py:954
  331.2 2.0 convolution_convert_fusion.5.refs_0_
  333.2 1.6 convolution_convert_fusion.15.refs_6_
  334.8 0.9 reshape.291
  336.2 2.3 convolution_convert_fusion.4.refs_4_
  338.5 36.4 %between_step.13 = (f32[128,1024]{1,0:T(8,128)S(1)}, f32[1,1024]{1,0:T(1,128)S(1)}, bf16[512,1024]{1,0:T(8,128)(2,1)S(1)}, f32[128,768]{1,0:T(8,128)S(1)}, f32[2...) custom-call(bf16[512,1024]{1,0:T(8,128)(2,1)S(1)} %copy-done.9, f32[128,1024]{1,0:T(8,128)S(1)} %get-tuple-element.86.refs_1_, ...), custom_call_target="tpu_custom_call" | custom-call | tf_op jit(solution)/shard_map/between_step/pallas_call | solution.py:568
  375.0 1.6 multiply_convert_fusion
  376.6 1.3 convolution_convert_fusion.6.refs_0_
  377.9 1.3 convolution_convert_fusion.1.refs_6_
  379.3 1.3 convolution_convert_fusion.refs_7_
  380.7 35.9 %close_step.1 = (f32[128,1024]{1,0:T(8,128)S(1)}, f32[7,256]{1,0:T(8,128)S(1)}, f32[5,1024]{1,0:T(8,128)S(1)}, f32[128,1024]{1,0:T(8,128)S(1)}, f32[1024,128]{1,0:T(8,128)S(1)}) custom-call(bf16[512,1024]{1,0:T(8,128)(2,1)S(1)} %convolution_convert_fusion.6.refs_0_, f32[7,256]{1,0:T(8,128)S(1)} %concatenate.18.refs_1_, ...), custom_call_target="tpu_custom_call" | custom-call | tf_op jit(solution)/shard_map/close_step/pallas_call | solution.py:568
  416.6 1.8 store_all.1
  420.4 0.9 copy.40
  (171 shorter events, 17.5 us)
Async XLA Ops:
  5.3 6.6 %copy-start = (f32[5,1024]{1,0:T(8,128)S(1)}, f32[5,1024]{1,0:T(8,128)}, u32[]{:S(2)}) copy-start(f32[5,1024]{1,0:T(8,128)} %refs_4_.5) | copy-start | bytes 61444
  5.3 6.6 %copy-start.1 = (bf16[1,128,1024]{2,1,0:T(8,128)(2,1)S(1)}, bf16[1,128,1024]{2,1,0:T(8,128)(2,1)}, u32[]{:S(2)}) copy-start(bf16[1,128,1024]{2,1,0:T(8,128)(2,1)} %param.17) | copy-start | bytes 786436
  5.3 6.6 %copy-start.22 = (bf16[128,1024]{1,0:T(8,128)(2,1)S(1)}, bf16[128,1024]{1,0:T(8,128)(2,1)}, u32[]{:S(2)}) copy-start(bf16[128,1024]{1,0:T(8,128)(2,1)} %refs_2_.8) | copy-start | bytes 786436
  5.3 6.6 %copy-start.23 = (bf16[1024,128]{1,0:T(8,128)(2,1)S(1)}, bf16[1024,128]{1,0:T(8,128)(2,1)}, u32[]{:S(2)}) copy-start(bf16[1024,128]{1,0:T(8,128)(2,1)} %refs_3_.2) | copy-start | bytes 786436
  42.3 2.0 copy-start.48
  42.4 2.3 copy-start.52
  84.2 4.0 copy-start.7
  85.8 2.5 copy-start.5
  88.3 9.8 %copy-start.21 = (bf16[16,8,2,256]{3,1,2,0:T(8,128)(2,1)S(1)}, bf16[16,8,2,256]{3,1,2,0:T(8,128)(2,1)}, u32[]{:S(2)}) copy-start(bf16[16,8,2,256]{3,1,2,0:T(8,128)(2,1)} %copy.42) | copy-start | bytes 393220
  88.3 9.8 %copy-start.40 = (bf16[1024,128]{1,0:T(8,128)(2,1)S(1)}, bf16[1024,128]{1,0:T(8,128)(2,1)}, u32[]{:S(2)}) copy-start(bf16[1024,128]{1,0:T(8,128)(2,1)} %refs_5_.3) | copy-start | bytes 786436
  88.3 9.8 %copy-start.45 = (bf16[256,128]{1,0:T(8,128)(2,1)S(1)}, bf16[256,128]{1,0:T(8,128)(2,1)}, u32[]{:S(2)}) copy-start(bf16[256,128]{1,0:T(8,128)(2,1)} %refs_4_.4) | copy-start | bytes 196612
  98.1 38.3 %copy-start.32 = (bf16[512,256]{1,0:T(8,128)(2,1)}, bf16[512,256]{1,0:T(8,128)(2,1)S(1)}, u32[]{:S(2)}) copy-start(bf16[512,256]{1,0:T(8,128)(2,1)S(1)} %get-tuple-element.103.query_v_ref) | copy-start | bytes 786436
  98.1 38.3 %copy-start.34 = (bf16[512,256]{1,0:T(8,128)(2,1)}, bf16[512,256]{1,0:T(8,128)(2,1)S(1)}, u32[]{:S(2)}) copy-start(bf16[512,256]{1,0:T(8,128)(2,1)S(1)} %get-tuple-element.104.key_ref) | copy-start | bytes 786436
  98.1 38.3 %copy-start.36 = (bf16[512,256]{1,0:T(8,128)(2,1)}, bf16[512,256]{1,0:T(8,128)(2,1)S(1)}, u32[]{:S(2)}) copy-start(bf16[512,256]{1,0:T(8,128)(2,1)S(1)} %get-tuple-element.105.value_ref) | copy-start | bytes 786436
  135.7 1.4 copy-start.50
  135.7 1.8 copy-start.54
  135.7 2.1 copy-start.56
  136.4 2.5 copy-start.60
  139.0 8.8 %copy-start.24 = (bf16[128,1024]{1,0:T(8,128)(2,1)S(1)}, bf16[128,1024]{1,0:T(8,128)(2,1)}, u32[]{:S(2)}) copy-start(bf16[128,1024]{1,0:T(8,128)(2,1)} %refs_3_.3) | copy-start | bytes 786436
  185.2 1.6 copy-start.51
  222.1 1.7 copy-start.26
  227.7 40.0 %copy-start.63 = (f32[512,256]{1,0:T(8,128)S(1)}, f32[512,256]{1,0:T(8,128)}, u32[]{:S(2)}) copy-start(f32[512,256]{1,0:T(8,128)} %get-tuple-element.185) | copy-start | bytes 1572868
  267.7 1.4 copy-start.11
  267.7 1.4 copy-start.13
  267.7 1.4 copy-start.15
  270.4 10.5 %copy-start.61 = (f32[512,512]{1,0:T(8,128)S(1)}, f32[512,512]{1,0:T(8,128)}, u32[]{:S(2)}) copy-start(f32[512,512]{1,0:T(8,128)} %copy-done.60) | copy-start | bytes 3145732
  284.0 37.3 %copy-start.3 = (f32[2,512,512]{2,1,0:T(8,128)S(1)}, f32[2,512,512]{2,1,0:T(8,128)}, u32[]{:S(2)}) copy-start(f32[2,512,512]{2,1,0:T(8,128)} %copy-done.2) | copy-start | bytes 6291460
  284.0 37.3 %copy-start.31 = (bf16[512,256]{1,0:T(8,128)(2,1)S(1)}, bf16[512,256]{1,0:T(8,128)(2,1)}, u32[]{:S(2)}) copy-start(bf16[512,256]{1,0:T(8,128)(2,1)} %copy-done.30) | copy-start | bytes 786436
  284.0 37.3 %copy-start.33 = (bf16[512,256]{1,0:T(8,128)(2,1)S(1)}, bf16[512,256]{1,0:T(8,128)(2,1)}, u32[]{:S(2)}) copy-start(bf16[512,256]{1,0:T(8,128)(2,1)} %copy-done.32) | copy-start | bytes 786436
  284.0 37.3 %copy-start.35 = (bf16[512,256]{1,0:T(8,128)(2,1)S(1)}, bf16[512,256]{1,0:T(8,128)(2,1)}, u32[]{:S(2)}) copy-start(bf16[512,256]{1,0:T(8,128)(2,1)} %copy-done.34) | copy-start | bytes 786436
  284.0 37.3 %copy-start.37 = (bf16[512,256]{1,0:T(8,128)(2,1)S(1)}, bf16[512,256]{1,0:T(8,128)(2,1)}, u32[]{:S(2)}) copy-start(bf16[512,256]{1,0:T(8,128)(2,1)} %copy-done.36) | copy-start | bytes 786436
  321.3 9.8 %copy-start.41 = (f32[256,128]{1,0:T(8,128)}, f32[256,128]{1,0:T(8,128)S(1)}, u32[]{:S(2)}) copy-start(f32[256,128]{1,0:T(8,128)S(1)} %get-tuple-element.122.refs_6_) | copy-start | bytes 393220
  321.3 9.8 %copy-start.6 = (bf16[1024,768]{1,0:T(8,128)(2,1)S(1)}, bf16[1024,768]{1,0:T(8,128)(2,1)}, u32[]{:S(2)}) copy-start(bf16[1024,768]{1,0:T(8,128)(2,1)} %copy-done.4) | copy-start | bytes 4718596
  331.2 3.6 copy-start.58
  331.2 2.0 copy-start.64
  333.2 1.6 copy-start.39
  333.2 2.5 copy-start.29
  334.7 1.4 copy-start.8
  336.1 2.3 copy-start.9
  336.1 2.3 copy-start.19
  336.1 2.3 copy-start.20
  338.5 36.4 %copy-start.49 = (bf16[1024,1024]{1,0:T(8,128)(2,1)S(1)}, bf16[1024,1024]{1,0:T(8,128)(2,1)}, u32[]{:S(2)}) copy-start(bf16[1024,1024]{1,0:T(8,128)(2,1)} %copy-done.48) | copy-start | bytes 6291460
  338.5 36.4 %copy-start.66 = (f32[512,1024]{1,0:T(8,128)S(1)}, f32[512,1024]{1,0:T(8,128)}, u32[]{:S(2)}) copy-start(f32[512,1024]{1,0:T(8,128)} %copy-done.65) | copy-start | bytes 6291460
  374.9 1.7 copy-start.47
  380.6 35.9 %copy-start.12 = (f32[128,1024]{1,0:T(8,128)S(1)}, f32[128,1024]{1,0:T(8,128)}, u32[]{:S(2)}) copy-start(f32[128,1024]{1,0:T(8,128)} %copy-done.11) | copy-start | bytes 1572868
  380.6 35.9 %copy-start.14 = (f32[1024,128]{1,0:T(8,128)S(1)}, f32[1024,128]{1,0:T(8,128)}, u32[]{:S(2)}) copy-start(f32[1024,128]{1,0:T(8,128)} %copy-done.13) | copy-start | bytes 1572868
  380.7 35.9 %copy-start.27 = (bf16[128,1024]{1,0:T(8,128)(2,1)S(1)}, bf16[128,1024]{1,0:T(8,128)(2,1)}, u32[]{:S(2)}) copy-start(bf16[128,1024]{1,0:T(8,128)(2,1)} %copy-done.26) | copy-start | bytes 786436
  380.7 35.9 %copy-start.42 = (f32[256,128]{1,0:T(8,128)S(1)}, f32[256,128]{1,0:T(8,128)}, u32[]{:S(2)}) copy-start(f32[256,128]{1,0:T(8,128)} %copy-done.41) | copy-start | bytes 393220
  (19 other events, 21.3 us)
